TPU v7x, 32 devices: a whole 2x2x4 slice. The times are simulated.
32 devices in a mesh: cam: 8 (over y, x, core), row: 4 (over z).
Axes of the slice: x: 2, y: 2, z: 4, core: 2. Of those that a mesh axis runs over, the one named last changes fastest.
Arguments:
- image: bfloat16 [8, 16, 128, 2048], P('cam', None, 'row'), may hold values from -6 to 6
- conv_first: bfloat16 [16, 144], replicated, may hold values from -0.5 to 0.5
- conv_second: bfloat16 [16, 144], replicated, may hold values from -0.5 to 0.5
- conv_uv: bfloat16 [16, 144], replicated, may hold values from -0.5 to 0.5
- send_block: int32 [8, 4, 32, 16], P('cam', 'row'), may hold values from 0 to 511
- send_shift: int32 [8, 4, 32, 16], P('cam', 'row'), may hold values from 0 to 127
- send_weight: int32 [8, 4, 32, 16], P('cam', 'row'), may hold values from 1 to 64
- send_count: int32 [8, 4, 32], P('cam', 'row'), may hold values from 0 to 16, as said below
- recv_tile: int32 [4, 8, 32, 16], P('row', 'cam'), may hold values from 0 to 1023
Outputs:
- texture: bfloat16 [16, 4096, 1024], P(None, 'row', 'cam')
Inputs may be any that keep to these rules, and one draw needn't show every extreme that they name: `send_count`: slots of a list at or beyond its count are padding. In every draw one atlas region receives 16 used slots from every strip.
All inputs are finite; a program needn't handle non-finite values.
Results may differ from a plain program's by a relative error of at most 0.0066.
Values may be sent and summed in bfloat16 or wider, within the bound.
No kernel may reach another device: no remote copies, remote signals or barrier semaphores. Data moves between devices by JAX's collectives and lax.ppermute only.
A program may use at most 192 MiB of HBM per device.

v0:
```python
import functools

import jax
import jax.numpy as jnp
from jax import lax
from jax.experimental import pallas as pl
from jax.experimental.pallas import tpu as pltpu
from jax.sharding import PartitionSpec as P

TL = 128
AR_DEV = 1024
GROUP = 8
VMEM_BYTES = 60 * 1024 * 1024
WHOLE = pl.BlockSpec(memory_space=pltpu.VMEM)
SCALARS = pl.BlockSpec(memory_space=pltpu.SMEM)


def neighbour(cells, axis, step):
    count = lax.axis_size(axis)
    pairs = [(i, i + step) for i in range(count) if 0 <= i + step < count]
    return lax.ppermute(cells, axis, pairs)


def band(weight, channel_major):
    tap_row = weight.shape[1] // 3
    rows = [
        jnp.pad(weight, ((0, 0), (tap_row * r, tap_row * (GROUP - 1 - r)))) for r in range(GROUP)
    ]
    stacked = jnp.stack(rows, axis=1 if channel_major else 0)
    return stacked.reshape(-1, stacked.shape[-1])


def lanes_of(shape):
    return lax.broadcasted_iota(jnp.int32, shape, len(shape) - 1)


def spread(row, lanes, taps_ref, cells):
    channels, width = cells.shape
    zero = jnp.zeros_like(cells)
    base = pl.multiple_of(row * (3 * channels), 3 * channels)
    taps_ref[pl.ds(base, channels), :] = jnp.where(lanes == 0, zero, pltpu.roll(cells, 1, 1))
    taps_ref[pl.ds(base + channels, channels), :] = cells
    taps_ref[pl.ds(base + 2 * channels, channels), :] = jnp.where(
        lanes == width - 1, zero, pltpu.roll(cells, width - 1, 1)
    )


def send_kernel(
    place_ref,
    block_ref,
    shift_ref,
    weight_ref,
    count_ref,
    image_ref,
    above_ref,
    below_ref,
    first_ref,
    second_ref,
    payload_ref,
    taps_ref,
    hidden_ref,
    feature_ref,
    slots_ref,
):
    rows, channels, width = image_ref.shape
    tap = 3 * channels
    reach = (GROUP + 2) * tap
    lanes = lanes_of((channels, width))
    for i in range(2):
        spread(i, lanes, taps_ref, above_ref[i])
        spread(rows + 2 + i, lanes, taps_ref, below_ref[i])

    @pl.loop(0, rows)
    def _(i):
        spread(i + 2, lanes, taps_ref, image_ref[i])

    step = 2 * TL
    has_above = (place_ref[0] > 0).astype(jnp.float32)
    has_below = (place_ref[0] < place_ref[1] - 1).astype(jnp.float32)

    @pl.loop(0, width // step)
    def _(j):
        cols = pl.ds(pl.multiple_of(j * step, step), step)

        def activate(v):
            return v / (1.0 + jnp.exp(-v))

        for g in range(rows // GROUP):
            window = taps_ref[pl.ds(g * GROUP * tap, reach), cols]
            out = activate(jnp.dot(first_ref[...], window, preferred_element_type=jnp.float32))
            out = out.reshape(GROUP, channels, step)
            if g == 0:
                out = jnp.concatenate([out[:1] * has_above, out[1:]], axis=0)
            hidden_ref[pl.ds(g * GROUP, GROUP), :, cols] = out.astype(jnp.bfloat16)
        window = taps_ref[pl.ds(rows * tap, 4 * tap), cols]
        out = activate(
            jnp.dot(
                first_ref[: 2 * channels, : 4 * tap], window, preferred_element_type=jnp.float32
            )
        ).reshape(2, channels, step)
        out = jnp.concatenate([out[:1], out[1:] * has_below], axis=0)
        hidden_ref[pl.ds(rows, 2), :, cols] = out.astype(jnp.bfloat16)

    @pl.loop(0, rows + 2)
    def _(i):
        spread(i, lanes, taps_ref, hidden_ref[i])

    per_row = width // TL

    @pl.loop(0, width // step)
    def _(j):
        cols = pl.ds(pl.multiple_of(j * step, step), step)
        for g in range(rows // GROUP):
            window = taps_ref[pl.ds(g * GROUP * tap, reach), cols]
            out = jnp.dot(second_ref[...], window, preferred_element_type=jnp.float32)
            out = out.astype(jnp.bfloat16).reshape(GROUP, channels, step)
            for r in range(GROUP):
                for half in range(2):
                    feature_ref[(g * GROUP + r) * per_row + 2 * j + half] = out[
                        r, :, half * TL : (half + 1) * TL
                    ]

    peers, capacity = block_ref.shape
    half = capacity // 2
    side = lanes_of((half, TL)) < TL // 2
    slot_row = lax.broadcasted_iota(jnp.int32, (half, TL), 0)

    @pl.loop(0, peers)
    def _(d):
        count = count_ref[0, d]
        factors = []
        for k in range(capacity):
            scale = jnp.where(k < count, weight_ref[d, k].astype(jnp.float32) * 0.0625, 0.0)
            factors.append(scale)
            cells = feature_ref[block_ref[d, k]].astype(jnp.float32)
            cells = pltpu.roll(cells, shift_ref[d, k], 1) * scale
            slots_ref[pl.ds(k, channels, stride=capacity), :] = cells
        payload_ref[d, : channels * capacity, :] = slots_ref[...].astype(jnp.bfloat16)
        record = jnp.zeros((half, TL), jnp.float32)
        for k in range(half):
            record = jnp.where(
                slot_row == k, jnp.where(side, factors[k], factors[k + half]), record
            )
        payload_ref[d, channels * capacity :, :] = record.astype(jnp.bfloat16)


def join_kernel(
    tile_ref, incoming_ref, joined_ref, first_ref, last_ref, onehot_ref, inverse_ref, cells_ref
):
    peers = incoming_ref.shape[0]
    entries = tile_ref.shape[1]
    capacity = entries // peers
    half = capacity // 2
    tiles = onehot_ref.shape[0]
    channels = joined_ref.shape[0] // tiles
    rows = 128

    @pl.loop(0, tiles // rows)
    def _(i):
        base = pl.multiple_of(i * rows, rows)
        ids = lax.broadcasted_iota(jnp.int32, (rows, entries), 0) + base
        onehot_ref[pl.ds(base, rows), :] = jnp.where(ids == tile_ref[...], 1.0, 0.0).astype(
            jnp.bfloat16
        )

    record = incoming_ref[:, channels * capacity :, :].astype(jnp.float32)
    record = record.reshape(peers * half, TL)
    other = pltpu.roll(record, TL // 2, 1)
    side = lanes_of(record.shape) < TL // 2
    low = jnp.where(side, record, other).reshape(peers, half, TL)
    high = jnp.where(side, other, record).reshape(peers, half, TL)
    scales = jnp.concatenate([low, high], axis=1).reshape(entries, TL).astype(jnp.bfloat16)
    total = jnp.dot(onehot_ref[...], scales, preferred_element_type=jnp.float32)
    inverse_ref[...] = 1.0 / jnp.maximum(total, 1.0)
    for q in range(0, channels, 2):
        pair = jnp.concatenate(
            [
                incoming_ref[:, p * capacity : (p + 1) * capacity, :].reshape(entries, TL)
                for p in (q, q + 1)
            ],
            axis=1,
        )
        total = jnp.dot(onehot_ref[...], pair, preferred_element_type=jnp.float32)
        for p in range(2):
            cells_ref[pl.ds(q + p, tiles, stride=channels), :] = (
                total[:, p * TL : (p + 1) * TL] * inverse_ref[...]
            )
    lanes = lanes_of((channels, TL))
    unroll = 8

    @pl.loop(0, tiles // TL)
    def _(i):
        def one(s, carry):
            left, right = carry
            for u in range(unroll):
                base = pl.multiple_of(((i * (TL // unroll) + s) * unroll + u) * channels, channels)
                cells = cells_ref[pl.ds(base, channels), :].astype(jnp.bfloat16)
                joined_ref[pl.ds(base, channels), :] = cells
                back = pltpu.roll(cells, TL - 1, 1)
                left = jnp.where(lanes == TL - 1, back, pltpu.roll(left, TL - 1, 1))
                right = jnp.where(lanes == TL - 1, cells, pltpu.roll(right, TL - 1, 1))
            return left, right

        zero = jnp.zeros((channels, TL), jnp.bfloat16)
        left, right = lax.fori_loop(0, TL // unroll, one, (zero, zero))
        cols = pl.ds(pl.multiple_of(i * TL, TL), TL)
        first_ref[:, cols] = left
        last_ref[:, cols] = right


def texture_kernel(
    joined_ref, above_ref, below_ref, before_ref, after_ref, weight_ref, residual_ref, texture_ref, taps_ref
):
    channels = texture_ref.shape[0]
    tiles = texture_ref.shape[1]
    tap = 3 * channels
    reach = (GROUP + 2) * tap
    lanes = lanes_of((channels, TL))

    def place(row, cells, before, after):
        base = pl.multiple_of(row * tap, channels)
        taps_ref[pl.ds(base, channels), :] = jnp.where(lanes == 0, before, pltpu.roll(cells, 1, 1))
        taps_ref[pl.ds(base + channels, channels), :] = cells
        taps_ref[pl.ds(base + 2 * channels, channels), :] = jnp.where(
            lanes == TL - 1, after, pltpu.roll(cells, TL - 1, 1)
        )

    def corner(ref, k, back):
        cells = ref[:, tiles + k * TL : tiles + (k + 1) * TL]
        return pltpu.roll(cells, 1 if back else TL - 1, 1)

    place(0, above_ref[...], corner(before_ref, 0, True), corner(after_ref, 0, False))
    place(tiles + 1, below_ref[...], corner(before_ref, 1, True), corner(after_ref, 1, False))
    unroll = 8

    @pl.loop(0, tiles // TL)
    def _(i):
        cols = pl.ds(pl.multiple_of(i * TL, TL), TL)

        def one(s, carry):
            before, after = carry
            for u in range(unroll):
                t = (i * (TL // unroll) + s) * unroll + u
                cells = joined_ref[pl.ds(pl.multiple_of(t * channels, channels), channels), :]
                place(t + 1, cells, before, after)
                before = pltpu.roll(before, TL - 1, 1)
                after = pltpu.roll(after, TL - 1, 1)
            return before, after

        lax.fori_loop(
            0, TL // unroll, one, (before_ref[:, cols], pltpu.roll(after_ref[:, cols], TL - 1, 1))
        )

    pair = 2 * GROUP

    @pl.loop(0, tiles // pair)
    def _(i):
        base = pl.multiple_of(i * (pair * tap), pair * tap)
        window = jnp.concatenate(
            [
                taps_ref[pl.ds(base, reach), :],
                taps_ref[pl.ds(base + GROUP * tap, reach), :],
            ],
            axis=1,
        )
        rows = pl.multiple_of(i * (pair * channels), pair * channels)
        own = jnp.concatenate(
            [
                joined_ref[pl.ds(rows, GROUP * channels), :],
                joined_ref[pl.ds(rows + GROUP * channels, GROUP * channels), :],
            ],
            axis=1,
        )
        out = jnp.dot(weight_ref[...], window, preferred_element_type=jnp.float32)
        out = out + jnp.dot(residual_ref[...], own, preferred_element_type=jnp.float32)
        out = out.reshape(channels, GROUP, 2 * TL)
        out = jnp.concatenate([out[:, :, :TL], out[:, :, TL:]], axis=1)
        texture_ref[:, pl.ds(pl.multiple_of(i * pair, pair), pair), :] = out.astype(jnp.bfloat16)


def call(kernel, outs, scratch, specs):
    return pl.pallas_call(
        kernel,
        out_shape=outs,
        in_specs=specs,
        out_specs=jax.tree.map(lambda _: WHOLE, outs),
        scratch_shapes=scratch,
        compiler_params=pltpu.CompilerParams(vmem_limit_bytes=VMEM_BYTES),
    )


def local(
    image,
    conv_first,
    conv_second,
    conv_uv,
    send_block,
    send_shift,
    send_weight,
    send_count,
    recv_tile,
):
    half = jnp.bfloat16
    pixels = image[0]
    channels, strip_rows, width = pixels.shape
    by_row = pixels.transpose(1, 0, 2)
    above = neighbour(by_row[-2:], "row", 1)
    below = neighbour(by_row[:2], "row", -1)
    place = jnp.stack([lax.axis_index("row"), lax.axis_size("row")]).astype(jnp.int32)
    peers, capacity = send_block.shape[2:]
    entries = peers * capacity
    message = channels * capacity + capacity // 2
    payload = call(
        send_kernel,
        jax.ShapeDtypeStruct((peers, message, TL), half),
        [
            pltpu.VMEM(((strip_rows + 4) * 3 * channels, width), half),
            pltpu.VMEM((strip_rows + 2, channels, width), half),
            pltpu.VMEM((strip_rows * width // TL, channels, TL), half),
            pltpu.VMEM((channels * capacity, TL), jnp.float32),
        ],
        [SCALARS] * 5 + [WHOLE] * 5,
    )(
        place,
        send_block[0, 0],
        send_shift[0, 0],
        send_weight[0, 0],
        send_count[0],
        by_row,
        above,
        below,
        band(conv_first, False),
        band(conv_second, False),
    )
    arrived = lax.all_to_all(payload, ("cam", "row"), split_axis=0, concat_axis=0, tiled=True)
    joined, first, last = call(
        join_kernel,
        (
            jax.ShapeDtypeStruct((AR_DEV * channels, TL), half),
            jax.ShapeDtypeStruct((channels, AR_DEV), half),
            jax.ShapeDtypeStruct((channels, AR_DEV), half),
        ),
        [
            pltpu.VMEM((AR_DEV, entries), half),
            pltpu.VMEM((AR_DEV, TL), jnp.float32),
            pltpu.VMEM((AR_DEV * channels, TL), jnp.float32),
        ],
        [WHOLE] * 2,
    )(recv_tile.reshape(1, entries), arrived)
    top = neighbour(joined[-channels:], "row", 1)
    bottom = neighbour(joined[:channels], "row", -1)
    before = neighbour(jnp.concatenate([last, top, bottom], axis=1), "cam", 1)
    after = neighbour(jnp.concatenate([first, top, bottom], axis=1), "cam", -1)
    same = (
        lax.broadcasted_iota(jnp.int32, (channels, GROUP, GROUP, channels), 0)
        == lax.broadcasted_iota(jnp.int32, (channels, GROUP, GROUP, channels), 3)
    ) & (
        lax.broadcasted_iota(jnp.int32, (channels, GROUP, GROUP, channels), 1)
        == lax.broadcasted_iota(jnp.int32, (channels, GROUP, GROUP, channels), 2)
    )
    residual = same.astype(half).reshape(channels * GROUP, GROUP * channels)
    return call(
        texture_kernel,
        jax.ShapeDtypeStruct((channels, AR_DEV, TL), half),
        [pltpu.VMEM(((AR_DEV + 2) * 3 * channels, TL), half)],
        [WHOLE] * 7,
    )(joined, top, bottom, before, after, band(conv_uv, True), residual)


def solution(mesh):
    return jax.shard_map(
        local,
        mesh=mesh,
        in_specs=(
            P("cam", None, "row", None),
            P(),
            P(),
            P(),
            P("cam", "row", None, None),
            P("cam", "row", None, None),
            P("cam", "row", None, None),
            P("cam", "row", None),
            P("row", "cam", None, None),
        ),
        out_specs=P(None, "row", "cam"),
        check_vma=False,
    )
```

profile of v0, /device:TPU:11, one launch (start us, length us, event | category | flops | bytes accessed | tf_op | source)
XLA Modules:
  0.0 272.1 jit_solution(1393604855067400758)
XLA Ops:
  0.0 2.8 %copy.24 = bf16[1,16,32,2048]{3,1,2,0:T(8,128)(2,1)S(1)} copy(bf16[1,16,32,2048]{3,2,1,0:T(8,128)(2,1)} %param.9) | data formatting | bytes 4194304 | tf_op args[0]
  2.9 2.1 collective-permute-start.1
  4.9 3.2 %collective-permute-start = (bf16[2,16,2048]{2,1,0:T(8,128)(2,1)S(1)}, bf16[2,16,2048]{2,1,0:T(8,128)(2,1)S(1)}, u32[]{:S(2)}, u32[]{:S(2)}) collective-permute-start(bf16[2,16,2048]{2,1,0:T(8,128)(2,1)S(1)} %get-tuple-element.14), channel_id=1, source_target_pairs={{0,1},{1,2},{2,3},{4,5},{5,6},{6,7},{8,9},{9,10},{10,11},{12,13},{... | collective-permute-start | bytes 393224 | tf_op jit(solution)/shard_map/ppermute | solution.py:21
  9.2 0.6 pad_add_fusion.place_ref
  9.8 0.7 copy.17
  10.4 0.7 copy.18
  11.1 0.7 copy.19
  11.9 0.6 copy-done.6
  12.6 19.6 %shard_map.91 = bf16[32,264,128]{2,1,0:T(8,128)(2,1)} custom-call(s32[2]{0:T(128)} %pad_add_fusion.place_ref, s32[32,16]{1,0:T(8,128)} %bitcast.70, s32[32,16]{1,0:T(8,128)} %bitcast.71, s32[32,16]{1,0:T(8,128)} %bitcast.72, s32[1,32]{1,0:T(1,128)} %bitcast.73, bf16[32,16,2048]{2,1,0:T(8,128)(2,1)} %bitcast.66, bf16[2,16,2048]{2,1,0:T(8,128)(2,1)} %copy-done.8, ...), custom_call_target="tpu_custom_call" | custom-call | tf_op jit(solution)/shard_map/pallas_call | solution.py:313
  32.3 6.4 %all-to-all-start = ((bf16[32,264,128]{2,1,0:T(8,128)(2,1)}), bf16[32,264,128]{2,1,0:T(8,128)(2,1)S(1)}, u32[]{:S(2)}, u32[]{:S(2)}) async-start(bf16[32,264,128]{2,1,0:T(8,128)(2,1)} %shard_map.91), calls=%async_computation | async-start | bytes 4325376 | tf_op jit(solution)/shard_map/all_to_all | solution.py:335
  39.2 0.7 reshape.17.tile_ref
  40.2 0.7 and_convert_fusion.residual_ref
  40.9 46.4 %all-to-all-done.incoming_ref = bf16[32,264,128]{2,1,0:T(8,128)(2,1)S(1)} async-done(((bf16[32,264,128]{2,1,0:T(8,128)(2,1)}), bf16[32,264,128]{2,1,0:T(8,128)(2,1)S(1)}, u32[]{:S(2)}, u32[]{:S(2)}) %all-to-all-start) | async-done | bytes 2162720 | tf_op jit(solution)/shard_map/all_to_all | solution.py:335
  87.3 1.3 copy-done.1
  88.7 78.4 %shard_map.92 = (bf16[16384,128]{1,0:T(8,128)(2,1)}, bf16[16,1024]{1,0:T(8,128)(2,1)}, bf16[16,1024]{1,0:T(8,128)(2,1)}) custom-call(s32[1,512]{1,0:T(1,128)} %reshape.17.tile_ref, bf16[32,264,128]{2,1,0:T(8,128)(2,1)} %copy-done.1), custom_call_target="tpu_custom_call" | custom-call | tf_op jit(solution)/shard_map/pallas_call | solution.py:336
  167.1 0.7 fusion
  167.8 3.4 %collective-permute-start.3 = (bf16[16,128]{1,0:T(8,128)(2,1)S(1)}, bf16[16,128]{1,0:T(8,128)(2,1)S(1)}, u32[]{:S(2)}, u32[]{:S(2)}) collective-permute-start(bf16[16,128]{1,0:T(8,128)(2,1)S(1)} %get-tuple-element.11), channel_id=1, source_target_pairs={{1,0},{2,1},{3,2},{5,4},{6,5},{7,6},{9,8},{10,9},{11,10},{13,12},{... | collective-permute-start | bytes 12296 | tf_op jit(solution)/shard_map/ppermute | solution.py:21
  171.2 1.9 collective-permute-start.2
  173.2 2.3 collective-permute-done.2.above_ref
  175.6 0.8 pad_maximum_fusion
  176.4 1.9 collective-permute-start.5
  178.3 4.5 %collective-permute-start.4 = (bf16[16,1280]{1,0:T(8,128)(2,1)S(1)}, bf16[16,1280]{1,0:T(8,128)(2,1)S(1)}, u32[]{:S(2)}, u32[]{:S(2)}) collective-permute-start(bf16[16,1280]{1,0:T(8,128)(2,1)S(1)} %get-tuple-element.16), channel_id=1, source_target_pairs={{0,4},{4,8},{8,12},{12,16},{16,20},{20,24},{24,28},{1,5},{5,9},{9,... | collective-permute-start | bytes 122888 | tf_op jit(solution)/shard_map/ppermute | solution.py:21
  182.9 0.7 copy.25
  184.5 87.6 %shard_map.93 = bf16[16,1024,128]{2,1,0:T(8,128)(2,1)} custom-call(bf16[16384,128]{1,0:T(8,128)(2,1)} %get-tuple-element.8.joined_ref, bf16[16,128]{1,0:T(8,128)(2,1)} %copy-done.12, bf16[16,128]{1,0:T(8,128)(2,1)} %copy-done.11, bf16[16,1280]{1,0:T(8,128)(2,1)} %copy-done.10, bf16[16,1280]{1,0:T(8,128)(2,1)} %copy-done.9, bf16[128,480]{1,0:T(8,128)(2,1)} %bitcast.67, ...), custom_call_target="tpu_custom_call" | custom-call | tf_op jit(solution)/shard_map/pallas_call | solution.py:362
  (71 shorter events, 3.1 us)
Async XLA Ops:
  0.0 8.2 %copy-start.2 = (bf16[16,144]{1,0:T(8,128)(2,1)S(1)}, bf16[16,144]{1,0:T(8,128)(2,1)}, u32[]{:S(2)}) copy-start(bf16[16,144]{1,0:T(8,128)(2,1)} %param.10) | copy-start | bytes 13828
  0.0 8.7 %copy-start.3 = (bf16[16,144]{1,0:T(8,128)(2,1)S(1)}, bf16[16,144]{1,0:T(8,128)(2,1)}, u32[]{:S(2)}) copy-start(bf16[16,144]{1,0:T(8,128)(2,1)} %param.11) | copy-start | bytes 13828
  0.0 9.8 %copy-start.13 = (s32[1,1,32,16]{2,3,1,0:T(8,128)S(1)}, s32[1,1,32,16]{2,3,1,0:T(8,128)}, u32[]{:S(2)}) copy-start(s32[1,1,32,16]{2,3,1,0:T(8,128)} %param.13) | copy-start | bytes 6148
  0.0 10.4 %copy-start.14 = (s32[1,1,32,16]{2,3,1,0:T(8,128)S(1)}, s32[1,1,32,16]{2,3,1,0:T(8,128)}, u32[]{:S(2)}) copy-start(s32[1,1,32,16]{2,3,1,0:T(8,128)} %param.14) | copy-start | bytes 6148
  0.0 11.1 %copy-start.15 = (s32[1,1,32,16]{2,3,1,0:T(8,128)S(1)}, s32[1,1,32,16]{2,3,1,0:T(8,128)}, u32[]{:S(2)}) copy-start(s32[1,1,32,16]{2,3,1,0:T(8,128)} %param.15) | copy-start | bytes 6148
  2.8 9.1 %copy-start = (bf16[1,16,32,2048]{3,1,2,0:T(8,128)(2,1)}, bf16[1,16,32,2048]{3,1,2,0:T(8,128)(2,1)S(1)}, u32[]{:S(2)}) copy-start(bf16[1,16,32,2048]{3,1,2,0:T(8,128)(2,1)S(1)} %copy.24) | copy-start | bytes 6291460
  2.9 9.0 %collective-permute-start.1 = (bf16[2,16,2048]{2,1,0:T(8,128)(2,1)S(1)}, bf16[2,16,2048]{2,1,0:T(8,128)(2,1)S(1)}, u32[]{:S(2)}, u32[]{:S(2)}) collective-permute-start(bf16[2,16,2048]{2,1,0:T(8,128)(2,1)S(1)} %get-tuple-element.13), channel_id=1, source_target_pairs={{1,0},{2,1},{3,2},{5,4},{6,5},{7,6},{9,8},{10,9},{11,10},{13,12},{... | collective-permute-start | bytes 393224 | tf_op jit(solution)/shard_map/ppermute | solution.py:21
  4.9 6.9 %collective-permute-start = (bf16[2,16,2048]{2,1,0:T(8,128)(2,1)S(1)}, bf16[2,16,2048]{2,1,0:T(8,128)(2,1)S(1)}, u32[]{:S(2)}, u32[]{:S(2)}) collective-permute-start(bf16[2,16,2048]{2,1,0:T(8,128)(2,1)S(1)} %get-tuple-element.14), channel_id=1, source_target_pairs={{0,1},{1,2},{2,3},{4,5},{5,6},{6,7},{8,9},{9,10},{10,11},{12,13},{... | collective-permute-start | bytes 393224 | tf_op jit(solution)/shard_map/ppermute | solution.py:21
  8.7 3.2 %copy-start.5 = (bf16[8,16,480]{2,1,0:T(8,128)(2,1)}, bf16[8,16,480]{2,1,0:T(8,128)(2,1)S(1)}, u32[]{:S(2)}) copy-start(bf16[8,16,480]{2,1,0:T(8,128)(2,1)S(1)} %constant_dynamic-update-slice_fusion) | copy-start | bytes 368644
  11.9 0.7 copy-start.6
  11.9 0.7 copy-start.7
  11.9 0.7 copy-start.8
  32.3 6.8 %copy-start.16 = (s32[1,1,32,16]{2,3,1,0:T(8,128)S(1)}, s32[1,1,32,16]{2,3,1,0:T(8,128)}, u32[]{:S(2)}) copy-start(s32[1,1,32,16]{2,3,1,0:T(8,128)} %param.17) | copy-start | bytes 6148
  32.3 7.6 %copy-start.4 = (bf16[16,144]{1,0:T(8,128)(2,1)S(1)}, bf16[16,144]{1,0:T(8,128)(2,1)}, u32[]{:S(2)}) copy-start(bf16[16,144]{1,0:T(8,128)(2,1)} %param.12) | copy-start | bytes 13828
  32.3 55.1 %all-to-all-start = ((bf16[32,264,128]{2,1,0:T(8,128)(2,1)}), bf16[32,264,128]{2,1,0:T(8,128)(2,1)S(1)}, u32[]{:S(2)}, u32[]{:S(2)}) async-start(bf16[32,264,128]{2,1,0:T(8,128)(2,1)} %shard_map.91), calls=%async_computation | async-start | bytes 4325376 | tf_op jit(solution)/shard_map/all_to_all | solution.py:335
  87.3 1.3 copy-start.1
  167.8 5.4 %collective-permute-start.3 = (bf16[16,128]{1,0:T(8,128)(2,1)S(1)}, bf16[16,128]{1,0:T(8,128)(2,1)S(1)}, u32[]{:S(2)}, u32[]{:S(2)}) collective-permute-start(bf16[16,128]{1,0:T(8,128)(2,1)S(1)} %get-tuple-element.11), channel_id=1, source_target_pairs={{1,0},{2,1},{3,2},{5,4},{6,5},{7,6},{9,8},{10,9},{11,10},{13,12},{... | collective-permute-start | bytes 12296 | tf_op jit(solution)/shard_map/ppermute | solution.py:21
  171.2 4.4 %collective-permute-start.2 = (bf16[16,128]{1,0:T(8,128)(2,1)S(1)}, bf16[16,128]{1,0:T(8,128)(2,1)S(1)}, u32[]{:S(2)}, u32[]{:S(2)}) collective-permute-start(bf16[16,128]{1,0:T(8,128)(2,1)S(1)} %get-tuple-element.12), channel_id=1, source_target_pairs={{0,1},{1,2},{2,3},{4,5},{5,6},{6,7},{8,9},{9,10},{10,11},{12,13},{... | collective-permute-start | bytes 12296 | tf_op jit(solution)/shard_map/ppermute | solution.py:21
  173.2 10.7 %copy-start.11 = (bf16[16,128]{1,0:T(8,128)(2,1)}, bf16[16,128]{1,0:T(8,128)(2,1)S(1)}, u32[]{:S(2)}) copy-start(bf16[16,128]{1,0:T(8,128)(2,1)S(1)} %collective-permute-done.3.below_ref) | copy-start | bytes 12292
  175.6 8.3 %copy-start.12 = (bf16[16,128]{1,0:T(8,128)(2,1)}, bf16[16,128]{1,0:T(8,128)(2,1)S(1)}, u32[]{:S(2)}) copy-start(bf16[16,128]{1,0:T(8,128)(2,1)S(1)} %collective-permute-done.2.above_ref) | copy-start | bytes 12292
  176.4 7.3 %collective-permute-start.5 = (bf16[16,1280]{1,0:T(8,128)(2,1)S(1)}, bf16[16,1280]{1,0:T(8,128)(2,1)S(1)}, u32[]{:S(2)}, u32[]{:S(2)}) collective-permute-start(bf16[16,1280]{1,0:T(8,128)(2,1)S(1)} %get-tuple-element.15), channel_id=1, source_target_pairs={{4,0},{8,4},{12,8},{16,12},{20,16},{24,20},{28,24},{5,1},{9,5},{13... | collective-permute-start | bytes 122888 | tf_op jit(solution)/shard_map/ppermute | solution.py:21
  178.3 5.6 %collective-permute-start.4 = (bf16[16,1280]{1,0:T(8,128)(2,1)S(1)}, bf16[16,1280]{1,0:T(8,128)(2,1)S(1)}, u32[]{:S(2)}, u32[]{:S(2)}) collective-permute-start(bf16[16,1280]{1,0:T(8,128)(2,1)S(1)} %get-tuple-element.16), channel_id=1, source_target_pairs={{0,4},{4,8},{8,12},{12,16},{16,20},{20,24},{24,28},{1,5},{5,9},{9,... | collective-permute-start | bytes 122888 | tf_op jit(solution)/shard_map/ppermute | solution.py:21
  183.6 0.6 copy-start.9
  183.9 0.6 copy-start.10
where the time goes:
time: 274 us; the launch traced here: 272 us
  Pallas kernels  186 us (68%)
  waiting for transfers between devices  49 us (18%)
  starting transfers between devices  23.5 us (9%)
  local copies, waits for them, and re-layouts  11.7 us (4%)
    pallas_call x1, Pallas kernels, local(): call(texture_kernel, jax.ShapeDtypeStruct((channels, AR_DEV, TL), half),...  87.6 us
    pallas_call x1, Pallas kernels, local(): call(join_kernel, (jax.ShapeDtypeStruct((AR_DEV * channels, TL), half), j...  78.4 us
    all_to_all x1, waiting for transfers between devices, local(): lax.all_to_all(payload, ('cam', 'row'), split_axis=0, concat_axis=0, tile...  46.4 us
    pallas_call x1, Pallas kernels, local(): call(send_kernel, jax.ShapeDtypeStruct((peers, message, TL), half), [pltp...  19.6 us
    ppermute x6, starting transfers between devices, neighbour(): return lax.ppermute(cells, axis, pairs)  17.1 us
    unnamed x60, local copies, waits for them, and re-layouts  8.99 us
    all_to_all x1, starting transfers between devices, local(): lax.all_to_all(payload, ('cam', 'row'), split_axis=0, concat_axis=0, tile...  6.42 us
  transfers between devices with their start and end apart: 7, of which 3 were waited for; matrix products, arithmetic and copies ran while one was open for 2% of the time, Pallas kernels for 0%

commit v1 on v0

--- a/solution.py
+++ b/solution.py
@@ -28,6 +28,10 @@
     ]
     stacked = jnp.stack(rows, axis=1 if channel_major else 0)
     return stacked.reshape(-1, stacked.shape[-1])
+
+
+def turn(cells, amount):
+    return pltpu.roll(cells, lax.rem(amount, TL), 1)
 
 
 def lanes_of(shape):
@@ -193,12 +197,12 @@
         def one(s, carry):
             left, right = carry
             for u in range(unroll):
-                base = pl.multiple_of(((i * (TL // unroll) + s) * unroll + u) * channels, channels)
+                t = s * unroll + u
+                base = pl.multiple_of((i * TL + t) * channels, channels)
                 cells = cells_ref[pl.ds(base, channels), :].astype(jnp.bfloat16)
                 joined_ref[pl.ds(base, channels), :] = cells
-                back = pltpu.roll(cells, TL - 1, 1)
-                left = jnp.where(lanes == TL - 1, back, pltpu.roll(left, TL - 1, 1))
-                right = jnp.where(lanes == TL - 1, cells, pltpu.roll(right, TL - 1, 1))
+                left = jnp.where(lanes == t, turn(cells, t), left)
+                right = jnp.where(lanes == t, turn(cells, t + 1), right)
             return left, right
 
         zero = jnp.zeros((channels, TL), jnp.bfloat16)
@@ -237,19 +241,16 @@
     def _(i):
         cols = pl.ds(pl.multiple_of(i * TL, TL), TL)
 
-        def one(s, carry):
-            before, after = carry
+        before = before_ref[:, cols]
+        after = after_ref[:, cols]
+
+        @pl.loop(0, TL // unroll)
+        def _(s):
             for u in range(unroll):
-                t = (i * (TL // unroll) + s) * unroll + u
-                cells = joined_ref[pl.ds(pl.multiple_of(t * channels, channels), channels), :]
-                place(t + 1, cells, before, after)
-                before = pltpu.roll(before, TL - 1, 1)
-                after = pltpu.roll(after, TL - 1, 1)
-            return before, after
-
-        lax.fori_loop(
-            0, TL // unroll, one, (before_ref[:, cols], pltpu.roll(after_ref[:, cols], TL - 1, 1))
-        )
+                t = s * unroll + u
+                row = i * TL + t
+                cells = joined_ref[pl.ds(pl.multiple_of(row * channels, channels), channels), :]
+                place(row + 1, cells, turn(before, TL - t), turn(after, TL - 1 - t))
 
     pair = 2 * GROUP
 

time: 274 us -> 160 us (0.58)
  Pallas kernels: 186 us -> 71.2 us
    pallas_call x1, Pallas kernels: 78.4 us -> 20.5 us  [local(): call(join_kernel, (jax.ShapeDtypeStruct((AR_DEV * channels, TL), half), j...]
    pallas_call x1, Pallas kernels: 87.6 us -> 31.1 us  [local(): call(texture_kernel, jax.ShapeDtypeStruct((channels, AR_DEV, TL), half),...]
  transfers between devices with their start and end apart: 7 -> 7, of which waited for: 3 -> 3; matrix products, arithmetic and copies ran while one was open for 2% -> 4% of each run, Pallas kernels for 0% -> 0%
where the time goes in v1:
time: 160 us; the launch traced here: 158 us
  Pallas kernels  71.2 us (44%)
  waiting for transfers between devices  49 us (31%)
  starting transfers between devices  23.5 us (15%)
  local copies, waits for them, and re-layouts  11.7 us (7%)
  other arithmetic  2.05 us (1%)
    all_to_all x1, waiting for transfers between devices, local(): lax.all_to_all(payload, ('cam', 'row'), split_axis=0, concat_axis=0, tile...  46.4 us
    pallas_call x1, Pallas kernels, local(): call(texture_kernel, jax.ShapeDtypeStruct((channels, AR_DEV, TL), half),...  31.1 us
    pallas_call x1, Pallas kernels, local(): call(join_kernel, (jax.ShapeDtypeStruct((AR_DEV * channels, TL), half), j...  20.5 us
    pallas_call x1, Pallas kernels, local(): call(send_kernel, jax.ShapeDtypeStruct((peers, message, TL), half), [pltp...  19.6 us
    ppermute x6, starting transfers between devices, neighbour(): return lax.ppermute(cells, axis, pairs)  17.1 us
    unnamed x60, local copies, waits for them, and re-layouts  8.99 us
    all_to_all x1, starting transfers between devices, local(): lax.all_to_all(payload, ('cam', 'row'), split_axis=0, concat_axis=0, tile...  6.42 us
  transfers between devices with their start and end apart: 7, of which 3 were waited for; matrix products, arithmetic and copies ran while one was open for 4% of the time, Pallas kernels for 0%

profile of v1, /device:TPU:11, one launch (start us, length us, event | category | flops | bytes accessed | tf_op | source)
XLA Modules:
  0.0 157.7 jit_solution(17621949897017233664)
XLA Ops:
  0.0 2.8 %copy.24 = bf16[1,16,32,2048]{3,1,2,0:T(8,128)(2,1)S(1)} copy(bf16[1,16,32,2048]{3,2,1,0:T(8,128)(2,1)} %param.9) | data formatting | bytes 4194304 | tf_op args[0]
  2.9 2.1 %collective-permute-start.1 = (bf16[2,16,2048]{2,1,0:T(8,128)(2,1)S(1)}, bf16[2,16,2048]{2,1,0:T(8,128)(2,1)S(1)}, u32[]{:S(2)}, u32[]{:S(2)}) collective-permute-start(bf16[2,16,2048]{2,1,0:T(8,128)(2,1)S(1)} %get-tuple-element.13), channel_id=1, source_target_pairs={{1,0},{2,1},{3,2},{5,4},{6,5},{7,6},{9,8},{10,9},{11,10},{13,12},{... | collective-permute-start | bytes 393224 | tf_op jit(solution)/shard_map/ppermute | solution.py:21
  4.9 3.2 %collective-permute-start = (bf16[2,16,2048]{2,1,0:T(8,128)(2,1)S(1)}, bf16[2,16,2048]{2,1,0:T(8,128)(2,1)S(1)}, u32[]{:S(2)}, u32[]{:S(2)}) collective-permute-start(bf16[2,16,2048]{2,1,0:T(8,128)(2,1)S(1)} %get-tuple-element.14), channel_id=1, source_target_pairs={{0,1},{1,2},{2,3},{4,5},{5,6},{6,7},{8,9},{9,10},{10,11},{12,13},{... | collective-permute-start | bytes 393224 | tf_op jit(solution)/shard_map/ppermute | solution.py:21
  9.2 0.6 pad_add_fusion.place_ref
  9.8 0.7 copy.17
  10.4 0.7 copy.18
  11.1 0.7 copy.19
  11.9 0.6 copy-done.6
  12.6 19.6 %shard_map.91 = bf16[32,264,128]{2,1,0:T(8,128)(2,1)} custom-call(s32[2]{0:T(128)} %pad_add_fusion.place_ref, s32[32,16]{1,0:T(8,128)} %bitcast.70, s32[32,16]{1,0:T(8,128)} %bitcast.71, s32[32,16]{1,0:T(8,128)} %bitcast.72, s32[1,32]{1,0:T(1,128)} %bitcast.73, bf16[32,16,2048]{2,1,0:T(8,128)(2,1)} %bitcast.66, bf16[2,16,2048]{2,1,0:T(8,128)(2,1)} %copy-done.8, ...), custom_call_target="tpu_custom_call" | custom-call | tf_op jit(solution)/shard_map/pallas_call | solution.py:314
  32.3 6.4 %all-to-all-start = ((bf16[32,264,128]{2,1,0:T(8,128)(2,1)}), bf16[32,264,128]{2,1,0:T(8,128)(2,1)S(1)}, u32[]{:S(2)}, u32[]{:S(2)}) async-start(bf16[32,264,128]{2,1,0:T(8,128)(2,1)} %shard_map.91), calls=%async_computation | async-start | bytes 4325376 | tf_op jit(solution)/shard_map/all_to_all | solution.py:336
  39.2 0.7 reshape.17.tile_ref
  40.2 0.7 and_convert_fusion.residual_ref
  40.9 46.4 %all-to-all-done.incoming_ref = bf16[32,264,128]{2,1,0:T(8,128)(2,1)S(1)} async-done(((bf16[32,264,128]{2,1,0:T(8,128)(2,1)}), bf16[32,264,128]{2,1,0:T(8,128)(2,1)S(1)}, u32[]{:S(2)}, u32[]{:S(2)}) %all-to-all-start) | async-done | bytes 2162720 | tf_op jit(solution)/shard_map/all_to_all | solution.py:336
  87.3 1.3 copy-done.1
  88.7 20.5 %shard_map.92 = (bf16[16384,128]{1,0:T(8,128)(2,1)}, bf16[16,1024]{1,0:T(8,128)(2,1)}, bf16[16,1024]{1,0:T(8,128)(2,1)}) custom-call(s32[1,512]{1,0:T(1,128)} %reshape.17.tile_ref, bf16[32,264,128]{2,1,0:T(8,128)(2,1)} %copy-done.1), custom_call_target="tpu_custom_call" | custom-call | tf_op jit(solution)/shard_map/pallas_call | solution.py:337
  109.2 0.7 fusion
  109.9 3.4 %collective-permute-start.3 = (bf16[16,128]{1,0:T(8,128)(2,1)S(1)}, bf16[16,128]{1,0:T(8,128)(2,1)S(1)}, u32[]{:S(2)}, u32[]{:S(2)}) collective-permute-start(bf16[16,128]{1,0:T(8,128)(2,1)S(1)} %get-tuple-element.11), channel_id=1, source_target_pairs={{1,0},{2,1},{3,2},{5,4},{6,5},{7,6},{9,8},{10,9},{11,10},{13,12},{... | collective-permute-start | bytes 12296 | tf_op jit(solution)/shard_map/ppermute | solution.py:21
  113.3 1.9 %collective-permute-start.2 = (bf16[16,128]{1,0:T(8,128)(2,1)S(1)}, bf16[16,128]{1,0:T(8,128)(2,1)S(1)}, u32[]{:S(2)}, u32[]{:S(2)}) collective-permute-start(bf16[16,128]{1,0:T(8,128)(2,1)S(1)} %get-tuple-element.12), channel_id=1, source_target_pairs={{0,1},{1,2},{2,3},{4,5},{5,6},{6,7},{8,9},{9,10},{10,11},{12,13},{... | collective-permute-start | bytes 12296 | tf_op jit(solution)/shard_map/ppermute | solution.py:21
  115.3 2.3 %collective-permute-done.2.above_ref = bf16[16,128]{1,0:T(8,128)(2,1)S(1)} collective-permute-done((bf16[16,128]{1,0:T(8,128)(2,1)S(1)}, bf16[16,128]{1,0:T(8,128)(2,1)S(1)}, u32[]{:S(2)}, u32[]{:S(2)}) %collective-permute-start.2) | collective-permute-done | bytes 4128 | tf_op jit(solution)/shard_map/ppermute | solution.py:21
  117.6 0.8 pad_maximum_fusion
  118.4 1.9 %collective-permute-start.5 = (bf16[16,1280]{1,0:T(8,128)(2,1)S(1)}, bf16[16,1280]{1,0:T(8,128)(2,1)S(1)}, u32[]{:S(2)}, u32[]{:S(2)}) collective-permute-start(bf16[16,1280]{1,0:T(8,128)(2,1)S(1)} %get-tuple-element.15), channel_id=1, source_target_pairs={{4,0},{8,4},{12,8},{16,12},{20,16},{24,20},{28,24},{5,1},{9,5},{13... | collective-permute-start | bytes 122888 | tf_op jit(solution)/shard_map/ppermute | solution.py:21
  120.4 4.5 %collective-permute-start.4 = (bf16[16,1280]{1,0:T(8,128)(2,1)S(1)}, bf16[16,1280]{1,0:T(8,128)(2,1)S(1)}, u32[]{:S(2)}, u32[]{:S(2)}) collective-permute-start(bf16[16,1280]{1,0:T(8,128)(2,1)S(1)} %get-tuple-element.16), channel_id=1, source_target_pairs={{0,4},{4,8},{8,12},{12,16},{16,20},{20,24},{24,28},{1,5},{5,9},{9,... | collective-permute-start | bytes 122888 | tf_op jit(solution)/shard_map/ppermute | solution.py:21
  125.0 0.7 copy.25
  126.6 31.1 %shard_map.93 = bf16[16,1024,128]{2,1,0:T(8,128)(2,1)} custom-call(bf16[16384,128]{1,0:T(8,128)(2,1)} %get-tuple-element.8.joined_ref, bf16[16,128]{1,0:T(8,128)(2,1)} %copy-done.12, bf16[16,128]{1,0:T(8,128)(2,1)} %copy-done.11, bf16[16,1280]{1,0:T(8,128)(2,1)} %copy-done.10, bf16[16,1280]{1,0:T(8,128)(2,1)} %copy-done.9, bf16[128,480]{1,0:T(8,128)(2,1)} %bitcast.67, ...), custom_call_target="tpu_custom_call" | custom-call | tf_op jit(solution)/shard_map/pallas_call | solution.py:363
  (71 shorter events, 3.1 us)
Async XLA Ops:
  0.0 8.2 %copy-start.2 = (bf16[16,144]{1,0:T(8,128)(2,1)S(1)}, bf16[16,144]{1,0:T(8,128)(2,1)}, u32[]{:S(2)}) copy-start(bf16[16,144]{1,0:T(8,128)(2,1)} %param.10) | copy-start | bytes 13828
  0.0 8.7 %copy-start.3 = (bf16[16,144]{1,0:T(8,128)(2,1)S(1)}, bf16[16,144]{1,0:T(8,128)(2,1)}, u32[]{:S(2)}) copy-start(bf16[16,144]{1,0:T(8,128)(2,1)} %param.11) | copy-start | bytes 13828
  0.0 9.8 %copy-start.13 = (s32[1,1,32,16]{2,3,1,0:T(8,128)S(1)}, s32[1,1,32,16]{2,3,1,0:T(8,128)}, u32[]{:S(2)}) copy-start(s32[1,1,32,16]{2,3,1,0:T(8,128)} %param.13) | copy-start | bytes 6148
  0.0 10.4 %copy-start.14 = (s32[1,1,32,16]{2,3,1,0:T(8,128)S(1)}, s32[1,1,32,16]{2,3,1,0:T(8,128)}, u32[]{:S(2)}) copy-start(s32[1,1,32,16]{2,3,1,0:T(8,128)} %param.14) | copy-start | bytes 6148
  0.0 11.1 %copy-start.15 = (s32[1,1,32,16]{2,3,1,0:T(8,128)S(1)}, s32[1,1,32,16]{2,3,1,0:T(8,128)}, u32[]{:S(2)}) copy-start(s32[1,1,32,16]{2,3,1,0:T(8,128)} %param.15) | copy-start | bytes 6148
  2.8 9.1 %copy-start = (bf16[1,16,32,2048]{3,1,2,0:T(8,128)(2,1)}, bf16[1,16,32,2048]{3,1,2,0:T(8,128)(2,1)S(1)}, u32[]{:S(2)}) copy-start(bf16[1,16,32,2048]{3,1,2,0:T(8,128)(2,1)S(1)} %copy.24) | copy-start | bytes 6291460
  2.9 9.0 %collective-permute-start.1 = (bf16[2,16,2048]{2,1,0:T(8,128)(2,1)S(1)}, bf16[2,16,2048]{2,1,0:T(8,128)(2,1)S(1)}, u32[]{:S(2)}, u32[]{:S(2)}) collective-permute-start(bf16[2,16,2048]{2,1,0:T(8,128)(2,1)S(1)} %get-tuple-element.13), channel_id=1, source_target_pairs={{1,0},{2,1},{3,2},{5,4},{6,5},{7,6},{9,8},{10,9},{11,10},{13,12},{... | collective-permute-start | bytes 393224 | tf_op jit(solution)/shard_map/ppermute | solution.py:21
  4.9 6.9 %collective-permute-start = (bf16[2,16,2048]{2,1,0:T(8,128)(2,1)S(1)}, bf16[2,16,2048]{2,1,0:T(8,128)(2,1)S(1)}, u32[]{:S(2)}, u32[]{:S(2)}) collective-permute-start(bf16[2,16,2048]{2,1,0:T(8,128)(2,1)S(1)} %get-tuple-element.14), channel_id=1, source_target_pairs={{0,1},{1,2},{2,3},{4,5},{5,6},{6,7},{8,9},{9,10},{10,11},{12,13},{... | collective-permute-start | bytes 393224 | tf_op jit(solution)/shard_map/ppermute | solution.py:21
  8.7 3.2 %copy-start.5 = (bf16[8,16,480]{2,1,0:T(8,128)(2,1)}, bf16[8,16,480]{2,1,0:T(8,128)(2,1)S(1)}, u32[]{:S(2)}) copy-start(bf16[8,16,480]{2,1,0:T(8,128)(2,1)S(1)} %constant_dynamic-update-slice_fusion) | copy-start | bytes 368644
  11.9 0.7 copy-start.6
  11.9 0.7 copy-start.7
  11.9 0.7 copy-start.8
  32.3 6.8 %copy-start.16 = (s32[1,1,32,16]{2,3,1,0:T(8,128)S(1)}, s32[1,1,32,16]{2,3,1,0:T(8,128)}, u32[]{:S(2)}) copy-start(s32[1,1,32,16]{2,3,1,0:T(8,128)} %param.17) | copy-start | bytes 6148
  32.3 7.6 %copy-start.4 = (bf16[16,144]{1,0:T(8,128)(2,1)S(1)}, bf16[16,144]{1,0:T(8,128)(2,1)}, u32[]{:S(2)}) copy-start(bf16[16,144]{1,0:T(8,128)(2,1)} %param.12) | copy-start | bytes 13828
  32.3 55.1 %all-to-all-start = ((bf16[32,264,128]{2,1,0:T(8,128)(2,1)}), bf16[32,264,128]{2,1,0:T(8,128)(2,1)S(1)}, u32[]{:S(2)}, u32[]{:S(2)}) async-start(bf16[32,264,128]{2,1,0:T(8,128)(2,1)} %shard_map.91), calls=%async_computation | async-start | bytes 4325376 | tf_op jit(solution)/shard_map/all_to_all | solution.py:336
  87.3 1.3 copy-start.1
  109.9 5.4 %collective-permute-start.3 = (bf16[16,128]{1,0:T(8,128)(2,1)S(1)}, bf16[16,128]{1,0:T(8,128)(2,1)S(1)}, u32[]{:S(2)}, u32[]{:S(2)}) collective-permute-start(bf16[16,128]{1,0:T(8,128)(2,1)S(1)} %get-tuple-element.11), channel_id=1, source_target_pairs={{1,0},{2,1},{3,2},{5,4},{6,5},{7,6},{9,8},{10,9},{11,10},{13,12},{... | collective-permute-start | bytes 12296 | tf_op jit(solution)/shard_map/ppermute | solution.py:21
  113.3 4.4 %collective-permute-start.2 = (bf16[16,128]{1,0:T(8,128)(2,1)S(1)}, bf16[16,128]{1,0:T(8,128)(2,1)S(1)}, u32[]{:S(2)}, u32[]{:S(2)}) collective-permute-start(bf16[16,128]{1,0:T(8,128)(2,1)S(1)} %get-tuple-element.12), channel_id=1, source_target_pairs={{0,1},{1,2},{2,3},{4,5},{5,6},{6,7},{8,9},{9,10},{10,11},{12,13},{... | collective-permute-start | bytes 12296 | tf_op jit(solution)/shard_map/ppermute | solution.py:21
  115.3 10.7 %copy-start.11 = (bf16[16,128]{1,0:T(8,128)(2,1)}, bf16[16,128]{1,0:T(8,128)(2,1)S(1)}, u32[]{:S(2)}) copy-start(bf16[16,128]{1,0:T(8,128)(2,1)S(1)} %collective-permute-done.3.below_ref) | copy-start | bytes 12292
  117.6 8.3 %copy-start.12 = (bf16[16,128]{1,0:T(8,128)(2,1)}, bf16[16,128]{1,0:T(8,128)(2,1)S(1)}, u32[]{:S(2)}) copy-start(bf16[16,128]{1,0:T(8,128)(2,1)S(1)} %collective-permute-done.2.above_ref) | copy-start | bytes 12292
  118.4 7.3 %collective-permute-start.5 = (bf16[16,1280]{1,0:T(8,128)(2,1)S(1)}, bf16[16,1280]{1,0:T(8,128)(2,1)S(1)}, u32[]{:S(2)}, u32[]{:S(2)}) collective-permute-start(bf16[16,1280]{1,0:T(8,128)(2,1)S(1)} %get-tuple-element.15), channel_id=1, source_target_pairs={{4,0},{8,4},{12,8},{16,12},{20,16},{24,20},{28,24},{5,1},{9,5},{13... | collective-permute-start | bytes 122888 | tf_op jit(solution)/shard_map/ppermute | solution.py:21
  120.4 5.6 %collective-permute-start.4 = (bf16[16,1280]{1,0:T(8,128)(2,1)S(1)}, bf16[16,1280]{1,0:T(8,128)(2,1)S(1)}, u32[]{:S(2)}, u32[]{:S(2)}) collective-permute-start(bf16[16,1280]{1,0:T(8,128)(2,1)S(1)} %get-tuple-element.16), channel_id=1, source_target_pairs={{0,4},{4,8},{8,12},{12,16},{16,20},{20,24},{24,28},{1,5},{5,9},{9,... | collective-permute-start | bytes 122888 | tf_op jit(solution)/shard_map/ppermute | solution.py:21
  125.7 0.6 copy-start.9
  126.0 0.6 copy-start.10

commit v2 on v1

--- a/solution.py
+++ b/solution.py
@@ -1,5 +1,3 @@
-import functools
-
 import jax
 import jax.numpy as jnp
 from jax import lax
@@ -213,70 +211,97 @@
 
 
 def texture_kernel(
-    joined_ref, above_ref, below_ref, before_ref, after_ref, weight_ref, residual_ref, texture_ref, taps_ref
+    joined_ref, prev_ref, next_ref, above_ref, below_ref, before_ref, after_ref, weight_ref, residual_ref,
+    texture_ref, even_ref, odd_ref
 ):
     channels = texture_ref.shape[0]
-    tiles = texture_ref.shape[1]
+    step = pl.program_id(0)
+    blocks = pl.num_programs(0) - 1
     tap = 3 * channels
     reach = (GROUP + 2) * tap
     lanes = lanes_of((channels, TL))
-
-    def place(row, cells, before, after):
-        base = pl.multiple_of(row * tap, channels)
-        taps_ref[pl.ds(base, channels), :] = jnp.where(lanes == 0, before, pltpu.roll(cells, 1, 1))
-        taps_ref[pl.ds(base + channels, channels), :] = cells
-        taps_ref[pl.ds(base + 2 * channels, channels), :] = jnp.where(
+    tiles = blocks * TL
+
+    def place(taps_ref, row, cells, before, after):
+        base = row * tap
+        taps_ref[base : base + channels, :] = jnp.where(lanes == 0, before, pltpu.roll(cells, 1, 1))
+        taps_ref[base + channels : base + 2 * channels, :] = cells
+        taps_ref[base + 2 * channels : base + 3 * channels, :] = jnp.where(
             lanes == TL - 1, after, pltpu.roll(cells, TL - 1, 1)
         )
 
-    def corner(ref, k, back):
-        cells = ref[:, tiles + k * TL : tiles + (k + 1) * TL]
-        return pltpu.roll(cells, 1 if back else TL - 1, 1)
-
-    place(0, above_ref[...], corner(before_ref, 0, True), corner(after_ref, 0, False))
-    place(tiles + 1, below_ref[...], corner(before_ref, 1, True), corner(after_ref, 1, False))
-    unroll = 8
-
-    @pl.loop(0, tiles // TL)
-    def _(i):
-        cols = pl.ds(pl.multiple_of(i * TL, TL), TL)
-
-        before = before_ref[:, cols]
-        after = after_ref[:, cols]
-
-        @pl.loop(0, TL // unroll)
-        def _(s):
-            for u in range(unroll):
-                t = s * unroll + u
-                row = i * TL + t
-                cells = joined_ref[pl.ds(pl.multiple_of(row * channels, channels), channels), :]
-                place(row + 1, cells, turn(before, TL - t), turn(after, TL - 1 - t))
-
-    pair = 2 * GROUP
-
-    @pl.loop(0, tiles // pair)
-    def _(i):
-        base = pl.multiple_of(i * (pair * tap), pair * tap)
-        window = jnp.concatenate(
-            [
-                taps_ref[pl.ds(base, reach), :],
-                taps_ref[pl.ds(base + GROUP * tap, reach), :],
-            ],
-            axis=1,
-        )
-        rows = pl.multiple_of(i * (pair * channels), pair * channels)
-        own = jnp.concatenate(
-            [
-                joined_ref[pl.ds(rows, GROUP * channels), :],
-                joined_ref[pl.ds(rows + GROUP * channels, GROUP * channels), :],
-            ],
-            axis=1,
-        )
-        out = jnp.dot(weight_ref[...], window, preferred_element_type=jnp.float32)
-        out = out + jnp.dot(residual_ref[...], own, preferred_element_type=jnp.float32)
-        out = out.reshape(channels, GROUP, 2 * TL)
-        out = jnp.concatenate([out[:, :, :TL], out[:, :, TL:]], axis=1)
-        texture_ref[:, pl.ds(pl.multiple_of(i * pair, pair), pair), :] = out.astype(jnp.bfloat16)
+    def fill(taps_ref):
+        i = jnp.minimum(step, blocks - 1)
+        here = pl.ds(pl.multiple_of(i * TL, TL), TL)
+        first = pl.ds(pl.multiple_of(jnp.where(i == 0, tiles, (i - 1) * TL), TL), TL)
+        last = pl.ds(pl.multiple_of(jnp.where(i == blocks - 1, tiles + TL, (i + 1) * TL), TL), TL)
+        cells = jnp.where(i == 0, above_ref[...], prev_ref[...])
+        place(taps_ref, 0, cells, pltpu.roll(before_ref[:, first], 1, 1), after_ref[:, first])
+        cells = jnp.where(i == blocks - 1, below_ref[...], next_ref[...])
+        place(taps_ref, TL + 1, cells, before_ref[:, last], pltpu.roll(after_ref[:, last], TL - 1, 1))
+        before = before_ref[:, here]
+        after = after_ref[:, here]
+        for t in range(TL):
+            cells = joined_ref[t * channels : (t + 1) * channels, :]
+            place(taps_ref, t + 1, cells, pltpu.roll(before, (TL - t) % TL, 1), pltpu.roll(after, TL - 1 - t, 1))
+
+    def convolve(taps_ref):
+        pair = 2 * GROUP
+        for i in range(TL // pair):
+            base = i * pair * tap
+            window = jnp.concatenate(
+                [taps_ref[base + h * GROUP * tap : base + h * GROUP * tap + reach, :] for h in range(2)], axis=1
+            )
+            out = jnp.dot(weight_ref[...], window, preferred_element_type=jnp.float32)
+            own = jnp.concatenate(
+                [
+                    jnp.concatenate(
+                        [
+                            taps_ref[base + (h * GROUP + r + 1) * tap + channels : base + (h * GROUP + r + 1) * tap + 2 * channels, :]
+                            for r in range(GROUP)
+                        ],
+                        axis=0,
+                    )
+                    for h in range(2)
+                ],
+                axis=1,
+            )
+            out = out + jnp.dot(residual_ref[...], own, preferred_element_type=jnp.float32)
+            out = out.reshape(channels, GROUP, 2 * TL)
+            out = jnp.concatenate([out[:, :, :TL], out[:, :, TL:]], axis=1)
+            texture_ref[:, i * pair : (i + 1) * pair, :] = out.astype(jnp.bfloat16)
+
+    @pl.when(lax.rem(step, 2) == 0)
+    def _():
+        fill(even_ref)
+        convolve(odd_ref)
+
+    @pl.when(lax.rem(step, 2) == 1)
+    def _():
+        fill(odd_ref)
+        convolve(even_ref)
+
+
+def texture_call(joined, above, below, before, after, weight, residual):
+    channels = above.shape[0]
+    tiles = joined.shape[0] // channels
+    blocks = tiles // TL
+    def at(i):
+        return jnp.minimum(i, blocks - 1)
+    whole = lambda x: pl.BlockSpec(x.shape, lambda i: (0,) * x.ndim)
+    return pl.pallas_call(
+        texture_kernel,
+        grid=(blocks + 1,),
+        out_shape=jax.ShapeDtypeStruct((channels, tiles, TL), jnp.bfloat16),
+        in_specs=[
+            pl.BlockSpec((TL * channels, TL), lambda i: (at(i), 0)),
+            pl.BlockSpec((channels, TL), lambda i: (jnp.maximum(at(i) * TL - 1, 0), 0)),
+            pl.BlockSpec((channels, TL), lambda i: (jnp.minimum((at(i) + 1) * TL, tiles - 1), 0)),
+        ] + [whole(x) for x in (above, below, before, after, weight, residual)],
+        out_specs=pl.BlockSpec((channels, TL, TL), lambda i: (0, jnp.maximum(i - 1, 0), 0)),
+        scratch_shapes=[pltpu.VMEM(((TL + 2) * 3 * channels, TL), jnp.bfloat16)] * 2,
+        compiler_params=pltpu.CompilerParams(vmem_limit_bytes=VMEM_BYTES),
+    )(joined, joined, joined, above, below, before, after, weight, residual)
 
 
 def call(kernel, outs, scratch, specs):
@@ -350,8 +375,8 @@
     )(recv_tile.reshape(1, entries), arrived)
     top = neighbour(joined[-channels:], "row", 1)
     bottom = neighbour(joined[:channels], "row", -1)
-    before = neighbour(jnp.concatenate([last, top, bottom], axis=1), "cam", 1)
-    after = neighbour(jnp.concatenate([first, top, bottom], axis=1), "cam", -1)
+    before = neighbour(jnp.concatenate([last, top, jnp.roll(bottom, 1, 1)], axis=1), "cam", 1)
+    after = neighbour(jnp.concatenate([first, jnp.roll(top, -1, 1), bottom], axis=1), "cam", -1)
     same = (
         lax.broadcasted_iota(jnp.int32, (channels, GROUP, GROUP, channels), 0)
         == lax.broadcasted_iota(jnp.int32, (channels, GROUP, GROUP, channels), 3)
@@ -360,12 +385,7 @@
         == lax.broadcasted_iota(jnp.int32, (channels, GROUP, GROUP, channels), 2)
     )
     residual = same.astype(half).reshape(channels * GROUP, GROUP * channels)
-    return call(
-        texture_kernel,
-        jax.ShapeDtypeStruct((channels, AR_DEV, TL), half),
-        [pltpu.VMEM(((AR_DEV + 2) * 3 * channels, TL), half)],
-        [WHOLE] * 7,
-    )(joined, top, bottom, before, after, band(conv_uv, True), residual)
+    return texture_call(joined, top, bottom, before, after, band(conv_uv, True), residual)
 
 
 def solution(mesh):

time: 160 us -> 141 us (0.88)
  Pallas kernels: 71.2 us -> 50.1 us
  waiting for transfers between devices: 49 us -> 52.2 us
  local copies, waits for them, and re-layouts: 11.7 us -> 13.5 us
    pallas_call x1, Pallas kernels: 31.1 us -> 9.92 us  [texture_call(): pl.pallas_call(texture_kernel, grid=(blocks + 1,), out_shape=jax.ShapeDty...]
    ppermute x6, waiting for transfers between devices: 2.62 us -> 5.75 us  [neighbour(): return lax.ppermute(cells, axis, pairs)]
    concatenate x0 -> x2, local copies, waits for them, and re-layouts: none -> 1.69 us  [the longest x1 0.84 us: local(): jnp.concatenate([last, top, jnp.roll(bottom, 1, 1)], axis=1)]
  transfers between devices with their start and end apart: 7 -> 7, of which waited for: 3 -> 3; matrix products, arithmetic and copies ran while one was open for 4% -> 6% of each run, Pallas kernels for 0% -> 0%
where the time goes in v2:
time: 141 us; the launch traced here: 140 us
  waiting for transfers between devices  52.2 us (37%)
  Pallas kernels  50.1 us (36%)
  starting transfers between devices  22.4 us (16%)
  local copies, waits for them, and re-layouts  13.5 us (10%)
    all_to_all x1, waiting for transfers between devices, local(): lax.all_to_all(payload, ('cam', 'row'), split_axis=0, concat_axis=0, tile...  46.4 us
    pallas_call x1, Pallas kernels, local(): call(join_kernel, (jax.ShapeDtypeStruct((AR_DEV * channels, TL), half), j...  20.5 us
    pallas_call x1, Pallas kernels, local(): call(send_kernel, jax.ShapeDtypeStruct((peers, message, TL), half), [pltp...  19.7 us
    ppermute x6, starting transfers between devices, neighbour(): return lax.ppermute(cells, axis, pairs)  16.1 us
    pallas_call x1, Pallas kernels, texture_call(): pl.pallas_call(texture_kernel, grid=(blocks + 1,), out_shape=jax.ShapeDty...  9.92 us
    unnamed x60, local copies, waits for them, and re-layouts  8.98 us
    all_to_all x1, starting transfers between devices, local(): lax.all_to_all(payload, ('cam', 'row'), split_axis=0, concat_axis=0, tile...  6.3 us
    ppermute x6, waiting for transfers between devices, neighbour(): return lax.ppermute(cells, axis, pairs)  5.75 us
  transfers between devices with their start and end apart: 7, of which 3 were waited for; matrix products, arithmetic and copies ran while one was open for 6% of the time, Pallas kernels for 0%

profile of v2, /device:TPU:11, one launch (start us, length us, event | category | flops | bytes accessed | tf_op | source)
XLA Modules:
  0.0 139.7 jit_solution(5962359588933536266)
XLA Ops:
  0.0 2.8 %copy.24 = bf16[1,16,32,2048]{3,1,2,0:T(8,128)(2,1)S(1)} copy(bf16[1,16,32,2048]{3,2,1,0:T(8,128)(2,1)} %param.9) | data formatting | bytes 4194304 | tf_op args[0]
  2.9 2.1 %collective-permute-start.1 = (bf16[2,16,2048]{2,1,0:T(8,128)(2,1)S(1)}, bf16[2,16,2048]{2,1,0:T(8,128)(2,1)S(1)}, u32[]{:S(2)}, u32[]{:S(2)}) collective-permute-start(bf16[2,16,2048]{2,1,0:T(8,128)(2,1)S(1)} %get-tuple-element.13), channel_id=1, source_target_pairs={{1,0},{2,1},{3,2},{5,4},{6,5},{7,6},{9,8},{10,9},{11,10},{13,12},{... | collective-permute-start | bytes 393224 | tf_op jit(solution)/shard_map/ppermute | solution.py:19
  4.9 3.2 %collective-permute-start = (bf16[2,16,2048]{2,1,0:T(8,128)(2,1)S(1)}, bf16[2,16,2048]{2,1,0:T(8,128)(2,1)S(1)}, u32[]{:S(2)}, u32[]{:S(2)}) collective-permute-start(bf16[2,16,2048]{2,1,0:T(8,128)(2,1)S(1)} %get-tuple-element.14), channel_id=1, source_target_pairs={{0,1},{1,2},{2,3},{4,5},{5,6},{6,7},{8,9},{9,10},{10,11},{12,13},{... | collective-permute-start | bytes 393224 | tf_op jit(solution)/shard_map/ppermute | solution.py:19
  9.2 0.7 pad_add_fusion.place_ref
  9.9 0.7 copy.17
  10.5 0.7 copy.18
  11.2 0.7 copy.19
  12.7 19.7 %shard_map.91 = bf16[32,264,128]{2,1,0:T(8,128)(2,1)} custom-call(s32[2]{0:T(128)} %pad_add_fusion.place_ref, s32[32,16]{1,0:T(8,128)} %bitcast.72, s32[32,16]{1,0:T(8,128)} %bitcast.73, s32[32,16]{1,0:T(8,128)} %bitcast.74, s32[1,32]{1,0:T(1,128)} %bitcast.77, bf16[32,16,2048]{2,1,0:T(8,128)(2,1)} %bitcast.68, bf16[2,16,2048]{2,1,0:T(8,128)(2,1)} %copy-done.8, ...), custom_call_target="tpu_custom_call" | custom-call | tf_op jit(solution)/shard_map/pallas_call | solution.py:339
  32.4 6.3 %all-to-all-start = ((bf16[32,264,128]{2,1,0:T(8,128)(2,1)}), bf16[32,264,128]{2,1,0:T(8,128)(2,1)S(1)}, u32[]{:S(2)}, u32[]{:S(2)}) async-start(bf16[32,264,128]{2,1,0:T(8,128)(2,1)} %shard_map.91), calls=%async_computation | async-start | bytes 4325376 | tf_op jit(solution)/shard_map/all_to_all | solution.py:361
  40.2 0.7 and_convert_fusion.residual_ref
  40.9 46.4 %all-to-all-done.incoming_ref = bf16[32,264,128]{2,1,0:T(8,128)(2,1)S(1)} async-done(((bf16[32,264,128]{2,1,0:T(8,128)(2,1)}), bf16[32,264,128]{2,1,0:T(8,128)(2,1)S(1)}, u32[]{:S(2)}, u32[]{:S(2)}) %all-to-all-start) | async-done | bytes 2162720 | tf_op jit(solution)/shard_map/all_to_all | solution.py:361
  87.3 1.3 copy-done.1
  88.7 20.5 %shard_map.92 = (bf16[16384,128]{1,0:T(8,128)(2,1)}, bf16[16,1024]{1,0:T(8,128)(2,1)}, bf16[16,1024]{1,0:T(8,128)(2,1)}) custom-call(s32[1,512]{1,0:T(1,128)} %reshape.17.tile_ref, bf16[32,264,128]{2,1,0:T(8,128)(2,1)} %copy-done.1), custom_call_target="tpu_custom_call" | custom-call | tf_op jit(solution)/shard_map/pallas_call | solution.py:362
  109.2 0.7 fusion
  109.9 3.4 %collective-permute-start.3 = (bf16[16,128]{1,0:T(8,128)(2,1)S(1)}, bf16[16,128]{1,0:T(8,128)(2,1)S(1)}, u32[]{:S(2)}, u32[]{:S(2)}) collective-permute-start(bf16[16,128]{1,0:T(8,128)(2,1)S(1)} %get-tuple-element.11), channel_id=1, source_target_pairs={{1,0},{2,1},{3,2},{5,4},{6,5},{7,6},{9,8},{10,9},{11,10},{13,12},{... | collective-permute-start | bytes 12296 | tf_op jit(solution)/shard_map/ppermute | solution.py:19
  113.3 1.9 %collective-permute-start.2 = (bf16[16,128]{1,0:T(8,128)(2,1)S(1)}, bf16[16,128]{1,0:T(8,128)(2,1)S(1)}, u32[]{:S(2)}, u32[]{:S(2)}) collective-permute-start(bf16[16,128]{1,0:T(8,128)(2,1)S(1)} %get-tuple-element.12), channel_id=1, source_target_pairs={{0,1},{1,2},{2,3},{4,5},{5,6},{6,7},{8,9},{9,10},{10,11},{12,13},{... | collective-permute-start | bytes 12296 | tf_op jit(solution)/shard_map/ppermute | solution.py:19
  115.4 2.3 %collective-permute-done.2.above_ref = bf16[16,128]{1,0:T(8,128)(2,1)S(1)} collective-permute-done((bf16[16,128]{1,0:T(8,128)(2,1)S(1)}, bf16[16,128]{1,0:T(8,128)(2,1)S(1)}, u32[]{:S(2)}, u32[]{:S(2)}) %collective-permute-start.2) | collective-permute-done | bytes 4128 | tf_op jit(solution)/shard_map/ppermute | solution.py:19
  117.6 0.8 concatenate.12
  118.5 3.6 %collective-permute-start.4 = (bf16[16,1280]{1,0:T(8,128)(2,1)S(1)}, bf16[16,1280]{1,0:T(8,128)(2,1)S(1)}, u32[]{:S(2)}, u32[]{:S(2)}) collective-permute-start(bf16[16,1280]{1,0:T(8,128)(2,1)S(1)} %concatenate.12), channel_id=1, source_target_pairs={{0,4},{4,8},{8,12},{12,16},{16,20},{20,24},{24,28},{1,5},{5,9},{9,... | collective-permute-start | bytes 122888 | tf_op jit(solution)/shard_map/ppermute | solution.py:19
  122.1 0.8 concatenate.13
  123.0 1.9 %collective-permute-start.5 = (bf16[16,1280]{1,0:T(8,128)(2,1)S(1)}, bf16[16,1280]{1,0:T(8,128)(2,1)S(1)}, u32[]{:S(2)}, u32[]{:S(2)}) collective-permute-start(bf16[16,1280]{1,0:T(8,128)(2,1)S(1)} %concatenate.13), channel_id=1, source_target_pairs={{4,0},{8,4},{12,8},{16,12},{20,16},{24,20},{28,24},{5,1},{9,5},{13... | collective-permute-start | bytes 122888 | tf_op jit(solution)/shard_map/ppermute | solution.py:19
  125.0 0.7 copy.25
  125.7 3.5 %collective-permute-done.5.after_ref = bf16[16,1280]{1,0:T(8,128)(2,1)S(1)} collective-permute-done((bf16[16,1280]{1,0:T(8,128)(2,1)S(1)}, bf16[16,1280]{1,0:T(8,128)(2,1)S(1)}, u32[]{:S(2)}, u32[]{:S(2)}) %collective-permute-start.5) | collective-permute-done | bytes 40992 | tf_op jit(solution)/shard_map/ppermute | solution.py:19
  129.8 9.9 %shard_map.93 = bf16[16,1024,128]{2,1,0:T(8,128)(2,1)} custom-call(bf16[16384,128]{1,0:T(8,128)(2,1)} %get-tuple-element.8.joined_ref.prev_ref.next_ref, bf16[16384,128]{1,0:T(8,128)(2,1)} %get-tuple-element.8.joined_ref.prev_ref.next_ref, bf16[16384,128]{1,0:T(8,128)(2,1)} %get-tuple-element.8.joined_ref.prev_ref.next_ref, bf16[16,128]{1,0:T(8,128)(2,1)} %copy-done.10, ...), custom_call_target="tpu_custom_call" | custom-call | tf_op jit(solution)/shard_map/pallas_call | solution.py:292
  (74 shorter events, 4.2 us)
Async XLA Ops:
  0.0 8.2 %copy-start.2 = (bf16[16,144]{1,0:T(8,128)(2,1)S(1)}, bf16[16,144]{1,0:T(8,128)(2,1)}, u32[]{:S(2)}) copy-start(bf16[16,144]{1,0:T(8,128)(2,1)} %param.10) | copy-start | bytes 13828
  0.0 8.7 %copy-start.3 = (bf16[16,144]{1,0:T(8,128)(2,1)S(1)}, bf16[16,144]{1,0:T(8,128)(2,1)}, u32[]{:S(2)}) copy-start(bf16[16,144]{1,0:T(8,128)(2,1)} %param.11) | copy-start | bytes 13828
  0.0 9.9 %copy-start.13 = (s32[1,1,32,16]{2,3,1,0:T(8,128)S(1)}, s32[1,1,32,16]{2,3,1,0:T(8,128)}, u32[]{:S(2)}) copy-start(s32[1,1,32,16]{2,3,1,0:T(8,128)} %param.13) | copy-start | bytes 6148
  0.0 10.5 %copy-start.14 = (s32[1,1,32,16]{2,3,1,0:T(8,128)S(1)}, s32[1,1,32,16]{2,3,1,0:T(8,128)}, u32[]{:S(2)}) copy-start(s32[1,1,32,16]{2,3,1,0:T(8,128)} %param.14) | copy-start | bytes 6148
  0.0 11.2 %copy-start.15 = (s32[1,1,32,16]{2,3,1,0:T(8,128)S(1)}, s32[1,1,32,16]{2,3,1,0:T(8,128)}, u32[]{:S(2)}) copy-start(s32[1,1,32,16]{2,3,1,0:T(8,128)} %param.15) | copy-start | bytes 6148
  2.8 9.2 %copy-start = (bf16[1,16,32,2048]{3,1,2,0:T(8,128)(2,1)}, bf16[1,16,32,2048]{3,1,2,0:T(8,128)(2,1)S(1)}, u32[]{:S(2)}) copy-start(bf16[1,16,32,2048]{3,1,2,0:T(8,128)(2,1)S(1)} %copy.24) | copy-start | bytes 6291460
  2.9 9.1 %collective-permute-start.1 = (bf16[2,16,2048]{2,1,0:T(8,128)(2,1)S(1)}, bf16[2,16,2048]{2,1,0:T(8,128)(2,1)S(1)}, u32[]{:S(2)}, u32[]{:S(2)}) collective-permute-start(bf16[2,16,2048]{2,1,0:T(8,128)(2,1)S(1)} %get-tuple-element.13), channel_id=1, source_target_pairs={{1,0},{2,1},{3,2},{5,4},{6,5},{7,6},{9,8},{10,9},{11,10},{13,12},{... | collective-permute-start | bytes 393224 | tf_op jit(solution)/shard_map/ppermute | solution.py:19
  4.9 7.0 %collective-permute-start = (bf16[2,16,2048]{2,1,0:T(8,128)(2,1)S(1)}, bf16[2,16,2048]{2,1,0:T(8,128)(2,1)S(1)}, u32[]{:S(2)}, u32[]{:S(2)}) collective-permute-start(bf16[2,16,2048]{2,1,0:T(8,128)(2,1)S(1)} %get-tuple-element.14), channel_id=1, source_target_pairs={{0,1},{1,2},{2,3},{4,5},{5,6},{6,7},{8,9},{9,10},{10,11},{12,13},{... | collective-permute-start | bytes 393224 | tf_op jit(solution)/shard_map/ppermute | solution.py:19
  8.7 3.3 %copy-start.5 = (bf16[8,16,480]{2,1,0:T(8,128)(2,1)}, bf16[8,16,480]{2,1,0:T(8,128)(2,1)S(1)}, u32[]{:S(2)}) copy-start(bf16[8,16,480]{2,1,0:T(8,128)(2,1)S(1)} %constant_dynamic-update-slice_fusion) | copy-start | bytes 368644
  12.0 0.7 copy-start.6
  12.0 0.7 copy-start.7
  12.0 0.7 copy-start.8
  32.4 6.7 %copy-start.16 = (s32[1,1,32,16]{2,3,1,0:T(8,128)S(1)}, s32[1,1,32,16]{2,3,1,0:T(8,128)}, u32[]{:S(2)}) copy-start(s32[1,1,32,16]{2,3,1,0:T(8,128)} %param.17) | copy-start | bytes 6148
  32.4 7.4 %copy-start.4 = (bf16[16,144]{1,0:T(8,128)(2,1)S(1)}, bf16[16,144]{1,0:T(8,128)(2,1)}, u32[]{:S(2)}) copy-start(bf16[16,144]{1,0:T(8,128)(2,1)} %param.12) | copy-start | bytes 13828
  32.4 54.9 %all-to-all-start = ((bf16[32,264,128]{2,1,0:T(8,128)(2,1)}), bf16[32,264,128]{2,1,0:T(8,128)(2,1)S(1)}, u32[]{:S(2)}, u32[]{:S(2)}) async-start(bf16[32,264,128]{2,1,0:T(8,128)(2,1)} %shard_map.91), calls=%async_computation | async-start | bytes 4325376 | tf_op jit(solution)/shard_map/all_to_all | solution.py:361
  87.3 1.3 copy-start.1
  109.9 5.4 %collective-permute-start.3 = (bf16[16,128]{1,0:T(8,128)(2,1)S(1)}, bf16[16,128]{1,0:T(8,128)(2,1)S(1)}, u32[]{:S(2)}, u32[]{:S(2)}) collective-permute-start(bf16[16,128]{1,0:T(8,128)(2,1)S(1)} %get-tuple-element.11), channel_id=1, source_target_pairs={{1,0},{2,1},{3,2},{5,4},{6,5},{7,6},{9,8},{10,9},{11,10},{13,12},{... | collective-permute-start | bytes 12296 | tf_op jit(solution)/shard_map/ppermute | solution.py:19
  113.3 4.4 %collective-permute-start.2 = (bf16[16,128]{1,0:T(8,128)(2,1)S(1)}, bf16[16,128]{1,0:T(8,128)(2,1)S(1)}, u32[]{:S(2)}, u32[]{:S(2)}) collective-permute-start(bf16[16,128]{1,0:T(8,128)(2,1)S(1)} %get-tuple-element.12), channel_id=1, source_target_pairs={{0,1},{1,2},{2,3},{4,5},{5,6},{6,7},{8,9},{9,10},{10,11},{12,13},{... | collective-permute-start | bytes 12296 | tf_op jit(solution)/shard_map/ppermute | solution.py:19
  115.3 13.9 %copy-start.9 = (bf16[16,128]{1,0:T(8,128)(2,1)}, bf16[16,128]{1,0:T(8,128)(2,1)S(1)}, u32[]{:S(2)}) copy-start(bf16[16,128]{1,0:T(8,128)(2,1)S(1)} %collective-permute-done.3.below_ref) | copy-start | bytes 12292
  117.6 11.6 %copy-start.10 = (bf16[16,128]{1,0:T(8,128)(2,1)}, bf16[16,128]{1,0:T(8,128)(2,1)S(1)}, u32[]{:S(2)}) copy-start(bf16[16,128]{1,0:T(8,128)(2,1)S(1)} %collective-permute-done.2.above_ref) | copy-start | bytes 12292
  118.5 7.2 %collective-permute-start.4 = (bf16[16,1280]{1,0:T(8,128)(2,1)S(1)}, bf16[16,1280]{1,0:T(8,128)(2,1)S(1)}, u32[]{:S(2)}, u32[]{:S(2)}) collective-permute-start(bf16[16,1280]{1,0:T(8,128)(2,1)S(1)} %concatenate.12), channel_id=1, source_target_pairs={{0,4},{4,8},{8,12},{12,16},{16,20},{20,24},{24,28},{1,5},{5,9},{9,... | collective-permute-start | bytes 122888 | tf_op jit(solution)/shard_map/ppermute | solution.py:19
  123.0 6.2 %collective-permute-start.5 = (bf16[16,1280]{1,0:T(8,128)(2,1)S(1)}, bf16[16,1280]{1,0:T(8,128)(2,1)S(1)}, u32[]{:S(2)}, u32[]{:S(2)}) collective-permute-start(bf16[16,1280]{1,0:T(8,128)(2,1)S(1)} %concatenate.13), channel_id=1, source_target_pairs={{4,0},{8,4},{12,8},{16,12},{20,16},{24,20},{28,24},{5,1},{9,5},{13... | collective-permute-start | bytes 122888 | tf_op jit(solution)/shard_map/ppermute | solution.py:19
  125.7 3.5 %copy-start.11 = (bf16[16,1280]{1,0:T(8,128)(2,1)}, bf16[16,1280]{1,0:T(8,128)(2,1)S(1)}, u32[]{:S(2)}) copy-start(bf16[16,1280]{1,0:T(8,128)(2,1)S(1)} %collective-permute-done.4.before_ref) | copy-start | bytes 122884
  129.2 0.6 copy-start.12

commit v3 on v2

--- a/solution.py
+++ b/solution.py
@@ -8,6 +8,8 @@
 TL = 128
 AR_DEV = 1024
 GROUP = 8
+SHIFT_BIT = 16
+WEIGHT_BIT = 23
 VMEM_BYTES = 60 * 1024 * 1024
 WHOLE = pl.BlockSpec(memory_space=pltpu.VMEM)
 SCALARS = pl.BlockSpec(memory_space=pltpu.SMEM)
@@ -26,10 +28,6 @@
     ]
     stacked = jnp.stack(rows, axis=1 if channel_major else 0)
     return stacked.reshape(-1, stacked.shape[-1])
-
-
-def turn(cells, amount):
-    return pltpu.roll(cells, lax.rem(amount, TL), 1)
 
 
 def lanes_of(shape):
@@ -49,10 +47,7 @@
 
 def send_kernel(
     place_ref,
-    block_ref,
-    shift_ref,
-    weight_ref,
-    count_ref,
+    slot_ref,
     image_ref,
     above_ref,
     below_ref,
@@ -122,58 +117,53 @@
                         r, :, half * TL : (half + 1) * TL
                     ]
 
-    peers, capacity = block_ref.shape
+    peers, capacity = slot_ref.shape
     half = capacity // 2
     side = lanes_of((half, TL)) < TL // 2
     slot_row = lax.broadcasted_iota(jnp.int32, (half, TL), 0)
 
     @pl.loop(0, peers)
     def _(d):
-        count = count_ref[0, d]
-        factors = []
+        record = jnp.zeros((half, TL), jnp.float32)
         for k in range(capacity):
-            scale = jnp.where(k < count, weight_ref[d, k].astype(jnp.float32) * 0.0625, 0.0)
-            factors.append(scale)
-            cells = feature_ref[block_ref[d, k]].astype(jnp.float32)
-            cells = pltpu.roll(cells, shift_ref[d, k], 1) * scale
+            slot = slot_ref[d, k]
+            scale = lax.shift_right_logical(slot, WEIGHT_BIT).astype(jnp.float32) * 0.0625
+            cells = feature_ref[slot & ((1 << SHIFT_BIT) - 1)]
+            shift = lax.shift_right_logical(slot, SHIFT_BIT) & (TL - 1)
+            cells = pltpu.roll(cells, shift, 1).astype(jnp.float32) * scale
             slots_ref[pl.ds(k, channels, stride=capacity), :] = cells
+            here = (slot_row == k % half) & (side == (k < half))
+            record = jnp.where(here, scale, record)
         payload_ref[d, : channels * capacity, :] = slots_ref[...].astype(jnp.bfloat16)
-        record = jnp.zeros((half, TL), jnp.float32)
-        for k in range(half):
-            record = jnp.where(
-                slot_row == k, jnp.where(side, factors[k], factors[k + half]), record
-            )
         payload_ref[d, channels * capacity :, :] = record.astype(jnp.bfloat16)
 
 
-def join_kernel(
-    tile_ref, incoming_ref, joined_ref, first_ref, last_ref, onehot_ref, inverse_ref, cells_ref
-):
+def scales_of(incoming_ref, entries):
+    peers, message, lanes = incoming_ref.shape
+    capacity = entries // peers
+    half = capacity // 2
+    record = incoming_ref[:, message - half :, :].astype(jnp.float32).reshape(peers * half, lanes)
+    other = pltpu.roll(record, lanes // 2, 1)
+    side = lanes_of(record.shape) < lanes // 2
+    low = jnp.where(side, record, other).reshape(peers, half, lanes)
+    high = jnp.where(side, other, record).reshape(peers, half, lanes)
+    return jnp.concatenate([low, high], axis=1).reshape(entries, lanes).astype(jnp.bfloat16)
+
+
+def join_kernel(tile_ref, incoming_ref, joined_ref, edge_ref, cells_ref, scales_ref):
     peers = incoming_ref.shape[0]
     entries = tile_ref.shape[1]
     capacity = entries // peers
-    half = capacity // 2
-    tiles = onehot_ref.shape[0]
-    channels = joined_ref.shape[0] // tiles
-    rows = 128
-
-    @pl.loop(0, tiles // rows)
-    def _(i):
-        base = pl.multiple_of(i * rows, rows)
-        ids = lax.broadcasted_iota(jnp.int32, (rows, entries), 0) + base
-        onehot_ref[pl.ds(base, rows), :] = jnp.where(ids == tile_ref[...], 1.0, 0.0).astype(
-            jnp.bfloat16
-        )
-
-    record = incoming_ref[:, channels * capacity :, :].astype(jnp.float32)
-    record = record.reshape(peers * half, TL)
-    other = pltpu.roll(record, TL // 2, 1)
-    side = lanes_of(record.shape) < TL // 2
-    low = jnp.where(side, record, other).reshape(peers, half, TL)
-    high = jnp.where(side, other, record).reshape(peers, half, TL)
-    scales = jnp.concatenate([low, high], axis=1).reshape(entries, TL).astype(jnp.bfloat16)
-    total = jnp.dot(onehot_ref[...], scales, preferred_element_type=jnp.float32)
-    inverse_ref[...] = 1.0 / jnp.maximum(total, 1.0)
+    channels = edge_ref.shape[0]
+
+    @pl.when(pl.program_id(0) == 0)
+    def _():
+        scales_ref[...] = scales_of(incoming_ref, entries)
+
+    ids = lax.broadcasted_iota(jnp.int32, (TL, entries), 0) + pl.program_id(0) * TL
+    onehot = jnp.where(ids == tile_ref[...], 1.0, 0.0).astype(jnp.bfloat16)
+    total = jnp.dot(onehot, scales_ref[...], preferred_element_type=jnp.float32)
+    inverse = 1.0 / jnp.maximum(total, 1.0)
     for q in range(0, channels, 2):
         pair = jnp.concatenate(
             [
@@ -182,32 +172,46 @@
             ],
             axis=1,
         )
-        total = jnp.dot(onehot_ref[...], pair, preferred_element_type=jnp.float32)
+        total = jnp.dot(onehot, pair, preferred_element_type=jnp.float32)
         for p in range(2):
-            cells_ref[pl.ds(q + p, tiles, stride=channels), :] = (
-                total[:, p * TL : (p + 1) * TL] * inverse_ref[...]
+            cells_ref[pl.ds(q + p, TL, stride=channels), :] = (
+                total[:, p * TL : (p + 1) * TL] * inverse
             )
     lanes = lanes_of((channels, TL))
-    unroll = 8
-
-    @pl.loop(0, tiles // TL)
-    def _(i):
-        def one(s, carry):
-            left, right = carry
-            for u in range(unroll):
-                t = s * unroll + u
-                base = pl.multiple_of((i * TL + t) * channels, channels)
-                cells = cells_ref[pl.ds(base, channels), :].astype(jnp.bfloat16)
-                joined_ref[pl.ds(base, channels), :] = cells
-                left = jnp.where(lanes == t, turn(cells, t), left)
-                right = jnp.where(lanes == t, turn(cells, t + 1), right)
-            return left, right
-
-        zero = jnp.zeros((channels, TL), jnp.bfloat16)
-        left, right = lax.fori_loop(0, TL // unroll, one, (zero, zero))
-        cols = pl.ds(pl.multiple_of(i * TL, TL), TL)
-        first_ref[:, cols] = left
-        last_ref[:, cols] = right
+    for part in range(2):
+        edge = jnp.zeros((channels, TL), jnp.bfloat16)
+        for u in range(TL // 2):
+            base = (part * (TL // 2) + u) * channels
+            cells = cells_ref[base : base + channels, :].astype(jnp.bfloat16)
+            joined_ref[base : base + channels, :] = cells
+            edge = jnp.where(lanes // 2 == u, pltpu.roll(cells, 2 * u + 1, 1), edge)
+        edge_ref[:, part * TL : (part + 1) * TL] = edge
+
+
+def join_call(tiles, incoming, channels):
+    half = jnp.bfloat16
+    entries = tiles.shape[1]
+    return pl.pallas_call(
+        join_kernel,
+        grid=(AR_DEV // TL,),
+        out_shape=(
+            jax.ShapeDtypeStruct((AR_DEV * channels, TL), half),
+            jax.ShapeDtypeStruct((channels, 2 * AR_DEV), half),
+        ),
+        in_specs=[
+            pl.BlockSpec(tiles.shape, lambda i: (0, 0)),
+            pl.BlockSpec(incoming.shape, lambda i: (0, 0, 0)),
+        ],
+        out_specs=(
+            pl.BlockSpec((TL * channels, TL), lambda i: (i, 0)),
+            pl.BlockSpec((channels, 2 * TL), lambda i: (0, i)),
+        ),
+        scratch_shapes=[
+            pltpu.VMEM((TL * channels, TL), jnp.float32),
+            pltpu.VMEM((entries, TL), half),
+        ],
+        compiler_params=pltpu.CompilerParams(vmem_limit_bytes=VMEM_BYTES),
+    )(tiles, incoming)
 
 
 def texture_kernel(
@@ -222,28 +226,53 @@
     lanes = lanes_of((channels, TL))
     tiles = blocks * TL
 
-    def place(taps_ref, row, cells, before, after):
+    def place(taps_ref, row, cells, edge):
         base = row * tap
-        taps_ref[base : base + channels, :] = jnp.where(lanes == 0, before, pltpu.roll(cells, 1, 1))
+        taps_ref[base : base + channels, :] = jnp.where(lanes == 0, edge, pltpu.roll(cells, 1, 1))
         taps_ref[base + channels : base + 2 * channels, :] = cells
         taps_ref[base + 2 * channels : base + 3 * channels, :] = jnp.where(
-            lanes == TL - 1, after, pltpu.roll(cells, TL - 1, 1)
+            lanes == TL - 1, edge, pltpu.roll(cells, TL - 1, 1)
+        )
+
+    odd = lanes % 2 == 1
+
+    def edges(before, after, before_lane, after_lane):
+        return jnp.where(
+            lanes == TL - 1,
+            pltpu.roll(after, TL - 1 - after_lane, 1),
+            pltpu.roll(before, TL - before_lane, 1),
         )
 
     def fill(taps_ref):
         i = jnp.minimum(step, blocks - 1)
-        here = pl.ds(pl.multiple_of(i * TL, TL), TL)
-        first = pl.ds(pl.multiple_of(jnp.where(i == 0, tiles, (i - 1) * TL), TL), TL)
-        last = pl.ds(pl.multiple_of(jnp.where(i == blocks - 1, tiles + TL, (i + 1) * TL), TL), TL)
-        cells = jnp.where(i == 0, above_ref[...], prev_ref[...])
-        place(taps_ref, 0, cells, pltpu.roll(before_ref[:, first], 1, 1), after_ref[:, first])
-        cells = jnp.where(i == blocks - 1, below_ref[...], next_ref[...])
-        place(taps_ref, TL + 1, cells, before_ref[:, last], pltpu.roll(after_ref[:, last], TL - 1, 1))
-        before = before_ref[:, here]
-        after = after_ref[:, here]
-        for t in range(TL):
-            cells = joined_ref[t * channels : (t + 1) * channels, :]
-            place(taps_ref, t + 1, cells, pltpu.roll(before, (TL - t) % TL, 1), pltpu.roll(after, TL - 1 - t, 1))
+
+        def both(part):
+            cols = pl.ds(pl.multiple_of(part * TL, TL), TL)
+            return before_ref[:, cols], after_ref[:, cols]
+
+        outer = edges(*both(2 * blocks), TL - 1, 0)
+        inner = edges(*both(jnp.maximum(2 * i - 1, 0)), TL - 2, TL - 1)
+        place(
+            taps_ref,
+            0,
+            jnp.where(i == 0, above_ref[...], prev_ref[...]),
+            jnp.where(i == 0, outer, inner),
+        )
+        outer = edges(*both(2 * blocks + 1), TL - 1, 0)
+        inner = edges(*both(jnp.minimum(2 * i + 2, 2 * blocks - 1)), 0, 1)
+        place(
+            taps_ref,
+            TL + 1,
+            jnp.where(i == blocks - 1, below_ref[...], next_ref[...]),
+            jnp.where(i == blocks - 1, outer, inner),
+        )
+        for part in range(2):
+            before, after = both(2 * i + part)
+            merged = jnp.where(odd, after, pltpu.roll(before, 2, 1))
+            for u in range(TL // 2):
+                t = part * (TL // 2) + u
+                cells = joined_ref[t * channels : (t + 1) * channels, :]
+                place(taps_ref, t + 1, cells, pltpu.roll(merged, TL - 2 - 2 * u, 1))
 
     def convolve(taps_ref):
         pair = 2 * GROUP
@@ -336,6 +365,12 @@
     peers, capacity = send_block.shape[2:]
     entries = peers * capacity
     message = channels * capacity + capacity // 2
+    used = lax.broadcasted_iota(jnp.int32, (peers, capacity), 1) < send_count.reshape(peers, 1)
+    slots = (
+        send_block[0, 0]
+        + (send_shift[0, 0] << SHIFT_BIT)
+        + (jnp.where(used, send_weight[0, 0], 0) << WEIGHT_BIT)
+    )
     payload = call(
         send_kernel,
         jax.ShapeDtypeStruct((peers, message, TL), half),
@@ -345,38 +380,15 @@
             pltpu.VMEM((strip_rows * width // TL, channels, TL), half),
             pltpu.VMEM((channels * capacity, TL), jnp.float32),
         ],
-        [SCALARS] * 5 + [WHOLE] * 5,
-    )(
-        place,
-        send_block[0, 0],
-        send_shift[0, 0],
-        send_weight[0, 0],
-        send_count[0],
-        by_row,
-        above,
-        below,
-        band(conv_first, False),
-        band(conv_second, False),
-    )
+        [SCALARS] * 2 + [WHOLE] * 5,
+    )(place, slots, by_row, above, below, band(conv_first, False), band(conv_second, False))
     arrived = lax.all_to_all(payload, ("cam", "row"), split_axis=0, concat_axis=0, tiled=True)
-    joined, first, last = call(
-        join_kernel,
-        (
-            jax.ShapeDtypeStruct((AR_DEV * channels, TL), half),
-            jax.ShapeDtypeStruct((channels, AR_DEV), half),
-            jax.ShapeDtypeStruct((channels, AR_DEV), half),
-        ),
-        [
-            pltpu.VMEM((AR_DEV, entries), half),
-            pltpu.VMEM((AR_DEV, TL), jnp.float32),
-            pltpu.VMEM((AR_DEV * channels, TL), jnp.float32),
-        ],
-        [WHOLE] * 2,
-    )(recv_tile.reshape(1, entries), arrived)
+    joined, edge = join_call(recv_tile.reshape(1, entries), arrived, channels)
     top = neighbour(joined[-channels:], "row", 1)
     bottom = neighbour(joined[:channels], "row", -1)
-    before = neighbour(jnp.concatenate([last, top, jnp.roll(bottom, 1, 1)], axis=1), "cam", 1)
-    after = neighbour(jnp.concatenate([first, jnp.roll(top, -1, 1), bottom], axis=1), "cam", -1)
+    rim = jnp.concatenate([edge, top, bottom], axis=1)
+    before = neighbour(rim, "cam", 1)
+    after = neighbour(rim, "cam", -1)
     same = (
         lax.broadcasted_iota(jnp.int32, (channels, GROUP, GROUP, channels), 0)
         == lax.broadcasted_iota(jnp.int32, (channels, GROUP, GROUP, channels), 3)

time: 141 us -> 128 us (0.908)
  the two profiles are of different devices: /device:TPU:11 before, /device:TPU:4 now
where the time goes in v3:
time: 128 us
  waiting for transfers between devices  53.3 us (42%)
  Pallas kernels  38.6 us (30%)
  starting transfers between devices  22.6 us (18%)
  local copies, waits for them, and re-layouts  10.8 us (8%)
  other arithmetic  2.05 us (2%)
    all_to_all x1, waiting for transfers between devices, local(): lax.all_to_all(payload, ('cam', 'row'), split_axis=0, concat_axis=0, tile...  45.8 us
    pallas_call x1, Pallas kernels, local(): call(send_kernel, jax.ShapeDtypeStruct((peers, message, TL), half), [pltp...  19.6 us
    ppermute x6, starting transfers between devices, neighbour(): return lax.ppermute(cells, axis, pairs)  15.9 us
    pallas_call x1, Pallas kernels, texture_call(): pl.pallas_call(texture_kernel, grid=(blocks + 1,), out_shape=jax.ShapeDty...  9.81 us
    pallas_call x1, Pallas kernels, join_call(): pl.pallas_call(join_kernel, grid=(AR_DEV // TL,), out_shape=(jax.ShapeDty...  9.14 us
    unnamed x64, local copies, waits for them, and re-layouts  8.08 us
    ppermute x6, waiting for transfers between devices, neighbour(): return lax.ppermute(cells, axis, pairs)  7.52 us
    all_to_all x1, starting transfers between devices, local(): lax.all_to_all(payload, ('cam', 'row'), split_axis=0, concat_axis=0, tile...  6.68 us
  transfers between devices with their start and end apart: 7, of which 3 were waited for; matrix products, arithmetic and copies ran while one was open for 5% of the time, Pallas kernels for 0%

profile of v3, /device:TPU:4, one launch (start us, length us, event | category | flops | bytes accessed | tf_op | source)
XLA Modules:
  0.0 127.5 jit_solution(14570143686092842418)
XLA Ops:
  0.0 2.8 %copy.31 = bf16[1,16,32,2048]{3,1,2,0:T(8,128)(2,1)S(1)} copy(bf16[1,16,32,2048]{3,2,1,0:T(8,128)(2,1)} %param.9) | data formatting | bytes 4194304 | tf_op args[0]
  2.9 1.3 %collective-permute-start.1 = (bf16[2,16,2048]{2,1,0:T(8,128)(2,1)S(1)}, bf16[2,16,2048]{2,1,0:T(8,128)(2,1)S(1)}, u32[]{:S(2)}, u32[]{:S(2)}) collective-permute-start(bf16[2,16,2048]{2,1,0:T(8,128)(2,1)S(1)} %get-tuple-element.11), channel_id=1, source_target_pairs={{1,0},{2,1},{3,2},{5,4},{6,5},{7,6},{9,8},{10,9},{11,10},{13,12},{... | collective-permute-start | bytes 393224 | tf_op jit(solution)/shard_map/ppermute | solution.py:21
  4.2 4.6 %collective-permute-start = (bf16[2,16,2048]{2,1,0:T(8,128)(2,1)S(1)}, bf16[2,16,2048]{2,1,0:T(8,128)(2,1)S(1)}, u32[]{:S(2)}, u32[]{:S(2)}) collective-permute-start(bf16[2,16,2048]{2,1,0:T(8,128)(2,1)S(1)} %get-tuple-element.12), channel_id=1, source_target_pairs={{0,1},{1,2},{2,3},{4,5},{5,6},{6,7},{8,9},{9,10},{10,11},{12,13},{... | collective-permute-start | bytes 393224 | tf_op jit(solution)/shard_map/ppermute | solution.py:21
  10.0 0.7 fusion.1.slot_ref
  10.7 0.7 pad_add_fusion.place_ref
  11.5 0.6 copy-done.6
  12.2 19.6 %shard_map.91 = bf16[32,264,128]{2,1,0:T(8,128)(2,1)} custom-call(s32[2]{0:T(128)} %pad_add_fusion.place_ref, s32[32,16]{1,0:T(8,128)} %fusion.1.slot_ref, bf16[32,16,2048]{2,1,0:T(8,128)(2,1)} %bitcast.71, bf16[2,16,2048]{2,1,0:T(8,128)(2,1)} %copy-done.8, bf16[2,16,2048]{2,1,0:T(8,128)(2,1)} %copy-done.7, bf16[128,480]{1,0:T(8,128)(2,1)} %bitcast.73, ...), custom_call_target="tpu_custom_call" | custom-call | tf_op jit(solution)/shard_map/pallas_call | solution.py:374
  31.8 6.7 %all-to-all-start = ((bf16[32,264,128]{2,1,0:T(8,128)(2,1)}), bf16[32,264,128]{2,1,0:T(8,128)(2,1)S(1)}, u32[]{:S(2)}, u32[]{:S(2)}) async-start(bf16[32,264,128]{2,1,0:T(8,128)(2,1)} %shard_map.91), calls=%async_computation | async-start | bytes 4325376 | tf_op jit(solution)/shard_map/all_to_all | solution.py:385
  38.9 0.7 reshape.22.tile_ref
  40.1 0.7 and_convert_fusion.residual_ref
  40.8 45.8 %all-to-all-done.incoming_ref = bf16[32,264,128]{2,1,0:T(8,128)(2,1)S(1)} async-done(((bf16[32,264,128]{2,1,0:T(8,128)(2,1)}), bf16[32,264,128]{2,1,0:T(8,128)(2,1)S(1)}, u32[]{:S(2)}, u32[]{:S(2)}) %all-to-all-start) | async-done | bytes 2162720 | tf_op jit(solution)/shard_map/all_to_all | solution.py:385
  86.6 1.3 %copy-done.1 = bf16[32,264,128]{2,1,0:T(8,128)(2,1)} copy-done((bf16[32,264,128]{2,1,0:T(8,128)(2,1)}, bf16[32,264,128]{2,1,0:T(8,128)(2,1)S(1)}, u32[]{:S(2)}) %copy-start.1) | copy-done | bytes 2162712
  88.0 9.1 %shard_map.92 = (bf16[16384,128]{1,0:T(8,128)(2,1)}, bf16[16,2048]{1,0:T(8,128)(2,1)}) custom-call(s32[1,512]{1,0:T(1,128)} %reshape.22.tile_ref, bf16[32,264,128]{2,1,0:T(8,128)(2,1)} %copy-done.1), custom_call_target="tpu_custom_call" | custom-call | tf_op jit(solution)/shard_map/pallas_call | solution.py:194
  97.1 0.7 fusion.2
  97.8 4.4 %collective-permute-start.2 = (bf16[16,128]{1,0:T(8,128)(2,1)S(1)}, bf16[16,128]{1,0:T(8,128)(2,1)S(1)}, u32[]{:S(2)}, u32[]{:S(2)}) collective-permute-start(bf16[16,128]{1,0:T(8,128)(2,1)S(1)} %get-tuple-element.10), channel_id=1, source_target_pairs={{0,1},{1,2},{2,3},{4,5},{5,6},{6,7},{8,9},{9,10},{10,11},{12,13},{... | collective-permute-start | bytes 12296 | tf_op jit(solution)/shard_map/ppermute | solution.py:21
  102.2 0.8 constant_dynamic-update-slice_fusion.18
  103.1 1.3 %collective-permute-start.3 = (bf16[16,128]{1,0:T(8,128)(2,1)S(1)}, bf16[16,128]{1,0:T(8,128)(2,1)S(1)}, u32[]{:S(2)}, u32[]{:S(2)}) collective-permute-start(bf16[16,128]{1,0:T(8,128)(2,1)S(1)} %get-tuple-element.9), channel_id=1, source_target_pairs={{1,0},{2,1},{3,2},{5,4},{6,5},{7,6},{9,8},{10,9},{11,10},{13,12},{... | collective-permute-start | bytes 12296 | tf_op jit(solution)/shard_map/ppermute | solution.py:21
  104.4 4.2 %collective-permute-done.3.below_ref = bf16[16,128]{1,0:T(8,128)(2,1)S(1)} collective-permute-done((bf16[16,128]{1,0:T(8,128)(2,1)S(1)}, bf16[16,128]{1,0:T(8,128)(2,1)S(1)}, u32[]{:S(2)}, u32[]{:S(2)}) %collective-permute-start.3) | collective-permute-done | bytes 4128 | tf_op jit(solution)/shard_map/ppermute | solution.py:21
  108.6 1.9 %collective-permute-start.5 = (bf16[16,2304]{1,0:T(8,128)(2,1)S(1)}, bf16[16,2304]{1,0:T(8,128)(2,1)S(1)}, u32[]{:S(2)}, u32[]{:S(2)}) collective-permute-start(bf16[16,2304]{1,0:T(8,128)(2,1)S(1)} %constant_dynamic-update-slice_fusion.16), channel_id=1, source_target_pairs={{4,0},{8,4},{12,8},{16,12},{20,16},{24,20},{28,24},{5,1},{9,5},{13... | collective-permute-start | bytes 221192 | tf_op jit(solution)/shard_map/ppermute | solution.py:21
  110.5 2.4 %collective-permute-start.4 = (bf16[16,2304]{1,0:T(8,128)(2,1)S(1)}, bf16[16,2304]{1,0:T(8,128)(2,1)S(1)}, u32[]{:S(2)}, u32[]{:S(2)}) collective-permute-start(bf16[16,2304]{1,0:T(8,128)(2,1)S(1)} %constant_dynamic-update-slice_fusion.16), channel_id=1, source_target_pairs={{0,4},{4,8},{8,12},{12,16},{16,20},{20,24},{24,28},{1,5},{5,9},{9,... | collective-permute-start | bytes 221192 | tf_op jit(solution)/shard_map/ppermute | solution.py:21
  113.0 0.7 copy.32
  113.7 3.3 %collective-permute-done.4.before_ref = bf16[16,2304]{1,0:T(8,128)(2,1)S(1)} collective-permute-done((bf16[16,2304]{1,0:T(8,128)(2,1)S(1)}, bf16[16,2304]{1,0:T(8,128)(2,1)S(1)}, u32[]{:S(2)}, u32[]{:S(2)}) %collective-permute-start.4) | collective-permute-done | bytes 73760 | tf_op jit(solution)/shard_map/ppermute | solution.py:21
  117.1 0.6 copy-done.10
  117.7 9.8 %shard_map.93 = bf16[16,1024,128]{2,1,0:T(8,128)(2,1)} custom-call(bf16[16384,128]{1,0:T(8,128)(2,1)} %get-tuple-element.7.joined_ref.prev_ref.next_ref, bf16[16384,128]{1,0:T(8,128)(2,1)} %get-tuple-element.7.joined_ref.prev_ref.next_ref, bf16[16384,128]{1,0:T(8,128)(2,1)} %get-tuple-element.7.joined_ref.prev_ref.next_ref, bf16[16,128]{1,0:T(8,128)(2,1)} %copy-done.11, ...), custom_call_target="tpu_custom_call" | custom-call | tf_op jit(solution)/shard_map/pallas_call | solution.py:321
  (76 shorter events, 2.5 us)
Async XLA Ops:
  0.0 8.7 %copy-start.13 = (s32[1,1,32,16]{2,3,1,0:T(8,128)S(1)}, s32[1,1,32,16]{2,3,1,0:T(8,128)}, u32[]{:S(2)}) copy-start(s32[1,1,32,16]{2,3,1,0:T(8,128)} %param.13) | copy-start | bytes 6148
  0.0 8.8 %copy-start.14 = (s32[1,1,32,16]{2,3,1,0:T(8,128)S(1)}, s32[1,1,32,16]{2,3,1,0:T(8,128)}, u32[]{:S(2)}) copy-start(s32[1,1,32,16]{2,3,1,0:T(8,128)} %param.14) | copy-start | bytes 6148
  0.0 8.9 %copy-start.15 = (s32[1,1,32,16]{2,3,1,0:T(8,128)S(1)}, s32[1,1,32,16]{2,3,1,0:T(8,128)}, u32[]{:S(2)}) copy-start(s32[1,1,32,16]{2,3,1,0:T(8,128)} %param.15) | copy-start | bytes 6148
  0.0 9.0 %copy-start.2 = (bf16[16,144]{1,0:T(8,128)(2,1)S(1)}, bf16[16,144]{1,0:T(8,128)(2,1)}, u32[]{:S(2)}) copy-start(bf16[16,144]{1,0:T(8,128)(2,1)} %param.10) | copy-start | bytes 13828
  0.0 9.5 %copy-start.3 = (bf16[16,144]{1,0:T(8,128)(2,1)S(1)}, bf16[16,144]{1,0:T(8,128)(2,1)}, u32[]{:S(2)}) copy-start(bf16[16,144]{1,0:T(8,128)(2,1)} %param.11) | copy-start | bytes 13828
  0.0 10.0 %copy-start.17 = (s32[1,1,32]{2,1,0:T(1,128)S(1)}, s32[1,1,32]{2,1,0:T(1,128)}, u32[]{:S(2)}) copy-start(s32[1,1,32]{2,1,0:T(1,128)} %param.16) | copy-start | bytes 388
  2.8 8.6 %copy-start = (bf16[1,16,32,2048]{3,1,2,0:T(8,128)(2,1)}, bf16[1,16,32,2048]{3,1,2,0:T(8,128)(2,1)S(1)}, u32[]{:S(2)}) copy-start(bf16[1,16,32,2048]{3,1,2,0:T(8,128)(2,1)S(1)} %copy.31) | copy-start | bytes 6291460
  2.9 8.6 %collective-permute-start.1 = (bf16[2,16,2048]{2,1,0:T(8,128)(2,1)S(1)}, bf16[2,16,2048]{2,1,0:T(8,128)(2,1)S(1)}, u32[]{:S(2)}, u32[]{:S(2)}) collective-permute-start(bf16[2,16,2048]{2,1,0:T(8,128)(2,1)S(1)} %get-tuple-element.11), channel_id=1, source_target_pairs={{1,0},{2,1},{3,2},{5,4},{6,5},{7,6},{9,8},{10,9},{11,10},{13,12},{... | collective-permute-start | bytes 393224 | tf_op jit(solution)/shard_map/ppermute | solution.py:21
  4.2 7.3 %collective-permute-start = (bf16[2,16,2048]{2,1,0:T(8,128)(2,1)S(1)}, bf16[2,16,2048]{2,1,0:T(8,128)(2,1)S(1)}, u32[]{:S(2)}, u32[]{:S(2)}) collective-permute-start(bf16[2,16,2048]{2,1,0:T(8,128)(2,1)S(1)} %get-tuple-element.12), channel_id=1, source_target_pairs={{0,1},{1,2},{2,3},{4,5},{5,6},{6,7},{8,9},{9,10},{10,11},{12,13},{... | collective-permute-start | bytes 393224 | tf_op jit(solution)/shard_map/ppermute | solution.py:21
  9.5 1.9 %copy-start.5 = (bf16[8,16,480]{2,1,0:T(8,128)(2,1)}, bf16[8,16,480]{2,1,0:T(8,128)(2,1)S(1)}, u32[]{:S(2)}) copy-start(bf16[8,16,480]{2,1,0:T(8,128)(2,1)S(1)} %constant_dynamic-update-slice_fusion) | copy-start | bytes 368644
  11.4 0.7 copy-start.6
  11.4 0.7 copy-start.7
  11.5 0.7 copy-start.8
  31.8 7.1 %copy-start.16 = (s32[1,1,32,16]{2,3,1,0:T(8,128)S(1)}, s32[1,1,32,16]{2,3,1,0:T(8,128)}, u32[]{:S(2)}) copy-start(s32[1,1,32,16]{2,3,1,0:T(8,128)} %param.17) | copy-start | bytes 6148
  31.8 7.8 %copy-start.4 = (bf16[16,144]{1,0:T(8,128)(2,1)S(1)}, bf16[16,144]{1,0:T(8,128)(2,1)}, u32[]{:S(2)}) copy-start(bf16[16,144]{1,0:T(8,128)(2,1)} %param.12) | copy-start | bytes 13828
  31.8 54.8 %all-to-all-start = ((bf16[32,264,128]{2,1,0:T(8,128)(2,1)}), bf16[32,264,128]{2,1,0:T(8,128)(2,1)S(1)}, u32[]{:S(2)}, u32[]{:S(2)}) async-start(bf16[32,264,128]{2,1,0:T(8,128)(2,1)} %shard_map.91), calls=%async_computation | async-start | bytes 4325376 | tf_op jit(solution)/shard_map/all_to_all | solution.py:385
  86.6 1.3 %copy-start.1 = (bf16[32,264,128]{2,1,0:T(8,128)(2,1)}, bf16[32,264,128]{2,1,0:T(8,128)(2,1)S(1)}, u32[]{:S(2)}) copy-start(bf16[32,264,128]{2,1,0:T(8,128)(2,1)S(1)} %all-to-all-done.incoming_ref) | copy-start | bytes 6488068
  97.8 6.6 %collective-permute-start.2 = (bf16[16,128]{1,0:T(8,128)(2,1)S(1)}, bf16[16,128]{1,0:T(8,128)(2,1)S(1)}, u32[]{:S(2)}, u32[]{:S(2)}) collective-permute-start(bf16[16,128]{1,0:T(8,128)(2,1)S(1)} %get-tuple-element.10), channel_id=1, source_target_pairs={{0,1},{1,2},{2,3},{4,5},{5,6},{6,7},{8,9},{9,10},{10,11},{12,13},{... | collective-permute-start | bytes 12296 | tf_op jit(solution)/shard_map/ppermute | solution.py:21
  103.1 5.5 %collective-permute-start.3 = (bf16[16,128]{1,0:T(8,128)(2,1)S(1)}, bf16[16,128]{1,0:T(8,128)(2,1)S(1)}, u32[]{:S(2)}, u32[]{:S(2)}) collective-permute-start(bf16[16,128]{1,0:T(8,128)(2,1)S(1)} %get-tuple-element.9), channel_id=1, source_target_pairs={{1,0},{2,1},{3,2},{5,4},{6,5},{7,6},{9,8},{10,9},{11,10},{13,12},{... | collective-permute-start | bytes 12296 | tf_op jit(solution)/shard_map/ppermute | solution.py:21
  104.4 12.7 %copy-start.11 = (bf16[16,128]{1,0:T(8,128)(2,1)}, bf16[16,128]{1,0:T(8,128)(2,1)S(1)}, u32[]{:S(2)}) copy-start(bf16[16,128]{1,0:T(8,128)(2,1)S(1)} %collective-permute-done.2.above_ref) | copy-start | bytes 12292
  108.6 8.5 %copy-start.12 = (bf16[16,128]{1,0:T(8,128)(2,1)}, bf16[16,128]{1,0:T(8,128)(2,1)S(1)}, u32[]{:S(2)}) copy-start(bf16[16,128]{1,0:T(8,128)(2,1)S(1)} %collective-permute-done.3.below_ref) | copy-start | bytes 12292
  108.6 5.1 %collective-permute-start.5 = (bf16[16,2304]{1,0:T(8,128)(2,1)S(1)}, bf16[16,2304]{1,0:T(8,128)(2,1)S(1)}, u32[]{:S(2)}, u32[]{:S(2)}) collective-permute-start(bf16[16,2304]{1,0:T(8,128)(2,1)S(1)} %constant_dynamic-update-slice_fusion.16), channel_id=1, source_target_pairs={{4,0},{8,4},{12,8},{16,12},{20,16},{24,20},{28,24},{5,1},{9,5},{13... | collective-permute-start | bytes 221192 | tf_op jit(solution)/shard_map/ppermute | solution.py:21
  110.5 6.6 %collective-permute-start.4 = (bf16[16,2304]{1,0:T(8,128)(2,1)S(1)}, bf16[16,2304]{1,0:T(8,128)(2,1)S(1)}, u32[]{:S(2)}, u32[]{:S(2)}) collective-permute-start(bf16[16,2304]{1,0:T(8,128)(2,1)S(1)} %constant_dynamic-update-slice_fusion.16), channel_id=1, source_target_pairs={{0,4},{4,8},{8,12},{12,16},{16,20},{20,24},{24,28},{1,5},{5,9},{9,... | collective-permute-start | bytes 221192 | tf_op jit(solution)/shard_map/ppermute | solution.py:21
  113.7 3.4 %copy-start.9 = (bf16[16,2304]{1,0:T(8,128)(2,1)}, bf16[16,2304]{1,0:T(8,128)(2,1)S(1)}, u32[]{:S(2)}) copy-start(bf16[16,2304]{1,0:T(8,128)(2,1)S(1)} %collective-permute-done.5.after_ref) | copy-start | bytes 221188
  (1 other events, 0.6 us)

commit v4 on v3

--- a/solution.py
+++ b/solution.py
@@ -10,15 +10,22 @@
 GROUP = 8
 SHIFT_BIT = 16
 WEIGHT_BIT = 23
-VMEM_BYTES = 60 * 1024 * 1024
+VMEM_BYTES = 32 * 1024 * 1024
 WHOLE = pl.BlockSpec(memory_space=pltpu.VMEM)
 SCALARS = pl.BlockSpec(memory_space=pltpu.SMEM)
 
 
-def neighbour(cells, axis, step):
+def swap(even_pairs, odd_pairs, axis):
     count = lax.axis_size(axis)
-    pairs = [(i, i + step) for i in range(count) if 0 <= i + step < count]
-    return lax.ppermute(cells, axis, pairs)
+    received = []
+    for start, cells in enumerate((even_pairs, odd_pairs)):
+        pairs = [(i, i + 1) for i in range(start, count - 1, 2)]
+        received.append(lax.ppermute(cells, axis, pairs + [(j, i) for i, j in pairs]))
+    return received
+
+
+def ordered(odd, even_pairs, odd_pairs):
+    return jnp.where(odd, even_pairs, odd_pairs), jnp.where(odd, odd_pairs, even_pairs)
 
 
 def band(weight, channel_major):
@@ -49,8 +56,8 @@
     place_ref,
     slot_ref,
     image_ref,
-    above_ref,
-    below_ref,
+    even_ref,
+    odd_ref,
     first_ref,
     second_ref,
     payload_ref,
@@ -63,9 +70,11 @@
     tap = 3 * channels
     reach = (GROUP + 2) * tap
     lanes = lanes_of((channels, width))
+    odd = place_ref[0] % 2 == 1
     for i in range(2):
-        spread(i, lanes, taps_ref, above_ref[i])
-        spread(rows + 2 + i, lanes, taps_ref, below_ref[i])
+        above, below = ordered(odd, even_ref[i], odd_ref[i])
+        spread(i, lanes, taps_ref, above)
+        spread(rows + 2 + i, lanes, taps_ref, below)
 
     @pl.loop(0, rows)
     def _(i):
@@ -150,7 +159,9 @@
     return jnp.concatenate([low, high], axis=1).reshape(entries, lanes).astype(jnp.bfloat16)
 
 
-def join_kernel(tile_ref, incoming_ref, joined_ref, edge_ref, cells_ref, scales_ref):
+def join_kernel(
+    place_ref, tile_ref, incoming_ref, joined_ref, edge_ref, even_ref, odd_ref, cells_ref, scales_ref
+):
     peers = incoming_ref.shape[0]
     entries = tile_ref.shape[1]
     capacity = entries // peers
@@ -187,8 +198,29 @@
             edge = jnp.where(lanes // 2 == u, pltpu.roll(cells, 2 * u + 1, 1), edge)
         edge_ref[:, part * TL : (part + 1) * TL] = edge
 
-
-def join_call(tiles, incoming, channels):
+    step = pl.program_id(0)
+    odd = place_ref[0] % 2
+    head = joined_ref[:channels, :]
+    tail = joined_ref[-channels:, :]
+
+    @pl.when((step == 0) & (odd == 1))
+    def _():
+        even_ref[...] = head
+
+    @pl.when((step == 0) & (odd == 0))
+    def _():
+        odd_ref[...] = head
+
+    @pl.when((step == pl.num_programs(0) - 1) & (odd == 1))
+    def _():
+        odd_ref[...] = tail
+
+    @pl.when((step == pl.num_programs(0) - 1) & (odd == 0))
+    def _():
+        even_ref[...] = tail
+
+
+def join_call(place, tiles, incoming, channels):
     half = jnp.bfloat16
     entries = tiles.shape[1]
     return pl.pallas_call(
@@ -197,26 +229,42 @@
         out_shape=(
             jax.ShapeDtypeStruct((AR_DEV * channels, TL), half),
             jax.ShapeDtypeStruct((channels, 2 * AR_DEV), half),
+            jax.ShapeDtypeStruct((channels, TL), half),
+            jax.ShapeDtypeStruct((channels, TL), half),
         ),
         in_specs=[
+            SCALARS,
             pl.BlockSpec(tiles.shape, lambda i: (0, 0)),
             pl.BlockSpec(incoming.shape, lambda i: (0, 0, 0)),
         ],
         out_specs=(
             pl.BlockSpec((TL * channels, TL), lambda i: (i, 0)),
             pl.BlockSpec((channels, 2 * TL), lambda i: (0, i)),
+            pl.BlockSpec((channels, TL), lambda i: (0, 0)),
+            pl.BlockSpec((channels, TL), lambda i: (0, 0)),
         ),
         scratch_shapes=[
             pltpu.VMEM((TL * channels, TL), jnp.float32),
             pltpu.VMEM((entries, TL), half),
         ],
         compiler_params=pltpu.CompilerParams(vmem_limit_bytes=VMEM_BYTES),
-    )(tiles, incoming)
+    )(place, tiles, incoming)
 
 
 def texture_kernel(
-    joined_ref, prev_ref, next_ref, above_ref, below_ref, before_ref, after_ref, weight_ref, residual_ref,
-    texture_ref, even_ref, odd_ref
+    place_ref,
+    joined_ref,
+    prev_ref,
+    next_ref,
+    even_end_ref,
+    odd_end_ref,
+    even_rim_ref,
+    odd_rim_ref,
+    weight_ref,
+    residual_ref,
+    texture_ref,
+    even_ref,
+    odd_ref,
 ):
     channels = texture_ref.shape[0]
     step = pl.program_id(0)
@@ -245,25 +293,28 @@
 
     def fill(taps_ref):
         i = jnp.minimum(step, blocks - 1)
+        odd_row = place_ref[0] % 2
+        odd_cam = place_ref[2] % 2 == 1
+        above, below = ordered(odd_row == 1, even_end_ref[...], odd_end_ref[...])
 
         def both(part):
             cols = pl.ds(pl.multiple_of(part * TL, TL), TL)
-            return before_ref[:, cols], after_ref[:, cols]
-
-        outer = edges(*both(2 * blocks), TL - 1, 0)
+            return ordered(odd_cam, even_rim_ref[:, cols], odd_rim_ref[:, cols])
+
+        outer = edges(*both(2 * blocks + 1 - odd_row), TL - 1, 0)
         inner = edges(*both(jnp.maximum(2 * i - 1, 0)), TL - 2, TL - 1)
         place(
             taps_ref,
             0,
-            jnp.where(i == 0, above_ref[...], prev_ref[...]),
+            jnp.where(i == 0, above, prev_ref[...]),
             jnp.where(i == 0, outer, inner),
         )
-        outer = edges(*both(2 * blocks + 1), TL - 1, 0)
+        outer = edges(*both(2 * blocks + odd_row), TL - 1, 0)
         inner = edges(*both(jnp.minimum(2 * i + 2, 2 * blocks - 1)), 0, 1)
         place(
             taps_ref,
             TL + 1,
-            jnp.where(i == blocks - 1, below_ref[...], next_ref[...]),
+            jnp.where(i == blocks - 1, below, next_ref[...]),
             jnp.where(i == blocks - 1, outer, inner),
         )
         for part in range(2):
@@ -311,8 +362,8 @@
         convolve(even_ref)
 
 
-def texture_call(joined, above, below, before, after, weight, residual):
-    channels = above.shape[0]
+def texture_call(place, joined, even_end, odd_end, even_rim, odd_rim, weight, residual):
+    channels = even_end.shape[0]
     tiles = joined.shape[0] // channels
     blocks = tiles // TL
     def at(i):
@@ -323,14 +374,15 @@
         grid=(blocks + 1,),
         out_shape=jax.ShapeDtypeStruct((channels, tiles, TL), jnp.bfloat16),
         in_specs=[
+            SCALARS,
             pl.BlockSpec((TL * channels, TL), lambda i: (at(i), 0)),
             pl.BlockSpec((channels, TL), lambda i: (jnp.maximum(at(i) * TL - 1, 0), 0)),
             pl.BlockSpec((channels, TL), lambda i: (jnp.minimum((at(i) + 1) * TL, tiles - 1), 0)),
-        ] + [whole(x) for x in (above, below, before, after, weight, residual)],
+        ] + [whole(x) for x in (even_end, odd_end, even_rim, odd_rim, weight, residual)],
         out_specs=pl.BlockSpec((channels, TL, TL), lambda i: (0, jnp.maximum(i - 1, 0), 0)),
         scratch_shapes=[pltpu.VMEM(((TL + 2) * 3 * channels, TL), jnp.bfloat16)] * 2,
         compiler_params=pltpu.CompilerParams(vmem_limit_bytes=VMEM_BYTES),
-    )(joined, joined, joined, above, below, before, after, weight, residual)
+    )(place, joined, joined, joined, even_end, odd_end, even_rim, odd_rim, weight, residual)
 
 
 def call(kernel, outs, scratch, specs):
@@ -359,9 +411,13 @@
     pixels = image[0]
     channels, strip_rows, width = pixels.shape
     by_row = pixels.transpose(1, 0, 2)
-    above = neighbour(by_row[-2:], "row", 1)
-    below = neighbour(by_row[:2], "row", -1)
-    place = jnp.stack([lax.axis_index("row"), lax.axis_size("row")]).astype(jnp.int32)
+    place = jnp.stack(
+        [lax.axis_index("row"), lax.axis_size("row"), lax.axis_index("cam")]
+    ).astype(jnp.int32)
+    odd = place[0] % 2 == 1
+    near = swap(
+        jnp.where(odd, by_row[:2], by_row[-2:]), jnp.where(odd, by_row[-2:], by_row[:2]), "row"
+    )
     peers, capacity = send_block.shape[2:]
     entries = peers * capacity
     message = channels * capacity + capacity // 2
@@ -381,14 +437,12 @@
             pltpu.VMEM((channels * capacity, TL), jnp.float32),
         ],
         [SCALARS] * 2 + [WHOLE] * 5,
-    )(place, slots, by_row, above, below, band(conv_first, False), band(conv_second, False))
+    )(place, slots, by_row, *near, band(conv_first, False), band(conv_second, False))
     arrived = lax.all_to_all(payload, ("cam", "row"), split_axis=0, concat_axis=0, tiled=True)
-    joined, edge = join_call(recv_tile.reshape(1, entries), arrived, channels)
-    top = neighbour(joined[-channels:], "row", 1)
-    bottom = neighbour(joined[:channels], "row", -1)
-    rim = jnp.concatenate([edge, top, bottom], axis=1)
-    before = neighbour(rim, "cam", 1)
-    after = neighbour(rim, "cam", -1)
+    joined, edge, *ends = join_call(place, recv_tile.reshape(1, entries), arrived, channels)
+    ends = swap(*ends, "row")
+    rim = jnp.concatenate([edge, *ends], axis=1)
+    rims = swap(rim, rim, "cam")
     same = (
         lax.broadcasted_iota(jnp.int32, (channels, GROUP, GROUP, channels), 0)
         == lax.broadcasted_iota(jnp.int32, (channels, GROUP, GROUP, channels), 3)
@@ -397,7 +451,7 @@
         == lax.broadcasted_iota(jnp.int32, (channels, GROUP, GROUP, channels), 2)
     )
     residual = same.astype(half).reshape(channels * GROUP, GROUP * channels)
-    return texture_call(joined, top, bottom, before, after, band(conv_uv, True), residual)
+    return texture_call(place, joined, *ends, *rims, band(conv_uv, True), residual)
 
 
 def solution(mesh):

time: 128 us -> 111 us (0.87)
  the two profiles are of different devices: /device:TPU:4 before, /device:TPU:11 now
where the time goes in v4:
time: 111 us
  waiting for transfers between devices  55.4 us (50%)
  Pallas kernels  32.7 us (29%)
  starting transfers between devices  15.8 us (14%)
  local copies, waits for them, and re-layouts  6.63 us (6%)
    all_to_all x1, waiting for transfers between devices, local(): lax.all_to_all(payload, ('cam', 'row'), split_axis=0, concat_axis=0, tile...  47.5 us
    pallas_call x1, Pallas kernels, local(): call(send_kernel, jax.ShapeDtypeStruct((peers, message, TL), half), [pltp...  17.3 us
    ppermute x6, starting transfers between devices, swap(): lax.ppermute(cells, axis, pairs + [(j, i) for i, j in pairs])  10.4 us
    ppermute x6, waiting for transfers between devices, swap(): lax.ppermute(cells, axis, pairs + [(j, i) for i, j in pairs])  7.89 us
    pallas_call x1, Pallas kernels, texture_call(): pl.pallas_call(texture_kernel, grid=(blocks + 1,), out_shape=jax.ShapeDty...  7.8 us
    pallas_call x1, Pallas kernels, join_call(): pl.pallas_call(join_kernel, grid=(AR_DEV // TL,), out_shape=(jax.ShapeDty...  7.55 us
    unnamed x46, local copies, waits for them, and re-layouts  5.88 us
    all_to_all x1, starting transfers between devices, local(): lax.all_to_all(payload, ('cam', 'row'), split_axis=0, concat_axis=0, tile...  5.41 us
  transfers between devices with their start and end apart: 7, of which 5 were waited for; matrix products, arithmetic and copies ran while one was open for 2% of the time, Pallas kernels for 0%

profile of v4, /device:TPU:11, one launch (start us, length us, event | category | flops | bytes accessed | tf_op | source)
XLA Modules:
  0.0 111.0 jit_solution(14135082300416633357)
XLA Ops:
  0.0 2.8 %copy.31 = bf16[1,16,32,2048]{3,1,2,0:T(8,128)(2,1)S(1)} copy(bf16[1,16,32,2048]{3,2,1,0:T(8,128)(2,1)} %param.9) | data formatting | bytes 4194304 | tf_op args[0]
  2.9 3.2 %collective-permute-start.1 = (bf16[2,16,2048]{2,1,0:T(8,128)(2,1)S(1)}, bf16[2,16,2048]{2,1,0:T(8,128)(2,1)S(1)}, u32[]{:S(2)}, u32[]{:S(2)}) collective-permute-start(bf16[2,16,2048]{2,1,0:T(8,128)(2,1)S(1)} %get-tuple-element.13), channel_id=1, source_target_pairs={{1,2},{2,1},{5,6},{6,5},{9,10},{10,9},{13,14},{14,13},{17,18},{18,... | collective-permute-start | bytes 393224 | tf_op jit(solution)/shard_map/ppermute | solution.py:23
  7.0 0.1 constant_dynamic-update-slice_fusion.14
  7.7 1.5 %collective-permute-done.1.odd_ref = bf16[2,16,2048]{2,1,0:T(8,128)(2,1)S(1)} collective-permute-done((bf16[2,16,2048]{2,1,0:T(8,128)(2,1)S(1)}, bf16[2,16,2048]{2,1,0:T(8,128)(2,1)S(1)}, u32[]{:S(2)}, u32[]{:S(2)}) %collective-permute-start.1) | collective-permute-done | bytes 131104 | tf_op jit(solution)/shard_map/ppermute | solution.py:23
  9.1 1.1 %collective-permute-done.even_ref = bf16[2,16,2048]{2,1,0:T(8,128)(2,1)S(1)} collective-permute-done((bf16[2,16,2048]{2,1,0:T(8,128)(2,1)S(1)}, bf16[2,16,2048]{2,1,0:T(8,128)(2,1)S(1)}, u32[]{:S(2)}, u32[]{:S(2)}) %collective-permute-start) | collective-permute-done | bytes 131104 | tf_op jit(solution)/shard_map/ppermute | solution.py:23
  10.3 17.3 %shard_map.91 = bf16[32,264,128]{2,1,0:T(8,128)(2,1)S(1)} custom-call(s32[3]{0:T(128)S(1)} %pad_add_fusion.place_ref, s32[32,16]{1,0:T(8,128)S(1)} %fusion.1.slot_ref, bf16[32,16,2048]{2,1,0:T(8,128)(2,1)S(1)} %bitcast.72, bf16[2,16,2048]{2,1,0:T(8,128)(2,1)S(1)} %collective-permute-done.even_ref, bf16[2,16,2048]{2,1,0:T(8,128)(2,1)S(1)} %collective-permute-done.1.odd_ref, ...), custom_call_target="tpu_custom_call" | custom-call | tf_op jit(solution)/shard_map/pallas_call | solution.py:430
  27.6 1.3 %copy-done = bf16[32,264,128]{2,1,0:T(8,128)(2,1)} copy-done((bf16[32,264,128]{2,1,0:T(8,128)(2,1)}, bf16[32,264,128]{2,1,0:T(8,128)(2,1)S(1)}, u32[]{:S(2)}) %copy-start) | copy-done | bytes 2162712
  28.9 5.4 %all-to-all-start = ((bf16[32,264,128]{2,1,0:T(8,128)(2,1)}), bf16[32,264,128]{2,1,0:T(8,128)(2,1)S(1)}, u32[]{:S(2)}, u32[]{:S(2)}) async-start(bf16[32,264,128]{2,1,0:T(8,128)(2,1)} %copy-done), calls=%async_computation | async-start | bytes 4325376 | tf_op jit(solution)/shard_map/all_to_all | solution.py:441
  34.3 0.1 iota.60
  34.4 0.1 iota.54
  34.5 0.1 iota.57
  34.6 0.1 iota.51
  34.8 0.1 reshape.22.tile_ref
  34.9 0.1 constant_dynamic-update-slice_fusion.25
  35.4 0.1 and_convert_fusion.residual_ref
  35.5 47.5 %all-to-all-done.incoming_ref = bf16[32,264,128]{2,1,0:T(8,128)(2,1)S(1)} async-done(((bf16[32,264,128]{2,1,0:T(8,128)(2,1)}), bf16[32,264,128]{2,1,0:T(8,128)(2,1)S(1)}, u32[]{:S(2)}, u32[]{:S(2)}) %all-to-all-start) | async-done | bytes 2162720 | tf_op jit(solution)/shard_map/all_to_all | solution.py:441
  83.0 7.6 %shard_map.92 = (bf16[16384,128]{1,0:T(8,128)(2,1)S(1)}, bf16[16,2048]{1,0:T(8,128)(2,1)S(1)}, bf16[16,128]{1,0:T(8,128)(2,1)S(1)}, bf16[16,128]{1,0:T(8,128)(2,1)S(1)}) custom-call(s32[3]{0:T(128)S(1)} %pad_add_fusion.place_ref, s32[1,512]{1,0:T(1,128)S(1)} %reshape.22.tile_ref, bf16[32,264,128]{2,1,0:T(8,128)(2,1)S(1)} %all-to-all-done.incoming_ref), custom_call_target="tpu_custom_call" | custom-call | tf_op jit(solution)/shard_map/pallas_call | solution.py:226
  90.5 1.6 %collective-permute-start.2 = (bf16[16,128]{1,0:T(8,128)(2,1)S(1)}, bf16[16,128]{1,0:T(8,128)(2,1)S(1)}, u32[]{:S(2)}, u32[]{:S(2)}) collective-permute-start(bf16[16,128]{1,0:T(8,128)(2,1)S(1)} %get-tuple-element.10), channel_id=1, source_target_pairs={{0,1},{2,3},{1,0},{3,2},{4,5},{6,7},{5,4},{7,6},{8,9},{10,11},{9,8... | collective-permute-start | bytes 12296 | tf_op jit(solution)/shard_map/ppermute | solution.py:23
  92.1 1.9 %collective-permute-start.3 = (bf16[16,128]{1,0:T(8,128)(2,1)S(1)}, bf16[16,128]{1,0:T(8,128)(2,1)S(1)}, u32[]{:S(2)}, u32[]{:S(2)}) collective-permute-start(bf16[16,128]{1,0:T(8,128)(2,1)S(1)} %get-tuple-element.11), channel_id=1, source_target_pairs={{1,2},{2,1},{5,6},{6,5},{9,10},{10,9},{13,14},{14,13},{17,18},{18,... | collective-permute-start | bytes 12296 | tf_op jit(solution)/shard_map/ppermute | solution.py:23
  94.1 2.4 %collective-permute-done.3.odd_end_ref = bf16[16,128]{1,0:T(8,128)(2,1)S(1)} collective-permute-done((bf16[16,128]{1,0:T(8,128)(2,1)S(1)}, bf16[16,128]{1,0:T(8,128)(2,1)S(1)}, u32[]{:S(2)}, u32[]{:S(2)}) %collective-permute-start.3) | collective-permute-done | bytes 4128 | tf_op jit(solution)/shard_map/ppermute | solution.py:23
  96.5 3.6 %collective-permute-start.5 = (bf16[16,2304]{1,0:T(8,128)(2,1)S(1)}, bf16[16,2304]{1,0:T(8,128)(2,1)S(1)}, u32[]{:S(2)}, u32[]{:S(2)}) collective-permute-start(bf16[16,2304]{1,0:T(8,128)(2,1)S(1)} %constant_dynamic-update-slice_fusion.16), channel_id=1, source_target_pairs={{4,8},{12,16},{20,24},{8,4},{16,12},{24,20},{5,9},{13,17},{21,25},... | collective-permute-start | bytes 221192 | tf_op jit(solution)/shard_map/ppermute | solution.py:23
  100.2 0.1 copy.32
  100.3 2.9 %collective-permute-done.5.odd_rim_ref = bf16[16,2304]{1,0:T(8,128)(2,1)S(1)} collective-permute-done((bf16[16,2304]{1,0:T(8,128)(2,1)S(1)}, bf16[16,2304]{1,0:T(8,128)(2,1)S(1)}, u32[]{:S(2)}, u32[]{:S(2)}) %collective-permute-start.5) | collective-permute-done | bytes 73760 | tf_op jit(solution)/shard_map/ppermute | solution.py:23
  103.2 7.8 %shard_map.93 = bf16[16,1024,128]{2,1,0:T(8,128)(2,1)} custom-call(s32[3]{0:T(128)S(1)} %pad_add_fusion.place_ref, bf16[16384,128]{1,0:T(8,128)(2,1)S(1)} %get-tuple-element.9.joined_ref.prev_ref.next_ref, bf16[16384,128]{1,0:T(8,128)(2,1)S(1)} %get-tuple-element.9.joined_ref.prev_ref.next_ref, ...), custom_call_target="tpu_custom_call" | custom-call | tf_op jit(solution)/shard_map/pallas_call | solution.py:372
  (57 shorter events, 2.2 us)
Async XLA Ops:
  0.0 6.2 %copy-start.4 = (s32[1,1,32,16]{2,3,1,0:T(8,128)S(1)}, s32[1,1,32,16]{2,3,1,0:T(8,128)}, u32[]{:S(2)}) copy-start(s32[1,1,32,16]{2,3,1,0:T(8,128)} %param.13) | copy-start | bytes 6148
  0.0 6.3 %copy-start.5 = (s32[1,1,32,16]{2,3,1,0:T(8,128)S(1)}, s32[1,1,32,16]{2,3,1,0:T(8,128)}, u32[]{:S(2)}) copy-start(s32[1,1,32,16]{2,3,1,0:T(8,128)} %param.14) | copy-start | bytes 6148
  0.0 6.3 %copy-start.6 = (s32[1,1,32,16]{2,3,1,0:T(8,128)S(1)}, s32[1,1,32,16]{2,3,1,0:T(8,128)}, u32[]{:S(2)}) copy-start(s32[1,1,32,16]{2,3,1,0:T(8,128)} %param.15) | copy-start | bytes 6148
  0.0 6.4 %copy-start.1 = (bf16[16,144]{1,0:T(8,128)(2,1)S(1)}, bf16[16,144]{1,0:T(8,128)(2,1)}, u32[]{:S(2)}) copy-start(bf16[16,144]{1,0:T(8,128)(2,1)} %param.10) | copy-start | bytes 13828
  0.0 6.9 %copy-start.2 = (bf16[16,144]{1,0:T(8,128)(2,1)S(1)}, bf16[16,144]{1,0:T(8,128)(2,1)}, u32[]{:S(2)}) copy-start(bf16[16,144]{1,0:T(8,128)(2,1)} %param.11) | copy-start | bytes 13828
  0.0 7.4 %copy-start.8 = (s32[1,1,32]{2,1,0:T(1,128)S(1)}, s32[1,1,32]{2,1,0:T(1,128)}, u32[]{:S(2)}) copy-start(s32[1,1,32]{2,1,0:T(1,128)} %param.16) | copy-start | bytes 388
  2.9 6.3 %collective-permute-start.1 = (bf16[2,16,2048]{2,1,0:T(8,128)(2,1)S(1)}, bf16[2,16,2048]{2,1,0:T(8,128)(2,1)S(1)}, u32[]{:S(2)}, u32[]{:S(2)}) collective-permute-start(bf16[2,16,2048]{2,1,0:T(8,128)(2,1)S(1)} %get-tuple-element.13), channel_id=1, source_target_pairs={{1,2},{2,1},{5,6},{6,5},{9,10},{10,9},{13,14},{14,13},{17,18},{18,... | collective-permute-start | bytes 393224 | tf_op jit(solution)/shard_map/ppermute | solution.py:23
  6.1 4.2 %collective-permute-start = (bf16[2,16,2048]{2,1,0:T(8,128)(2,1)S(1)}, bf16[2,16,2048]{2,1,0:T(8,128)(2,1)S(1)}, u32[]{:S(2)}, u32[]{:S(2)}) collective-permute-start(bf16[2,16,2048]{2,1,0:T(8,128)(2,1)S(1)} %get-tuple-element.14), channel_id=1, source_target_pairs={{0,1},{2,3},{1,0},{3,2},{4,5},{6,7},{5,4},{7,6},{8,9},{10,11},{9,8... | collective-permute-start | bytes 393224 | tf_op jit(solution)/shard_map/ppermute | solution.py:23
  27.6 1.3 %copy-start = (bf16[32,264,128]{2,1,0:T(8,128)(2,1)}, bf16[32,264,128]{2,1,0:T(8,128)(2,1)S(1)}, u32[]{:S(2)}) copy-start(bf16[32,264,128]{2,1,0:T(8,128)(2,1)S(1)} %shard_map.91) | copy-start | bytes 6488068
  28.9 5.8 %copy-start.7 = (s32[1,1,32,16]{2,3,1,0:T(8,128)S(1)}, s32[1,1,32,16]{2,3,1,0:T(8,128)}, u32[]{:S(2)}) copy-start(s32[1,1,32,16]{2,3,1,0:T(8,128)} %param.17) | copy-start | bytes 6148
  28.9 6.0 %copy-start.3 = (bf16[16,144]{1,0:T(8,128)(2,1)S(1)}, bf16[16,144]{1,0:T(8,128)(2,1)}, u32[]{:S(2)}) copy-start(bf16[16,144]{1,0:T(8,128)(2,1)} %param.12) | copy-start | bytes 13828
  28.9 54.0 %all-to-all-start = ((bf16[32,264,128]{2,1,0:T(8,128)(2,1)}), bf16[32,264,128]{2,1,0:T(8,128)(2,1)S(1)}, u32[]{:S(2)}, u32[]{:S(2)}) async-start(bf16[32,264,128]{2,1,0:T(8,128)(2,1)} %copy-done), calls=%async_computation | async-start | bytes 4325376 | tf_op jit(solution)/shard_map/all_to_all | solution.py:441
  90.5 3.5 %collective-permute-start.2 = (bf16[16,128]{1,0:T(8,128)(2,1)S(1)}, bf16[16,128]{1,0:T(8,128)(2,1)S(1)}, u32[]{:S(2)}, u32[]{:S(2)}) collective-permute-start(bf16[16,128]{1,0:T(8,128)(2,1)S(1)} %get-tuple-element.10), channel_id=1, source_target_pairs={{0,1},{2,3},{1,0},{3,2},{4,5},{6,7},{5,4},{7,6},{8,9},{10,11},{9,8... | collective-permute-start | bytes 12296 | tf_op jit(solution)/shard_map/ppermute | solution.py:23
  92.1 4.3 %collective-permute-start.3 = (bf16[16,128]{1,0:T(8,128)(2,1)S(1)}, bf16[16,128]{1,0:T(8,128)(2,1)S(1)}, u32[]{:S(2)}, u32[]{:S(2)}) collective-permute-start(bf16[16,128]{1,0:T(8,128)(2,1)S(1)} %get-tuple-element.11), channel_id=1, source_target_pairs={{1,2},{2,1},{5,6},{6,5},{9,10},{10,9},{13,14},{14,13},{17,18},{18,... | collective-permute-start | bytes 12296 | tf_op jit(solution)/shard_map/ppermute | solution.py:23
  96.5 6.8 %collective-permute-start.5 = (bf16[16,2304]{1,0:T(8,128)(2,1)S(1)}, bf16[16,2304]{1,0:T(8,128)(2,1)S(1)}, u32[]{:S(2)}, u32[]{:S(2)}) collective-permute-start(bf16[16,2304]{1,0:T(8,128)(2,1)S(1)} %constant_dynamic-update-slice_fusion.16), channel_id=1, source_target_pairs={{4,8},{12,16},{20,24},{8,4},{16,12},{24,20},{5,9},{13,17},{21,25},... | collective-permute-start | bytes 221192 | tf_op jit(solution)/shard_map/ppermute | solution.py:23
  100.1 3.2 %collective-permute-start.4 = (bf16[16,2304]{1,0:T(8,128)(2,1)S(1)}, bf16[16,2304]{1,0:T(8,128)(2,1)S(1)}, u32[]{:S(2)}, u32[]{:S(2)}) collective-permute-start(bf16[16,2304]{1,0:T(8,128)(2,1)S(1)} %constant_dynamic-update-slice_fusion.16), channel_id=1, source_target_pairs={{0,4},{8,12},{16,20},{24,28},{4,0},{12,8},{20,16},{28,24},{1,5},{9... | collective-permute-start | bytes 221192 | tf_op jit(solution)/shard_map/ppermute | solution.py:23

commit v5 on v4

v5 whole, which is shorter than its diff:
```python
import jax
import jax.numpy as jnp
from jax import lax
from jax.experimental import pallas as pl
from jax.experimental.pallas import tpu as pltpu
from jax.sharding import PartitionSpec as P

TL = 128
AR_DEV = 1024
GROUP = 8
CHUNK = 512
PAD = 4
SHIFT_BIT = 16
WEIGHT_BIT = 23
VMEM_BYTES = 32 * 1024 * 1024
SEND_BYTES = 36 * 1024 * 1024
WHOLE = pl.BlockSpec(memory_space=pltpu.VMEM)
SCALARS = pl.BlockSpec(memory_space=pltpu.SMEM)


def swap(even_pairs, odd_pairs, axis):
    count = lax.axis_size(axis)
    received = []
    for start, cells in enumerate((even_pairs, odd_pairs)):
        pairs = [(i, i + 1) for i in range(start, count - 1, 2)]
        received.append(lax.ppermute(cells, axis, pairs + [(j, i) for i, j in pairs]))
    return received


def ordered(odd, even_pairs, odd_pairs):
    return jnp.where(odd, even_pairs, odd_pairs), jnp.where(odd, odd_pairs, even_pairs)


def band(weight, channel_major):
    tap_row = weight.shape[1] // 3
    rows = [
        jnp.pad(weight, ((0, 0), (tap_row * r, tap_row * (GROUP - 1 - r)))) for r in range(GROUP)
    ]
    stacked = jnp.stack(rows, axis=1 if channel_major else 0)
    return stacked.reshape(-1, stacked.shape[-1])


def lanes_of(shape):
    return lax.broadcasted_iota(jnp.int32, shape, len(shape) - 1)


def send_kernel(
    place_ref,
    slot_ref,
    image_ref,
    even_ref,
    odd_ref,
    first_ref,
    second_ref,
    sent_ref,
    pixel_ref,
    taps_ref,
    hidden_ref,
    hidden_taps_ref,
    feature_ref,
    slots_ref,
    payload_ref,
    sent_sems,
):
    channels, rows, width = image_ref.shape
    tap = 3 * channels
    reach = (GROUP + 2) * tap
    lanes = lanes_of((channels, TL))
    zero = jnp.zeros((channels, TL), jnp.bfloat16)
    per_row = width // TL
    chunk = CHUNK // TL
    chunks = per_row // chunk
    odd = place_ref[0] % 2 == 1
    has_above = (place_ref[0] > 0).astype(jnp.float32)
    has_below = (place_ref[0] < place_ref[1] - 1).astype(jnp.float32)

    def spread(c, count, tile_of, out_ref):
        begin = c * chunk
        for i in range(count):
            tiles = [
                tile_of(i, m) if 0 <= m < per_row else zero
                for m in range(begin - 1, begin + chunk + 1)
            ]
            ahead = [pltpu.roll(cells, 1, 1) for cells in tiles[:-1]]
            back = [pltpu.roll(cells, TL - 1, 1) for cells in tiles[1:]]
            for k in range(chunk):
                cols = slice((begin + k) * TL, (begin + k + 1) * TL)
                base = i * tap
                out_ref[base : base + channels, cols] = jnp.where(lanes == 0, ahead[k], ahead[k + 1])
                out_ref[base + channels : base + 2 * channels, cols] = tiles[k + 1]
                out_ref[base + 2 * channels : base + tap, cols] = jnp.where(
                    lanes == TL - 1, back[k + 1], back[k]
                )

    def turn_rows(c):
        for m in range(c * chunk, (c + 1) * chunk):
            for q in range(channels):
                cells = image_ref[q, :, m * TL : (m + 1) * TL]
                base = q * (rows + PAD)
                pixel_ref[m, base : base + rows, :] = cells.astype(jnp.float32)

    def pixel_tile(i, m):
        cols = slice(m * TL, (m + 1) * TL)
        if i < 2 or i >= rows + 2:
            r = i if i < 2 else i - rows - 2
            above, below = ordered(odd, even_ref[r, :, cols], odd_ref[r, :, cols])
            return above if i < 2 else below
        return pixel_ref[m, pl.ds(i - 2, channels, stride=rows + PAD), :].astype(jnp.bfloat16)

    def hidden_tile(i, m):
        return hidden_ref[i, :, m * TL : (m + 1) * TL]

    def activate(v):
        half = 0.5 * v
        return half + half * jnp.tanh(half)

    step = 2 * TL

    def convolve_first(c):
        for j in range(c * CHUNK // step, (c + 1) * CHUNK // step):
            cols = slice(j * step, (j + 1) * step)
            for g in range(rows // GROUP):
                window = taps_ref[g * GROUP * tap : g * GROUP * tap + reach, cols]
                out = activate(jnp.dot(first_ref[...], window, preferred_element_type=jnp.float32))
                out = out.reshape(GROUP, channels, step)
                if g == 0:
                    out = jnp.concatenate([out[:1] * has_above, out[1:]], axis=0)
                hidden_ref[g * GROUP : (g + 1) * GROUP, :, cols] = out.astype(jnp.bfloat16)
            window = taps_ref[rows * tap : (rows + 4) * tap, cols]
            out = activate(
                jnp.dot(
                    first_ref[: 2 * channels, : 4 * tap], window, preferred_element_type=jnp.float32
                )
            ).reshape(2, channels, step)
            out = jnp.concatenate([out[:1], out[1:] * has_below], axis=0)
            hidden_ref[rows : rows + 2, :, cols] = out.astype(jnp.bfloat16)

    def convolve_second(c):
        for j in range(c * CHUNK // step, (c + 1) * CHUNK // step):
            cols = slice(j * step, (j + 1) * step)
            for g in range(rows // GROUP):
                window = hidden_taps_ref[g * GROUP * tap : g * GROUP * tap + reach, cols]
                out = jnp.dot(second_ref[...], window, preferred_element_type=jnp.float32)
                out = out.astype(jnp.bfloat16).reshape(GROUP, channels, step)
                for r in range(GROUP):
                    for half in range(2):
                        feature_ref[(g * GROUP + r) * per_row + 2 * j + half] = out[
                            r, :, half * TL : (half + 1) * TL
                        ]

    turn_rows(0)
    for s in range(chunks + 4):
        if s + 1 < chunks:
            turn_rows(s + 1)
        if s < chunks:
            spread(s, rows + 4, pixel_tile, taps_ref)
        if 0 <= s - 1 < chunks:
            convolve_first(s - 1)
        if 0 <= s - 3 < chunks:
            spread(s - 3, rows + 2, hidden_tile, hidden_taps_ref)
        if 0 <= s - 4 < chunks:
            convolve_second(s - 4)

    peers, capacity = slot_ref.shape
    half = capacity // 2
    side = lanes_of((half, TL)) < TL // 2
    slot_row = lax.broadcasted_iota(jnp.int32, (half, TL), 0)

    chunks = sent_sems.shape[0]
    batch = peers // chunks

    def flush(c):
        part = pl.ds(c * batch, batch)
        return pltpu.make_async_copy(payload_ref.at[part], sent_ref.at[part], sent_sems.at[c])

    @pl.loop(0, peers)
    def _(d):
        record = jnp.zeros((half, TL), jnp.float32)
        for k in range(capacity):
            slot = slot_ref[d, k]
            scale = lax.shift_right_logical(slot, WEIGHT_BIT).astype(jnp.float32) * 0.0625
            cells = feature_ref[slot & ((1 << SHIFT_BIT) - 1)]
            shift = lax.shift_right_logical(slot, SHIFT_BIT) & (TL - 1)
            cells = pltpu.roll(cells, shift, 1).astype(jnp.float32) * scale
            slots_ref[pl.ds(k, channels, stride=capacity + PAD), :] = cells
            here = (slot_row == k % half) & (side == (k < half))
            record = jnp.where(here, scale, record)
        for q in range(channels):
            base = q * (capacity + PAD)
            payload_ref[d, q * capacity : (q + 1) * capacity, :] = slots_ref[
                base : base + capacity, :
            ].astype(jnp.bfloat16)
        payload_ref[d, channels * capacity :, :] = record.astype(jnp.bfloat16)

        @pl.when(d % batch == batch - 1)
        def _():
            flush(d // batch).start()

    for c in range(chunks):
        flush(c).wait()


def scales_of(incoming_ref, entries):
    peers, message, lanes = incoming_ref.shape
    capacity = entries // peers
    half = capacity // 2
    record = incoming_ref[:, message - half :, :].astype(jnp.float32).reshape(peers * half, lanes)
    other = pltpu.roll(record, lanes // 2, 1)
    side = lanes_of(record.shape) < lanes // 2
    low = jnp.where(side, record, other).reshape(peers, half, lanes)
    high = jnp.where(side, other, record).reshape(peers, half, lanes)
    return jnp.concatenate([low, high], axis=1).reshape(entries, lanes).astype(jnp.bfloat16)


def join_kernel(
    place_ref,
    tile_ref,
    incoming_ref,
    joined_ref,
    edge_ref,
    even_ref,
    odd_ref,
    even_cells_ref,
    odd_cells_ref,
    scales_ref,
):
    peers = incoming_ref.shape[0]
    entries = tile_ref.shape[1]
    capacity = entries // peers
    channels = edge_ref.shape[0]
    blocks = joined_ref.shape[0] // (TL * channels)
    lanes = lanes_of((channels, TL))
    scales_ref[...] = scales_of(incoming_ref, entries)

    def gather(i, cells_ref):
        ids = lax.broadcasted_iota(jnp.int32, (TL, entries), 0) + i * TL
        onehot = jnp.where(ids == tile_ref[...], 1.0, 0.0).astype(jnp.bfloat16)
        total = jnp.dot(onehot, scales_ref[...], preferred_element_type=jnp.float32)
        inverse = 1.0 / jnp.maximum(total, 1.0)
        for q in range(0, channels, 2):
            pair = jnp.concatenate(
                [
                    incoming_ref[:, p * capacity : (p + 1) * capacity, :].reshape(entries, TL)
                    for p in (q, q + 1)
                ],
                axis=1,
            )
            total = jnp.dot(onehot, pair, preferred_element_type=jnp.float32)
            for p in range(2):
                cells_ref[pl.ds(q + p, TL, stride=channels + PAD), :] = (
                    total[:, p * TL : (p + 1) * TL] * inverse
                )

    def pack(i, cells_ref):
        for part in range(2):
            edge = jnp.zeros((channels, TL), jnp.bfloat16)
            for u in range(TL // 2):
                t = part * (TL // 2) + u
                base = t * (channels + PAD)
                cells = cells_ref[base : base + channels, :].astype(jnp.bfloat16)
                row = pl.multiple_of((i * TL + t) * channels, channels)
                joined_ref[pl.ds(row, channels), :] = cells
                edge = jnp.where(lanes // 2 == u, pltpu.roll(cells, 2 * u + 1, 1), edge)
            edge_ref[:, pl.ds(pl.multiple_of((2 * i + part) * TL, TL), TL)] = edge

    gather(0, even_cells_ref)

    @pl.loop(0, blocks // 2)
    def _(h):
        pack(2 * h, even_cells_ref)
        gather(2 * h + 1, odd_cells_ref)
        pack(2 * h + 1, odd_cells_ref)
        gather(jnp.minimum(2 * h + 2, blocks - 1), even_cells_ref)

    odd = place_ref[0] % 2 == 1
    head = joined_ref[:channels, :]
    tail = joined_ref[-channels:, :]
    even_ref[...] = jnp.where(odd, head, tail)
    odd_ref[...] = jnp.where(odd, tail, head)


def join_call(place, tiles, incoming, channels):
    half = jnp.bfloat16
    entries = tiles.shape[1]
    return pl.pallas_call(
        join_kernel,
        out_shape=(
            jax.ShapeDtypeStruct((AR_DEV * channels, TL), half),
            jax.ShapeDtypeStruct((channels, 2 * AR_DEV), half),
            jax.ShapeDtypeStruct((channels, TL), half),
            jax.ShapeDtypeStruct((channels, TL), half),
        ),
        in_specs=[SCALARS, WHOLE, WHOLE],
        out_specs=(WHOLE,) * 4,
        scratch_shapes=[
            pltpu.VMEM((TL * (channels + PAD), TL), jnp.float32),
            pltpu.VMEM((TL * (channels + PAD), TL), jnp.float32),
            pltpu.VMEM((entries, TL), half),
        ],
        compiler_params=pltpu.CompilerParams(vmem_limit_bytes=VMEM_BYTES),
    )(place, tiles, incoming)


def texture_kernel(
    place_ref,
    joined_ref,
    even_end_ref,
    odd_end_ref,
    even_rim_ref,
    odd_rim_ref,
    weight_ref,
    residual_ref,
    texture_ref,
    even_ref,
    odd_ref,
    even_out_ref,
    odd_out_ref,
    sems,
):
    channels = texture_ref.shape[0]
    blocks = texture_ref.shape[1] // TL
    tap = 3 * channels
    reach = (GROUP + 2) * tap
    lanes = lanes_of((channels, TL))
    odd_row = place_ref[0] % 2
    odd_cam = place_ref[2] % 2 == 1
    above, below = ordered(odd_row == 1, even_end_ref[...], odd_end_ref[...])

    def place(taps_ref, row, cells, edge):
        base = row * tap
        taps_ref[base : base + channels, :] = jnp.where(lanes == 0, edge, pltpu.roll(cells, 1, 1))
        taps_ref[base + channels : base + 2 * channels, :] = cells
        taps_ref[base + 2 * channels : base + 3 * channels, :] = jnp.where(
            lanes == TL - 1, edge, pltpu.roll(cells, TL - 1, 1)
        )

    def edges(before, after, before_lane, after_lane):
        return jnp.where(
            lanes == TL - 1,
            pltpu.roll(after, TL - 1 - after_lane, 1),
            pltpu.roll(before, TL - before_lane, 1),
        )

    def both(part):
        cols = pl.ds(pl.multiple_of(part * TL, TL), TL)
        return ordered(odd_cam, even_rim_ref[:, cols], odd_rim_ref[:, cols])

    def tile(t):
        return joined_ref[pl.ds(pl.multiple_of(t * channels, channels), channels), :]

    def fill(i, taps_ref):
        outer = edges(*both(2 * blocks + 1 - odd_row), TL - 1, 0)
        inner = edges(*both(jnp.maximum(2 * i - 1, 0)), TL - 2, TL - 1)
        cells = jnp.where(i == 0, above, tile(jnp.maximum(i * TL - 1, 0)))
        place(taps_ref, 0, cells, jnp.where(i == 0, outer, inner))
        last = blocks - 1
        outer = edges(*both(2 * blocks + odd_row), TL - 1, 0)
        inner = edges(*both(jnp.minimum(2 * i + 2, 2 * blocks - 1)), 0, 1)
        cells = jnp.where(i == last, below, tile(jnp.minimum((i + 1) * TL, blocks * TL - 1)))
        place(taps_ref, TL + 1, cells, jnp.where(i == last, outer, inner))
        for part in range(2):
            before, after = both(2 * i + part)
            merged = jnp.where(lanes % 2 == 1, after, pltpu.roll(before, 2, 1))
            for u in range(TL // 2):
                t = part * (TL // 2) + u
                place(taps_ref, t + 1, tile(i * TL + t), pltpu.roll(merged, TL - 2 - 2 * u, 1))

    def convolve(taps_ref, out_ref):
        pair = 2 * GROUP
        for i in range(TL // pair):
            base = i * pair * tap

            def side_by_side(start, size, rows):
                return jnp.concatenate(
                    [
                        jnp.concatenate(
                            [
                                taps_ref[at + k * tap : at + k * tap + size, :]
                                for k in range(rows)
                            ],
                            axis=0,
                        )
                        for at in (base + start, base + start + GROUP * tap)
                    ],
                    axis=1,
                )

            out = jnp.dot(
                weight_ref[...], side_by_side(0, reach, 1), preferred_element_type=jnp.float32
            )
            own = side_by_side(tap + channels, channels, GROUP)
            out = out + jnp.dot(residual_ref[...], own, preferred_element_type=jnp.float32)
            out = out.reshape(channels, GROUP, 2 * TL)
            out = jnp.concatenate([out[:, :, :TL], out[:, :, TL:]], axis=1)
            out_ref[:, i * pair : (i + 1) * pair, :] = out.astype(jnp.bfloat16)

    def flush(i, out_ref, slot):
        rows = pl.ds(pl.multiple_of(i * TL, TL), TL)
        return pltpu.make_async_copy(out_ref, texture_ref.at[:, rows, :], sems.at[slot])

    fill(0, even_ref)

    @pl.loop(0, blocks // 2)
    def _(h):
        @pl.when(h > 0)
        def _():
            flush(2 * h - 2, even_out_ref, 0).wait()

        fill(2 * h + 1, odd_ref)
        convolve(even_ref, even_out_ref)
        flush(2 * h, even_out_ref, 0).start()

        @pl.when(h > 0)
        def _():
            flush(2 * h - 1, odd_out_ref, 1).wait()

        fill(jnp.minimum(2 * h + 2, blocks - 1), even_ref)
        convolve(odd_ref, odd_out_ref)
        flush(2 * h + 1, odd_out_ref, 1).start()

    flush(blocks - 2, even_out_ref, 0).wait()
    flush(blocks - 1, odd_out_ref, 1).wait()


def texture_call(place, joined, even_end, odd_end, even_rim, odd_rim, weight, residual):
    channels = even_end.shape[0]
    half = jnp.bfloat16
    taps = pltpu.VMEM(((TL + 2) * 3 * channels, TL), half)
    block = pltpu.VMEM((channels, TL, TL), half)
    return pl.pallas_call(
        texture_kernel,
        out_shape=jax.ShapeDtypeStruct((channels, joined.shape[0] // channels, TL), half),
        in_specs=[SCALARS] + [WHOLE] * 7,
        out_specs=pl.BlockSpec(memory_space=pl.ANY),
        scratch_shapes=[taps, taps, block, block, pltpu.SemaphoreType.DMA((2,))],
        compiler_params=pltpu.CompilerParams(vmem_limit_bytes=VMEM_BYTES),
    )(place, joined, even_end, odd_end, even_rim, odd_rim, weight, residual)


def local(
    image,
    conv_first,
    conv_second,
    conv_uv,
    send_block,
    send_shift,
    send_weight,
    send_count,
    recv_tile,
):
    half = jnp.bfloat16
    pixels = image[0]
    channels, strip_rows, width = pixels.shape
    place = jnp.stack(
        [lax.axis_index("row"), lax.axis_size("row"), lax.axis_index("cam")]
    ).astype(jnp.int32)
    odd = place[0] % 2 == 1
    head = pixels[:, :2].transpose(1, 0, 2)
    tail = pixels[:, -2:].transpose(1, 0, 2)
    near = swap(jnp.where(odd, head, tail), jnp.where(odd, tail, head), "row")
    peers, capacity = send_block.shape[2:]
    entries = peers * capacity
    message = channels * capacity + capacity // 2
    used = lax.broadcasted_iota(jnp.int32, (peers, capacity), 1) < send_count.reshape(peers, 1)
    slots = (
        send_block[0, 0]
        + (send_shift[0, 0] << SHIFT_BIT)
        + (jnp.where(used, send_weight[0, 0], 0) << WEIGHT_BIT)
    )
    payload = pl.pallas_call(
        send_kernel,
        out_shape=jax.ShapeDtypeStruct((peers, message, TL), half),
        scratch_shapes=[
            pltpu.VMEM((width // TL, channels * (strip_rows + PAD), TL), jnp.float32),
            pltpu.VMEM(((strip_rows + 4) * 3 * channels, width), half),
            pltpu.VMEM((strip_rows + 2, channels, width), half),
            pltpu.VMEM(((strip_rows + 2) * 3 * channels, width), half),
            pltpu.VMEM((strip_rows * width // TL, channels, TL), half),
            pltpu.VMEM((channels * (capacity + PAD), TL), jnp.float32),
            pltpu.VMEM((peers, message, TL), half),
            pltpu.SemaphoreType.DMA((8,)),
        ],
        in_specs=[SCALARS] * 2 + [WHOLE] * 5,
        out_specs=pl.BlockSpec(memory_space=pl.ANY),
        compiler_params=pltpu.CompilerParams(vmem_limit_bytes=SEND_BYTES),
    )(place, slots, pixels, *near, band(conv_first, False), band(conv_second, False))
    arrived = lax.all_to_all(payload, ("cam", "row"), split_axis=0, concat_axis=0, tiled=True)
    joined, edge, *ends = join_call(place, recv_tile.reshape(1, entries), arrived, channels)
    ends = swap(*ends, "row")
    rim = jnp.concatenate([edge, *ends], axis=1)
    rims = swap(rim, rim, "cam")
    same = (
        lax.broadcasted_iota(jnp.int32, (channels, GROUP, GROUP, channels), 0)
        == lax.broadcasted_iota(jnp.int32, (channels, GROUP, GROUP, channels), 3)
    ) & (
        lax.broadcasted_iota(jnp.int32, (channels, GROUP, GROUP, channels), 1)
        == lax.broadcasted_iota(jnp.int32, (channels, GROUP, GROUP, channels), 2)
    )
    residual = same.astype(half).reshape(channels * GROUP, GROUP * channels)
    return texture_call(place, joined, *ends, *rims, band(conv_uv, True), residual)


def solution(mesh):
    return jax.shard_map(
        local,
        mesh=mesh,
        in_specs=(
            P("cam", None, "row", None),
            P(),
            P(),
            P(),
            P("cam", "row", None, None),
            P("cam", "row", None, None),
            P("cam", "row", None, None),
            P("cam", "row", None),
            P("row", "cam", None, None),
        ),
        out_specs=P(None, "row", "cam"),
        check_vma=False,
    )
```

time: 111 us -> 100 us (0.901)
  Pallas kernels: 32.7 us -> 22.6 us
  local copies, waits for them, and re-layouts: 6.63 us -> 5.4 us
    pallas_call x3, Pallas kernels: 32.7 us -> 22.6 us  [the longest x1 10.2 us: local(): pl.pallas_call(send_kernel, out_shape=jax.ShapeDtypeStruct((peers, messag...]
    unnamed x46, local copies, waits for them, and re-layouts: 5.88 us -> 4.65 us
  transfers between devices with their start and end apart: 7 -> 7, of which waited for: 5 -> 5; matrix products, arithmetic and copies ran while one was open for 2% -> 3% of each run, Pallas kernels for 0% -> 0%
where the time goes in v5:
time: 100 us; the launch traced here: 99.7 us
  waiting for transfers between devices  55.4 us (55%)
  Pallas kernels  22.6 us (23%)
  starting transfers between devices  15.8 us (16%)
  local copies, waits for them, and re-layouts  5.4 us (5%)
    all_to_all x1, waiting for transfers between devices, local(): lax.all_to_all(payload, ('cam', 'row'), split_axis=0, concat_axis=0, tile...  47.5 us
    ppermute x6, starting transfers between devices, swap(): lax.ppermute(cells, axis, pairs + [(j, i) for i, j in pairs])  10.4 us
    pallas_call x1, Pallas kernels, local(): pl.pallas_call(send_kernel, out_shape=jax.ShapeDtypeStruct((peers, messag...  10.2 us
    ppermute x6, waiting for transfers between devices, swap(): lax.ppermute(cells, axis, pairs + [(j, i) for i, j in pairs])  7.89 us
    pallas_call x1, Pallas kernels, texture_call(): pl.pallas_call(texture_kernel, out_shape=jax.ShapeDtypeStruct((channels,...  7.4 us
    all_to_all x1, starting transfers between devices, local(): lax.all_to_all(payload, ('cam', 'row'), split_axis=0, concat_axis=0, tile...  5.41 us
    pallas_call x1, Pallas kernels, join_call(): pl.pallas_call(join_kernel, out_shape=(jax.ShapeDtypeStruct((AR_DEV * cha...  4.94 us
    unnamed x46, local copies, waits for them, and re-layouts  4.65 us
  transfers between devices with their start and end apart: 7, of which 5 were waited for; matrix products, arithmetic and copies ran while one was open for 3% of the time, Pallas kernels for 0%

profile of v5, /device:TPU:11, one launch (start us, length us, event | category | flops | bytes accessed | tf_op | source)
XLA Modules:
  0.0 99.7 jit_solution(3843898809155394164)
XLA Ops:
  0.0 2.9 %copy.35 = bf16[1,16,32,2048]{3,1,2,0:T(8,128)(2,1)S(1)} copy(bf16[1,16,32,2048]{3,2,1,0:T(8,128)(2,1)} %param.9) | data formatting | bytes 4194304 | tf_op args[0]
  3.0 3.2 %collective-permute-start.1 = (bf16[2,16,2048]{2,1,0:T(8,128)(2,1)S(1)}, bf16[2,16,2048]{2,1,0:T(8,128)(2,1)S(1)}, u32[]{:S(2)}, u32[]{:S(2)}) collective-permute-start(bf16[2,16,2048]{2,1,0:T(8,128)(2,1)S(1)} %get-tuple-element.13), channel_id=1, source_target_pairs={{1,2},{2,1},{5,6},{6,5},{9,10},{10,9},{13,14},{14,13},{17,18},{18,... | collective-permute-start | bytes 393224 | tf_op jit(solution)/shard_map/ppermute | solution.py:26
  6.5 0.1 constant_dynamic-update-slice_fusion.6
  7.1 0.1 constant_dynamic-update-slice_fusion.14
  7.8 1.5 %collective-permute-done.1.odd_ref = bf16[2,16,2048]{2,1,0:T(8,128)(2,1)S(1)} collective-permute-done((bf16[2,16,2048]{2,1,0:T(8,128)(2,1)S(1)}, bf16[2,16,2048]{2,1,0:T(8,128)(2,1)S(1)}, u32[]{:S(2)}, u32[]{:S(2)}) %collective-permute-start.1) | collective-permute-done | bytes 131104 | tf_op jit(solution)/shard_map/ppermute | solution.py:26
  9.3 1.1 %collective-permute-done.even_ref = bf16[2,16,2048]{2,1,0:T(8,128)(2,1)S(1)} collective-permute-done((bf16[2,16,2048]{2,1,0:T(8,128)(2,1)S(1)}, bf16[2,16,2048]{2,1,0:T(8,128)(2,1)S(1)}, u32[]{:S(2)}, u32[]{:S(2)}) %collective-permute-start) | collective-permute-done | bytes 131104 | tf_op jit(solution)/shard_map/ppermute | solution.py:26
  10.4 10.2 %shard_map.91 = bf16[32,264,128]{2,1,0:T(8,128)(2,1)} custom-call(s32[3]{0:T(128)S(1)} %pad_add_fusion.place_ref, s32[32,16]{1,0:T(8,128)S(1)} %fusion.1.slot_ref, bf16[16,32,2048]{2,1,0:T(8,128)(2,1)S(1)} %bitcast.74, bf16[2,16,2048]{2,1,0:T(8,128)(2,1)S(1)} %collective-permute-done.even_ref, bf16[2,16,2048]{2,1,0:T(8,128)(2,1)S(1)} %collective-permute-done.1.odd_ref, ...), custom_call_target="tpu_custom_call" | custom-call | tf_op jit(solution)/shard_map/pallas_call | solution.py:470
  20.6 5.4 %all-to-all-start = ((bf16[32,264,128]{2,1,0:T(8,128)(2,1)}), bf16[32,264,128]{2,1,0:T(8,128)(2,1)S(1)}, u32[]{:S(2)}, u32[]{:S(2)}) async-start(bf16[32,264,128]{2,1,0:T(8,128)(2,1)} %shard_map.91), calls=%async_computation | async-start | bytes 4325376 | tf_op jit(solution)/shard_map/all_to_all | solution.py:487
  26.1 0.1 iota.60
  26.2 0.1 iota.54
  26.2 0.1 iota.57
  26.3 0.1 iota.51
  26.5 0.1 reshape.22.tile_ref
  26.6 0.1 constant_dynamic-update-slice_fusion.25
  27.1 0.1 and_convert_fusion.residual_ref
  27.2 47.5 %all-to-all-done.incoming_ref = bf16[32,264,128]{2,1,0:T(8,128)(2,1)S(1)} async-done(((bf16[32,264,128]{2,1,0:T(8,128)(2,1)}), bf16[32,264,128]{2,1,0:T(8,128)(2,1)S(1)}, u32[]{:S(2)}, u32[]{:S(2)}) %all-to-all-start) | async-done | bytes 2162720 | tf_op jit(solution)/shard_map/all_to_all | solution.py:487
  74.7 4.9 %shard_map.92 = (bf16[16384,128]{1,0:T(8,128)(2,1)S(1)}, bf16[16,2048]{1,0:T(8,128)(2,1)S(1)}, bf16[16,128]{1,0:T(8,128)(2,1)S(1)}, bf16[16,128]{1,0:T(8,128)(2,1)S(1)}) custom-call(s32[3]{0:T(128)S(1)} %pad_add_fusion.place_ref, s32[1,512]{1,0:T(1,128)S(1)} %reshape.22.tile_ref, bf16[32,264,128]{2,1,0:T(8,128)(2,1)S(1)} %all-to-all-done.incoming_ref), custom_call_target="tpu_custom_call" | custom-call | tf_op jit(solution)/shard_map/pallas_call | solution.py:285
  79.6 1.6 %collective-permute-start.2 = (bf16[16,128]{1,0:T(8,128)(2,1)S(1)}, bf16[16,128]{1,0:T(8,128)(2,1)S(1)}, u32[]{:S(2)}, u32[]{:S(2)}) collective-permute-start(bf16[16,128]{1,0:T(8,128)(2,1)S(1)} %get-tuple-element.10), channel_id=1, source_target_pairs={{0,1},{2,3},{1,0},{3,2},{4,5},{6,7},{5,4},{7,6},{8,9},{10,11},{9,8... | collective-permute-start | bytes 12296 | tf_op jit(solution)/shard_map/ppermute | solution.py:26
  81.2 1.9 %collective-permute-start.3 = (bf16[16,128]{1,0:T(8,128)(2,1)S(1)}, bf16[16,128]{1,0:T(8,128)(2,1)S(1)}, u32[]{:S(2)}, u32[]{:S(2)}) collective-permute-start(bf16[16,128]{1,0:T(8,128)(2,1)S(1)} %get-tuple-element.11), channel_id=1, source_target_pairs={{1,2},{2,1},{5,6},{6,5},{9,10},{10,9},{13,14},{14,13},{17,18},{18,... | collective-permute-start | bytes 12296 | tf_op jit(solution)/shard_map/ppermute | solution.py:26
  83.2 2.4 %collective-permute-done.3.odd_end_ref = bf16[16,128]{1,0:T(8,128)(2,1)S(1)} collective-permute-done((bf16[16,128]{1,0:T(8,128)(2,1)S(1)}, bf16[16,128]{1,0:T(8,128)(2,1)S(1)}, u32[]{:S(2)}, u32[]{:S(2)}) %collective-permute-start.3) | collective-permute-done | bytes 4128 | tf_op jit(solution)/shard_map/ppermute | solution.py:26
  85.6 3.6 %collective-permute-start.5 = (bf16[16,2304]{1,0:T(8,128)(2,1)S(1)}, bf16[16,2304]{1,0:T(8,128)(2,1)S(1)}, u32[]{:S(2)}, u32[]{:S(2)}) collective-permute-start(bf16[16,2304]{1,0:T(8,128)(2,1)S(1)} %constant_dynamic-update-slice_fusion.16), channel_id=1, source_target_pairs={{4,8},{12,16},{20,24},{8,4},{16,12},{24,20},{5,9},{13,17},{21,25},... | collective-permute-start | bytes 221192 | tf_op jit(solution)/shard_map/ppermute | solution.py:26
  89.3 0.1 copy.36
  89.4 2.9 %collective-permute-done.5.odd_rim_ref = bf16[16,2304]{1,0:T(8,128)(2,1)S(1)} collective-permute-done((bf16[16,2304]{1,0:T(8,128)(2,1)S(1)}, bf16[16,2304]{1,0:T(8,128)(2,1)S(1)}, u32[]{:S(2)}, u32[]{:S(2)}) %collective-permute-start.5) | collective-permute-done | bytes 73760 | tf_op jit(solution)/shard_map/ppermute | solution.py:26
  92.3 7.4 %shard_map.93 = bf16[16,1024,128]{2,1,0:T(8,128)(2,1)} custom-call(s32[3]{0:T(128)S(1)} %pad_add_fusion.place_ref, bf16[16384,128]{1,0:T(8,128)(2,1)S(1)} %get-tuple-element.9.joined_ref, bf16[16,128]{1,0:T(8,128)(2,1)S(1)} %collective-permute-done.2.even_end_ref, bf16[16,128]{1,0:T(8,128)(2,1)S(1)} %collective-permute-done.3.odd_end_ref, ...), custom_call_target="tpu_custom_call" | custom-call | tf_op jit(solution)/shard_map/pallas_call | solution.py:430
  (57 shorter events, 2.1 us)
Async XLA Ops:
  0.0 6.3 %copy-start.4 = (s32[1,1,32,16]{2,3,1,0:T(8,128)S(1)}, s32[1,1,32,16]{2,3,1,0:T(8,128)}, u32[]{:S(2)}) copy-start(s32[1,1,32,16]{2,3,1,0:T(8,128)} %param.13) | copy-start | bytes 6148
  0.0 6.4 %copy-start.5 = (s32[1,1,32,16]{2,3,1,0:T(8,128)S(1)}, s32[1,1,32,16]{2,3,1,0:T(8,128)}, u32[]{:S(2)}) copy-start(s32[1,1,32,16]{2,3,1,0:T(8,128)} %param.14) | copy-start | bytes 6148
  0.0 6.4 %copy-start.6 = (s32[1,1,32,16]{2,3,1,0:T(8,128)S(1)}, s32[1,1,32,16]{2,3,1,0:T(8,128)}, u32[]{:S(2)}) copy-start(s32[1,1,32,16]{2,3,1,0:T(8,128)} %param.15) | copy-start | bytes 6148
  0.0 6.5 %copy-start.1 = (bf16[16,144]{1,0:T(8,128)(2,1)S(1)}, bf16[16,144]{1,0:T(8,128)(2,1)}, u32[]{:S(2)}) copy-start(bf16[16,144]{1,0:T(8,128)(2,1)} %param.10) | copy-start | bytes 13828
  0.0 7.1 %copy-start.2 = (bf16[16,144]{1,0:T(8,128)(2,1)S(1)}, bf16[16,144]{1,0:T(8,128)(2,1)}, u32[]{:S(2)}) copy-start(bf16[16,144]{1,0:T(8,128)(2,1)} %param.11) | copy-start | bytes 13828
  0.0 7.5 %copy-start.8 = (s32[1,1,32]{2,1,0:T(1,128)S(1)}, s32[1,1,32]{2,1,0:T(1,128)}, u32[]{:S(2)}) copy-start(s32[1,1,32]{2,1,0:T(1,128)} %param.16) | copy-start | bytes 388
  0.0 10.3 %copy-start = (bf16[1,16,32,2048]{3,2,1,0:T(8,128)(2,1)S(1)}, bf16[1,16,32,2048]{3,2,1,0:T(8,128)(2,1)}, u32[]{:S(2)}) copy-start(bf16[1,16,32,2048]{3,2,1,0:T(8,128)(2,1)} %param.9) | copy-start | bytes 6291460
  3.0 6.3 %collective-permute-start.1 = (bf16[2,16,2048]{2,1,0:T(8,128)(2,1)S(1)}, bf16[2,16,2048]{2,1,0:T(8,128)(2,1)S(1)}, u32[]{:S(2)}, u32[]{:S(2)}) collective-permute-start(bf16[2,16,2048]{2,1,0:T(8,128)(2,1)S(1)} %get-tuple-element.13), channel_id=1, source_target_pairs={{1,2},{2,1},{5,6},{6,5},{9,10},{10,9},{13,14},{14,13},{17,18},{18,... | collective-permute-start | bytes 393224 | tf_op jit(solution)/shard_map/ppermute | solution.py:26
  6.2 4.2 %collective-permute-start = (bf16[2,16,2048]{2,1,0:T(8,128)(2,1)S(1)}, bf16[2,16,2048]{2,1,0:T(8,128)(2,1)S(1)}, u32[]{:S(2)}, u32[]{:S(2)}) collective-permute-start(bf16[2,16,2048]{2,1,0:T(8,128)(2,1)S(1)} %get-tuple-element.14), channel_id=1, source_target_pairs={{0,1},{2,3},{1,0},{3,2},{4,5},{6,7},{5,4},{7,6},{8,9},{10,11},{9,8... | collective-permute-start | bytes 393224 | tf_op jit(solution)/shard_map/ppermute | solution.py:26
  20.6 5.8 %copy-start.7 = (s32[1,1,32,16]{2,3,1,0:T(8,128)S(1)}, s32[1,1,32,16]{2,3,1,0:T(8,128)}, u32[]{:S(2)}) copy-start(s32[1,1,32,16]{2,3,1,0:T(8,128)} %param.17) | copy-start | bytes 6148
  20.6 6.0 %copy-start.3 = (bf16[16,144]{1,0:T(8,128)(2,1)S(1)}, bf16[16,144]{1,0:T(8,128)(2,1)}, u32[]{:S(2)}) copy-start(bf16[16,144]{1,0:T(8,128)(2,1)} %param.12) | copy-start | bytes 13828
  20.6 54.1 %all-to-all-start = ((bf16[32,264,128]{2,1,0:T(8,128)(2,1)}), bf16[32,264,128]{2,1,0:T(8,128)(2,1)S(1)}, u32[]{:S(2)}, u32[]{:S(2)}) async-start(bf16[32,264,128]{2,1,0:T(8,128)(2,1)} %shard_map.91), calls=%async_computation | async-start | bytes 4325376 | tf_op jit(solution)/shard_map/all_to_all | solution.py:487
  79.6 3.5 %collective-permute-start.2 = (bf16[16,128]{1,0:T(8,128)(2,1)S(1)}, bf16[16,128]{1,0:T(8,128)(2,1)S(1)}, u32[]{:S(2)}, u32[]{:S(2)}) collective-permute-start(bf16[16,128]{1,0:T(8,128)(2,1)S(1)} %get-tuple-element.10), channel_id=1, source_target_pairs={{0,1},{2,3},{1,0},{3,2},{4,5},{6,7},{5,4},{7,6},{8,9},{10,11},{9,8... | collective-permute-start | bytes 12296 | tf_op jit(solution)/shard_map/ppermute | solution.py:26
  81.2 4.3 %collective-permute-start.3 = (bf16[16,128]{1,0:T(8,128)(2,1)S(1)}, bf16[16,128]{1,0:T(8,128)(2,1)S(1)}, u32[]{:S(2)}, u32[]{:S(2)}) collective-permute-start(bf16[16,128]{1,0:T(8,128)(2,1)S(1)} %get-tuple-element.11), channel_id=1, source_target_pairs={{1,2},{2,1},{5,6},{6,5},{9,10},{10,9},{13,14},{14,13},{17,18},{18,... | collective-permute-start | bytes 12296 | tf_op jit(solution)/shard_map/ppermute | solution.py:26
  85.6 6.8 %collective-permute-start.5 = (bf16[16,2304]{1,0:T(8,128)(2,1)S(1)}, bf16[16,2304]{1,0:T(8,128)(2,1)S(1)}, u32[]{:S(2)}, u32[]{:S(2)}) collective-permute-start(bf16[16,2304]{1,0:T(8,128)(2,1)S(1)} %constant_dynamic-update-slice_fusion.16), channel_id=1, source_target_pairs={{4,8},{12,16},{20,24},{8,4},{16,12},{24,20},{5,9},{13,17},{21,25},... | collective-permute-start | bytes 221192 | tf_op jit(solution)/shard_map/ppermute | solution.py:26
  89.2 3.2 %collective-permute-start.4 = (bf16[16,2304]{1,0:T(8,128)(2,1)S(1)}, bf16[16,2304]{1,0:T(8,128)(2,1)S(1)}, u32[]{:S(2)}, u32[]{:S(2)}) collective-permute-start(bf16[16,2304]{1,0:T(8,128)(2,1)S(1)} %constant_dynamic-update-slice_fusion.16), channel_id=1, source_target_pairs={{0,4},{8,12},{16,20},{24,28},{4,0},{12,8},{20,16},{28,24},{1,5},{9... | collective-permute-start | bytes 221192 | tf_op jit(solution)/shard_map/ppermute | solution.py:26

commit v6 on v5

--- a/solution.py
+++ b/solution.py
@@ -50,17 +50,19 @@
     image_ref,
     even_ref,
     odd_ref,
+    first_kernel_ref,
+    second_kernel_ref,
+    sent_ref,
     first_ref,
     second_ref,
-    sent_ref,
     pixel_ref,
     taps_ref,
     hidden_ref,
     hidden_taps_ref,
     feature_ref,
-    slots_ref,
     payload_ref,
     sent_sems,
+    *slots_refs,
 ):
     channels, rows, width = image_ref.shape
     tap = 3 * channels
@@ -109,6 +111,12 @@
 
     def hidden_tile(i, m):
         return hidden_ref[i, :, m * TL : (m + 1) * TL]
+
+    for kernel_ref, band_ref in ((first_kernel_ref, first_ref), (second_kernel_ref, second_ref)):
+        band_ref[...] = jnp.zeros_like(band_ref)
+        for r in range(GROUP):
+            reached = slice(r * tap, (r + 3) * tap)
+            band_ref[r * channels : (r + 1) * channels, reached] = kernel_ref[...]
 
     def activate(v):
         half = 0.5 * v
@@ -173,8 +181,7 @@
         part = pl.ds(c * batch, batch)
         return pltpu.make_async_copy(payload_ref.at[part], sent_ref.at[part], sent_sems.at[c])
 
-    @pl.loop(0, peers)
-    def _(d):
+    def send_to(d, slots_ref):
         record = jnp.zeros((half, TL), jnp.float32)
         for k in range(capacity):
             slot = slot_ref[d, k]
@@ -192,9 +199,11 @@
             ].astype(jnp.bfloat16)
         payload_ref[d, channels * capacity :, :] = record.astype(jnp.bfloat16)
 
-        @pl.when(d % batch == batch - 1)
-        def _():
-            flush(d // batch).start()
+    @pl.loop(0, chunks)
+    def _(c):
+        for u in range(batch):
+            send_to(c * batch + u, slots_refs[u % len(slots_refs)])
+        flush(c).start()
 
     for c in range(chunks):
         flush(c).wait()
@@ -217,6 +226,7 @@
     tile_ref,
     incoming_ref,
     joined_ref,
+    plain_ref,
     edge_ref,
     even_ref,
     odd_ref,
@@ -247,9 +257,10 @@
             )
             total = jnp.dot(onehot, pair, preferred_element_type=jnp.float32)
             for p in range(2):
-                cells_ref[pl.ds(q + p, TL, stride=channels + PAD), :] = (
-                    total[:, p * TL : (p + 1) * TL] * inverse
-                )
+                cells = total[:, p * TL : (p + 1) * TL] * inverse
+                cells_ref[pl.ds(q + p, TL, stride=channels + PAD), :] = cells
+                rows = pl.ds(pl.multiple_of(i * TL, TL), TL)
+                plain_ref[q + p, rows, :] = cells.astype(jnp.bfloat16)
 
     def pack(i, cells_ref):
         for part in range(2):
@@ -286,12 +297,13 @@
         join_kernel,
         out_shape=(
             jax.ShapeDtypeStruct((AR_DEV * channels, TL), half),
+            jax.ShapeDtypeStruct((channels, AR_DEV, TL), half),
             jax.ShapeDtypeStruct((channels, 2 * AR_DEV), half),
             jax.ShapeDtypeStruct((channels, TL), half),
             jax.ShapeDtypeStruct((channels, TL), half),
         ),
         in_specs=[SCALARS, WHOLE, WHOLE],
-        out_specs=(WHOLE,) * 4,
+        out_specs=(WHOLE,) * 5,
         scratch_shapes=[
             pltpu.VMEM((TL * (channels + PAD), TL), jnp.float32),
             pltpu.VMEM((TL * (channels + PAD), TL), jnp.float32),
@@ -304,12 +316,12 @@
 def texture_kernel(
     place_ref,
     joined_ref,
+    plain_ref,
     even_end_ref,
     odd_end_ref,
     even_rim_ref,
     odd_rim_ref,
     weight_ref,
-    residual_ref,
     texture_ref,
     even_ref,
     odd_ref,
@@ -365,34 +377,19 @@
                 t = part * (TL // 2) + u
                 place(taps_ref, t + 1, tile(i * TL + t), pltpu.roll(merged, TL - 2 - 2 * u, 1))
 
-    def convolve(taps_ref, out_ref):
+    def convolve(i, taps_ref, out_ref):
         pair = 2 * GROUP
-        for i in range(TL // pair):
-            base = i * pair * tap
-
-            def side_by_side(start, size, rows):
-                return jnp.concatenate(
-                    [
-                        jnp.concatenate(
-                            [
-                                taps_ref[at + k * tap : at + k * tap + size, :]
-                                for k in range(rows)
-                            ],
-                            axis=0,
-                        )
-                        for at in (base + start, base + start + GROUP * tap)
-                    ],
-                    axis=1,
-                )
-
-            out = jnp.dot(
-                weight_ref[...], side_by_side(0, reach, 1), preferred_element_type=jnp.float32
+        for k in range(TL // pair):
+            base = k * pair * tap
+            window = jnp.concatenate(
+                [taps_ref[at : at + reach, :] for at in (base, base + GROUP * tap)], axis=1
             )
-            own = side_by_side(tap + channels, channels, GROUP)
-            out = out + jnp.dot(residual_ref[...], own, preferred_element_type=jnp.float32)
+            out = jnp.dot(weight_ref[...], window, preferred_element_type=jnp.float32)
             out = out.reshape(channels, GROUP, 2 * TL)
             out = jnp.concatenate([out[:, :, :TL], out[:, :, TL:]], axis=1)
-            out_ref[:, i * pair : (i + 1) * pair, :] = out.astype(jnp.bfloat16)
+            rows = pl.ds(pl.multiple_of(i * TL + k * pair, pair), pair)
+            out = out + plain_ref[:, rows, :].astype(jnp.float32)
+            out_ref[:, k * pair : (k + 1) * pair, :] = out.astype(jnp.bfloat16)
 
     def flush(i, out_ref, slot):
         rows = pl.ds(pl.multiple_of(i * TL, TL), TL)
@@ -407,7 +404,7 @@
             flush(2 * h - 2, even_out_ref, 0).wait()
 
         fill(2 * h + 1, odd_ref)
-        convolve(even_ref, even_out_ref)
+        convolve(2 * h, even_ref, even_out_ref)
         flush(2 * h, even_out_ref, 0).start()
 
         @pl.when(h > 0)
@@ -415,26 +412,26 @@
             flush(2 * h - 1, odd_out_ref, 1).wait()
 
         fill(jnp.minimum(2 * h + 2, blocks - 1), even_ref)
-        convolve(odd_ref, odd_out_ref)
+        convolve(2 * h + 1, odd_ref, odd_out_ref)
         flush(2 * h + 1, odd_out_ref, 1).start()
 
     flush(blocks - 2, even_out_ref, 0).wait()
     flush(blocks - 1, odd_out_ref, 1).wait()
 
 
-def texture_call(place, joined, even_end, odd_end, even_rim, odd_rim, weight, residual):
-    channels = even_end.shape[0]
+def texture_call(place, joined, plain, *edges):
+    channels = plain.shape[0]
     half = jnp.bfloat16
     taps = pltpu.VMEM(((TL + 2) * 3 * channels, TL), half)
     block = pltpu.VMEM((channels, TL, TL), half)
     return pl.pallas_call(
         texture_kernel,
-        out_shape=jax.ShapeDtypeStruct((channels, joined.shape[0] // channels, TL), half),
-        in_specs=[SCALARS] + [WHOLE] * 7,
+        out_shape=jax.ShapeDtypeStruct(plain.shape, half),
+        in_specs=[SCALARS] + [WHOLE] * (2 + len(edges)),
         out_specs=pl.BlockSpec(memory_space=pl.ANY),
         scratch_shapes=[taps, taps, block, block, pltpu.SemaphoreType.DMA((2,))],
         compiler_params=pltpu.CompilerParams(vmem_limit_bytes=VMEM_BYTES),
-    )(place, joined, even_end, odd_end, even_rim, odd_rim, weight, residual)
+    )(place, joined, plain, *edges)
 
 
 def local(
@@ -471,33 +468,27 @@
         send_kernel,
         out_shape=jax.ShapeDtypeStruct((peers, message, TL), half),
         scratch_shapes=[
+            pltpu.VMEM((GROUP * channels, (GROUP + 2) * 3 * channels), half),
+            pltpu.VMEM((GROUP * channels, (GROUP + 2) * 3 * channels), half),
             pltpu.VMEM((width // TL, channels * (strip_rows + PAD), TL), jnp.float32),
             pltpu.VMEM(((strip_rows + 4) * 3 * channels, width), half),
             pltpu.VMEM((strip_rows + 2, channels, width), half),
             pltpu.VMEM(((strip_rows + 2) * 3 * channels, width), half),
             pltpu.VMEM((strip_rows * width // TL, channels, TL), half),
-            pltpu.VMEM((channels * (capacity + PAD), TL), jnp.float32),
             pltpu.VMEM((peers, message, TL), half),
             pltpu.SemaphoreType.DMA((8,)),
-        ],
+        ]
+        + [pltpu.VMEM((channels * (capacity + PAD), TL), jnp.float32) for _ in range(4)],
         in_specs=[SCALARS] * 2 + [WHOLE] * 5,
         out_specs=pl.BlockSpec(memory_space=pl.ANY),
         compiler_params=pltpu.CompilerParams(vmem_limit_bytes=SEND_BYTES),
-    )(place, slots, pixels, *near, band(conv_first, False), band(conv_second, False))
+    )(place, slots, pixels, *near, conv_first, conv_second)
     arrived = lax.all_to_all(payload, ("cam", "row"), split_axis=0, concat_axis=0, tiled=True)
-    joined, edge, *ends = join_call(place, recv_tile.reshape(1, entries), arrived, channels)
+    joined, plain, edge, *ends = join_call(place, recv_tile.reshape(1, entries), arrived, channels)
     ends = swap(*ends, "row")
     rim = jnp.concatenate([edge, *ends], axis=1)
     rims = swap(rim, rim, "cam")
-    same = (
-        lax.broadcasted_iota(jnp.int32, (channels, GROUP, GROUP, channels), 0)
-        == lax.broadcasted_iota(jnp.int32, (channels, GROUP, GROUP, channels), 3)
-    ) & (
-        lax.broadcasted_iota(jnp.int32, (channels, GROUP, GROUP, channels), 1)
-        == lax.broadcasted_iota(jnp.int32, (channels, GROUP, GROUP, channels), 2)
-    )
-    residual = same.astype(half).reshape(channels * GROUP, GROUP * channels)
-    return texture_call(place, joined, *ends, *rims, band(conv_uv, True), residual)
+    return texture_call(place, joined, plain, *ends, *rims, band(conv_uv, True))
 
 
 def solution(mesh):

time: 100 us -> 98 us (0.980)
  Pallas kernels: 22.6 us -> 20.6 us
  waiting for transfers between devices: 55.4 us -> 57 us
  local copies, waits for them, and re-layouts: 5.4 us -> 3.96 us
    pallas_call x1, Pallas kernels: 10.2 us -> 8.35 us  [local(): pl.pallas_call(send_kernel, out_shape=jax.ShapeDtypeStruct((peers, messag...]
    ppermute x6, waiting for transfers between devices: 7.89 us -> 9.01 us  [swap(): lax.ppermute(cells, axis, pairs + [(j, i) for i, j in pairs])]
    unnamed x46 -> x32, local copies, waits for them, and re-layouts: 4.65 us -> 3.72 us
  transfers between devices with their start and end apart: 7 -> 7, of which waited for: 5 -> 5; matrix products, arithmetic and copies ran while one was open for 3% -> 1% of each run, Pallas kernels for 0% -> 0%
where the time goes in v6:
time: 98 us; the launch traced here: 97.8 us
  waiting for transfers between devices  57 us (58%)
  Pallas kernels  20.6 us (21%)
  starting transfers between devices  15.8 us (16%)
  local copies, waits for them, and re-layouts  3.96 us (4%)
    all_to_all x1, waiting for transfers between devices, local(): lax.all_to_all(payload, ('cam', 'row'), split_axis=0, concat_axis=0, tile...  48 us
    ppermute x6, starting transfers between devices, swap(): lax.ppermute(cells, axis, pairs + [(j, i) for i, j in pairs])  10.4 us
    ppermute x6, waiting for transfers between devices, swap(): lax.ppermute(cells, axis, pairs + [(j, i) for i, j in pairs])  9.01 us
    pallas_call x1, Pallas kernels, local(): pl.pallas_call(send_kernel, out_shape=jax.ShapeDtypeStruct((peers, messag...  8.35 us
    pallas_call x1, Pallas kernels, texture_call(): pl.pallas_call(texture_kernel, out_shape=jax.ShapeDtypeStruct(plain.shape...  7.21 us
    all_to_all x1, starting transfers between devices, local(): lax.all_to_all(payload, ('cam', 'row'), split_axis=0, concat_axis=0, tile...  5.41 us
    pallas_call x1, Pallas kernels, join_call(): pl.pallas_call(join_kernel, out_shape=(jax.ShapeDtypeStruct((AR_DEV * cha...  5.04 us
    unnamed x32, local copies, waits for them, and re-layouts  3.72 us
  transfers between devices with their start and end apart: 7, of which 5 were waited for; matrix products, arithmetic and copies ran while one was open for 1% of the time, Pallas kernels for 0%

profile of v6, /device:TPU:11, one launch (start us, length us, event | category | flops | bytes accessed | tf_op | source)
XLA Modules:
  0.0 97.8 jit_solution(6820186575060013806)
XLA Ops:
  0.0 2.9 %copy.35 = bf16[1,16,32,2048]{3,1,2,0:T(8,128)(2,1)S(1)} copy(bf16[1,16,32,2048]{3,2,1,0:T(8,128)(2,1)} %param.9) | data formatting | bytes 4194304 | tf_op args[0]
  3.0 3.2 %collective-permute-start.1 = (bf16[2,16,2048]{2,1,0:T(8,128)(2,1)S(1)}, bf16[2,16,2048]{2,1,0:T(8,128)(2,1)S(1)}, u32[]{:S(2)}, u32[]{:S(2)}) collective-permute-start(bf16[2,16,2048]{2,1,0:T(8,128)(2,1)S(1)} %get-tuple-element.15), channel_id=1, source_target_pairs={{1,2},{2,1},{5,6},{6,5},{9,10},{10,9},{13,14},{14,13},{17,18},{18,... | collective-permute-start | bytes 393224 | tf_op jit(solution)/shard_map/ppermute | solution.py:26
  6.6 0.1 pad_add_fusion.place_ref
  6.7 2.6 %collective-permute-done.1.odd_ref = bf16[2,16,2048]{2,1,0:T(8,128)(2,1)S(1)} collective-permute-done((bf16[2,16,2048]{2,1,0:T(8,128)(2,1)S(1)}, bf16[2,16,2048]{2,1,0:T(8,128)(2,1)S(1)}, u32[]{:S(2)}, u32[]{:S(2)}) %collective-permute-start.1) | collective-permute-done | bytes 131104 | tf_op jit(solution)/shard_map/ppermute | solution.py:26
  9.3 1.1 %collective-permute-done.even_ref = bf16[2,16,2048]{2,1,0:T(8,128)(2,1)S(1)} collective-permute-done((bf16[2,16,2048]{2,1,0:T(8,128)(2,1)S(1)}, bf16[2,16,2048]{2,1,0:T(8,128)(2,1)S(1)}, u32[]{:S(2)}, u32[]{:S(2)}) %collective-permute-start) | collective-permute-done | bytes 131104 | tf_op jit(solution)/shard_map/ppermute | solution.py:26
  10.4 8.3 %shard_map.91 = bf16[32,264,128]{2,1,0:T(8,128)(2,1)} custom-call(s32[3]{0:T(128)S(1)} %pad_add_fusion.place_ref, s32[32,16]{1,0:T(8,128)S(1)} %fusion.1.slot_ref, bf16[16,32,2048]{2,1,0:T(8,128)(2,1)S(1)} %bitcast.40, bf16[2,16,2048]{2,1,0:T(8,128)(2,1)S(1)} %collective-permute-done.even_ref, bf16[2,16,2048]{2,1,0:T(8,128)(2,1)S(1)} %collective-permute-done.1.odd_ref, ...), custom_call_target="tpu_custom_call" | custom-call | tf_op jit(solution)/shard_map/pallas_call | solution.py:467
  18.8 5.4 %all-to-all-start = ((bf16[32,264,128]{2,1,0:T(8,128)(2,1)}), bf16[32,264,128]{2,1,0:T(8,128)(2,1)S(1)}, u32[]{:S(2)}, u32[]{:S(2)}) async-start(bf16[32,264,128]{2,1,0:T(8,128)(2,1)} %shard_map.91), calls=%async_computation | async-start | bytes 4325376 | tf_op jit(solution)/shard_map/all_to_all | solution.py:486
  24.3 0.1 reshape.11.tile_ref
  24.4 0.1 constant_dynamic-update-slice_fusion.9
  24.4 0.1 constant_dynamic-update-slice_fusion.8
  24.5 0.1 constant_dynamic-update-slice_fusion.7
  24.6 0.1 constant_dynamic-update-slice_fusion.6
  24.7 0.1 constant_dynamic-update-slice_fusion.5
  24.8 0.1 constant_dynamic-update-slice_fusion.4
  24.8 48.0 %all-to-all-done.incoming_ref = bf16[32,264,128]{2,1,0:T(8,128)(2,1)S(1)} async-done(((bf16[32,264,128]{2,1,0:T(8,128)(2,1)}), bf16[32,264,128]{2,1,0:T(8,128)(2,1)S(1)}, u32[]{:S(2)}, u32[]{:S(2)}) %all-to-all-start) | async-done | bytes 2162720 | tf_op jit(solution)/shard_map/all_to_all | solution.py:486
  72.8 5.0 %shard_map.92 = (bf16[16384,128]{1,0:T(8,128)(2,1)S(1)}, bf16[16,1024,128]{2,1,0:T(8,128)(2,1)S(1)}, bf16[16,2048]{1,0:T(8,128)(2,1)S(1)}, bf16[16,128]{1,0:T(8,128)(2,1)S(1)}, bf16[16,128]{1,0:T(8,128)(2,1)S(1)}) custom-call(s32[3]{0:T(128)S(1)} %pad_add_fusion.place_ref, s32[1,512]{1,0:T(1,128)S(1)} %reshape.11.tile_ref, ...), custom_call_target="tpu_custom_call" | custom-call | tf_op jit(solution)/shard_map/pallas_call | solution.py:296
  77.9 1.6 %collective-permute-start.2 = (bf16[16,128]{1,0:T(8,128)(2,1)S(1)}, bf16[16,128]{1,0:T(8,128)(2,1)S(1)}, u32[]{:S(2)}, u32[]{:S(2)}) collective-permute-start(bf16[16,128]{1,0:T(8,128)(2,1)S(1)} %get-tuple-element.12), channel_id=1, source_target_pairs={{0,1},{2,3},{1,0},{3,2},{4,5},{6,7},{5,4},{7,6},{8,9},{10,11},{9,8... | collective-permute-start | bytes 12296 | tf_op jit(solution)/shard_map/ppermute | solution.py:26
  79.4 1.9 %collective-permute-start.3 = (bf16[16,128]{1,0:T(8,128)(2,1)S(1)}, bf16[16,128]{1,0:T(8,128)(2,1)S(1)}, u32[]{:S(2)}, u32[]{:S(2)}) collective-permute-start(bf16[16,128]{1,0:T(8,128)(2,1)S(1)} %get-tuple-element.13), channel_id=1, source_target_pairs={{1,2},{2,1},{5,6},{6,5},{9,10},{10,9},{13,14},{14,13},{17,18},{18,... | collective-permute-start | bytes 12296 | tf_op jit(solution)/shard_map/ppermute | solution.py:26
  81.4 2.4 %collective-permute-done.3.odd_end_ref = bf16[16,128]{1,0:T(8,128)(2,1)S(1)} collective-permute-done((bf16[16,128]{1,0:T(8,128)(2,1)S(1)}, bf16[16,128]{1,0:T(8,128)(2,1)S(1)}, u32[]{:S(2)}, u32[]{:S(2)}) %collective-permute-start.3) | collective-permute-done | bytes 4128 | tf_op jit(solution)/shard_map/ppermute | solution.py:26
  83.8 3.6 %collective-permute-start.5 = (bf16[16,2304]{1,0:T(8,128)(2,1)S(1)}, bf16[16,2304]{1,0:T(8,128)(2,1)S(1)}, u32[]{:S(2)}, u32[]{:S(2)}) collective-permute-start(bf16[16,2304]{1,0:T(8,128)(2,1)S(1)} %constant_dynamic-update-slice_fusion), channel_id=1, source_target_pairs={{4,8},{12,16},{20,24},{8,4},{16,12},{24,20},{5,9},{13,17},{21,25},... | collective-permute-start | bytes 221192 | tf_op jit(solution)/shard_map/ppermute | solution.py:26
  87.5 0.1 constant_dynamic-update-slice_fusion.3
  87.6 0.1 copy.36
  87.6 2.9 %collective-permute-done.5.odd_rim_ref = bf16[16,2304]{1,0:T(8,128)(2,1)S(1)} collective-permute-done((bf16[16,2304]{1,0:T(8,128)(2,1)S(1)}, bf16[16,2304]{1,0:T(8,128)(2,1)S(1)}, u32[]{:S(2)}, u32[]{:S(2)}) %collective-permute-start.5) | collective-permute-done | bytes 73760 | tf_op jit(solution)/shard_map/ppermute | solution.py:26
  90.5 7.2 %shard_map.93 = bf16[16,1024,128]{2,1,0:T(8,128)(2,1)} custom-call(s32[3]{0:T(128)S(1)} %pad_add_fusion.place_ref, bf16[16384,128]{1,0:T(8,128)(2,1)S(1)} %get-tuple-element.10.joined_ref, bf16[16,1024,128]{2,1,0:T(8,128)(2,1)S(1)} %get-tuple-element.11.plain_ref, bf16[16,128]{1,0:T(8,128)(2,1)S(1)} %collective-permute-done.2.even_end_ref, ...), custom_call_target="tpu_custom_call" | custom-call | tf_op jit(solution)/shard_map/pallas_call | solution.py:427
  (32 shorter events, 0.6 us)
Async XLA Ops:
  0.0 6.3 %copy-start.4 = (s32[1,1,32,16]{2,3,1,0:T(8,128)S(1)}, s32[1,1,32,16]{2,3,1,0:T(8,128)}, u32[]{:S(2)}) copy-start(s32[1,1,32,16]{2,3,1,0:T(8,128)} %param.13) | copy-start | bytes 6148
  0.0 6.4 %copy-start.5 = (s32[1,1,32,16]{2,3,1,0:T(8,128)S(1)}, s32[1,1,32,16]{2,3,1,0:T(8,128)}, u32[]{:S(2)}) copy-start(s32[1,1,32,16]{2,3,1,0:T(8,128)} %param.14) | copy-start | bytes 6148
  0.0 6.4 %copy-start.6 = (s32[1,1,32,16]{2,3,1,0:T(8,128)S(1)}, s32[1,1,32,16]{2,3,1,0:T(8,128)}, u32[]{:S(2)}) copy-start(s32[1,1,32,16]{2,3,1,0:T(8,128)} %param.15) | copy-start | bytes 6148
  0.0 6.5 %copy-start.8 = (s32[1,1,32]{2,1,0:T(1,128)S(1)}, s32[1,1,32]{2,1,0:T(1,128)}, u32[]{:S(2)}) copy-start(s32[1,1,32]{2,1,0:T(1,128)} %param.16) | copy-start | bytes 388
  0.0 10.4 %copy-start = (bf16[1,16,32,2048]{3,2,1,0:T(8,128)(2,1)S(1)}, bf16[1,16,32,2048]{3,2,1,0:T(8,128)(2,1)}, u32[]{:S(2)}) copy-start(bf16[1,16,32,2048]{3,2,1,0:T(8,128)(2,1)} %param.9) | copy-start | bytes 6291460
  0.0 10.3 %copy-start.1 = (bf16[16,144]{1,0:T(8,128)(2,1)S(1)}, bf16[16,144]{1,0:T(8,128)(2,1)}, u32[]{:S(2)}) copy-start(bf16[16,144]{1,0:T(8,128)(2,1)} %first_kernel_ref.1) | copy-start | bytes 13828
  0.0 10.3 %copy-start.2 = (bf16[16,144]{1,0:T(8,128)(2,1)S(1)}, bf16[16,144]{1,0:T(8,128)(2,1)}, u32[]{:S(2)}) copy-start(bf16[16,144]{1,0:T(8,128)(2,1)} %second_kernel_ref.1) | copy-start | bytes 13828
  3.0 6.3 %collective-permute-start.1 = (bf16[2,16,2048]{2,1,0:T(8,128)(2,1)S(1)}, bf16[2,16,2048]{2,1,0:T(8,128)(2,1)S(1)}, u32[]{:S(2)}, u32[]{:S(2)}) collective-permute-start(bf16[2,16,2048]{2,1,0:T(8,128)(2,1)S(1)} %get-tuple-element.15), channel_id=1, source_target_pairs={{1,2},{2,1},{5,6},{6,5},{9,10},{10,9},{13,14},{14,13},{17,18},{18,... | collective-permute-start | bytes 393224 | tf_op jit(solution)/shard_map/ppermute | solution.py:26
  6.2 4.2 %collective-permute-start = (bf16[2,16,2048]{2,1,0:T(8,128)(2,1)S(1)}, bf16[2,16,2048]{2,1,0:T(8,128)(2,1)S(1)}, u32[]{:S(2)}, u32[]{:S(2)}) collective-permute-start(bf16[2,16,2048]{2,1,0:T(8,128)(2,1)S(1)} %get-tuple-element.16), channel_id=1, source_target_pairs={{0,1},{2,3},{1,0},{3,2},{4,5},{6,7},{5,4},{7,6},{8,9},{10,11},{9,8... | collective-permute-start | bytes 393224 | tf_op jit(solution)/shard_map/ppermute | solution.py:26
  18.7 5.4 %copy-start.7 = (s32[1,1,32,16]{2,3,1,0:T(8,128)S(1)}, s32[1,1,32,16]{2,3,1,0:T(8,128)}, u32[]{:S(2)}) copy-start(s32[1,1,32,16]{2,3,1,0:T(8,128)} %param.17) | copy-start | bytes 6148
  18.7 5.6 %copy-start.3 = (bf16[16,144]{1,0:T(8,128)(2,1)S(1)}, bf16[16,144]{1,0:T(8,128)(2,1)}, u32[]{:S(2)}) copy-start(bf16[16,144]{1,0:T(8,128)(2,1)} %param.12) | copy-start | bytes 13828
  18.8 54.1 %all-to-all-start = ((bf16[32,264,128]{2,1,0:T(8,128)(2,1)}), bf16[32,264,128]{2,1,0:T(8,128)(2,1)S(1)}, u32[]{:S(2)}, u32[]{:S(2)}) async-start(bf16[32,264,128]{2,1,0:T(8,128)(2,1)} %shard_map.91), calls=%async_computation | async-start | bytes 4325376 | tf_op jit(solution)/shard_map/all_to_all | solution.py:486
  77.9 3.5 %collective-permute-start.2 = (bf16[16,128]{1,0:T(8,128)(2,1)S(1)}, bf16[16,128]{1,0:T(8,128)(2,1)S(1)}, u32[]{:S(2)}, u32[]{:S(2)}) collective-permute-start(bf16[16,128]{1,0:T(8,128)(2,1)S(1)} %get-tuple-element.12), channel_id=1, source_target_pairs={{0,1},{2,3},{1,0},{3,2},{4,5},{6,7},{5,4},{7,6},{8,9},{10,11},{9,8... | collective-permute-start | bytes 12296 | tf_op jit(solution)/shard_map/ppermute | solution.py:26
  79.4 4.3 %collective-permute-start.3 = (bf16[16,128]{1,0:T(8,128)(2,1)S(1)}, bf16[16,128]{1,0:T(8,128)(2,1)S(1)}, u32[]{:S(2)}, u32[]{:S(2)}) collective-permute-start(bf16[16,128]{1,0:T(8,128)(2,1)S(1)} %get-tuple-element.13), channel_id=1, source_target_pairs={{1,2},{2,1},{5,6},{6,5},{9,10},{10,9},{13,14},{14,13},{17,18},{18,... | collective-permute-start | bytes 12296 | tf_op jit(solution)/shard_map/ppermute | solution.py:26
  83.8 6.8 %collective-permute-start.5 = (bf16[16,2304]{1,0:T(8,128)(2,1)S(1)}, bf16[16,2304]{1,0:T(8,128)(2,1)S(1)}, u32[]{:S(2)}, u32[]{:S(2)}) collective-permute-start(bf16[16,2304]{1,0:T(8,128)(2,1)S(1)} %constant_dynamic-update-slice_fusion), channel_id=1, source_target_pairs={{4,8},{12,16},{20,24},{8,4},{16,12},{24,20},{5,9},{13,17},{21,25},... | collective-permute-start | bytes 221192 | tf_op jit(solution)/shard_map/ppermute | solution.py:26
  87.4 3.2 %collective-permute-start.4 = (bf16[16,2304]{1,0:T(8,128)(2,1)S(1)}, bf16[16,2304]{1,0:T(8,128)(2,1)S(1)}, u32[]{:S(2)}, u32[]{:S(2)}) collective-permute-start(bf16[16,2304]{1,0:T(8,128)(2,1)S(1)} %constant_dynamic-update-slice_fusion), channel_id=1, source_target_pairs={{0,4},{8,12},{16,20},{24,28},{4,0},{12,8},{20,16},{28,24},{1,5},{9... | collective-permute-start | bytes 221192 | tf_op jit(solution)/shard_map/ppermute | solution.py:26

commit v7 on v6

--- a/solution.py
+++ b/solution.py
@@ -13,7 +13,8 @@
 SHIFT_BIT = 16
 WEIGHT_BIT = 23
 VMEM_BYTES = 32 * 1024 * 1024
-SEND_BYTES = 36 * 1024 * 1024
+SEND_BYTES = 24 * 1024 * 1024
+STRIP_BYTES = 12 * 1024 * 1024
 WHOLE = pl.BlockSpec(memory_space=pltpu.VMEM)
 SCALARS = pl.BlockSpec(memory_space=pltpu.SMEM)
 
@@ -44,19 +45,67 @@
     return lax.broadcasted_iota(jnp.int32, shape, len(shape) - 1)
 
 
+def spread(lanes, begin, count, per_row, base_of, tiles_of, out_ref):
+    channels = lanes.shape[0]
+    zero = jnp.zeros((channels, TL), jnp.bfloat16)
+    for base, tile_of in zip(base_of, tiles_of):
+        tiles = [
+            tile_of(m) if 0 <= m < per_row else zero for m in range(begin - 1, begin + count + 1)
+        ]
+        ahead = [pltpu.roll(cells, 1, 1) for cells in tiles[:-1]]
+        back = [pltpu.roll(cells, TL - 1, 1) for cells in tiles[1:]]
+        for k in range(count):
+            cols = slice((begin + k) * TL, (begin + k + 1) * TL)
+            out_ref[base : base + channels, cols] = jnp.where(lanes == 0, ahead[k], ahead[k + 1])
+            out_ref[base + channels : base + 2 * channels, cols] = tiles[k + 1]
+            out_ref[base + 2 * channels : base + 3 * channels, cols] = jnp.where(
+                lanes == TL - 1, back[k + 1], back[k]
+            )
+
+
+def strip_kernel(image_ref, taps_ref, pixel_ref):
+    channels, rows, width = image_ref.shape
+    lanes = lanes_of((channels, TL))
+    per_row = width // TL
+    chunk = CHUNK // TL
+
+    def turn_rows(c):
+        for m in range(c * chunk, (c + 1) * chunk):
+            for q in range(channels):
+                cells = image_ref[q, :, m * TL : (m + 1) * TL]
+                base = q * (rows + PAD)
+                pixel_ref[m, base : base + rows, :] = cells.astype(jnp.float32)
+
+    def tile_of(i):
+        return lambda m: pixel_ref[m, pl.ds(i, channels, stride=rows + PAD), :].astype(jnp.bfloat16)
+
+    turn_rows(0)
+    for c in range(per_row // chunk):
+        if (c + 1) * chunk < per_row:
+            turn_rows(c + 1)
+        spread(
+            lanes,
+            c * chunk,
+            chunk,
+            per_row,
+            [i * 3 * channels for i in range(rows)],
+            [tile_of(i) for i in range(rows)],
+            taps_ref,
+        )
+
+
 def send_kernel(
     place_ref,
     slot_ref,
-    image_ref,
+    strip_ref,
     even_ref,
     odd_ref,
     first_kernel_ref,
     second_kernel_ref,
     sent_ref,
+    halo_ref,
     first_ref,
     second_ref,
-    pixel_ref,
-    taps_ref,
     hidden_ref,
     hidden_taps_ref,
     feature_ref,
@@ -64,11 +113,12 @@
     sent_sems,
     *slots_refs,
 ):
-    channels, rows, width = image_ref.shape
+    channels = even_ref.shape[1]
+    width = even_ref.shape[2]
     tap = 3 * channels
+    rows = strip_ref.shape[0] // tap
     reach = (GROUP + 2) * tap
     lanes = lanes_of((channels, TL))
-    zero = jnp.zeros((channels, TL), jnp.bfloat16)
     per_row = width // TL
     chunk = CHUNK // TL
     chunks = per_row // chunk
@@ -76,41 +126,39 @@
     has_above = (place_ref[0] > 0).astype(jnp.float32)
     has_below = (place_ref[0] < place_ref[1] - 1).astype(jnp.float32)
 
-    def spread(c, count, tile_of, out_ref):
-        begin = c * chunk
-        for i in range(count):
-            tiles = [
-                tile_of(i, m) if 0 <= m < per_row else zero
-                for m in range(begin - 1, begin + chunk + 1)
-            ]
-            ahead = [pltpu.roll(cells, 1, 1) for cells in tiles[:-1]]
-            back = [pltpu.roll(cells, TL - 1, 1) for cells in tiles[1:]]
-            for k in range(chunk):
-                cols = slice((begin + k) * TL, (begin + k + 1) * TL)
-                base = i * tap
-                out_ref[base : base + channels, cols] = jnp.where(lanes == 0, ahead[k], ahead[k + 1])
-                out_ref[base + channels : base + 2 * channels, cols] = tiles[k + 1]
-                out_ref[base + 2 * channels : base + tap, cols] = jnp.where(
-                    lanes == TL - 1, back[k + 1], back[k]
-                )
-
-    def turn_rows(c):
-        for m in range(c * chunk, (c + 1) * chunk):
-            for q in range(channels):
-                cells = image_ref[q, :, m * TL : (m + 1) * TL]
-                base = q * (rows + PAD)
-                pixel_ref[m, base : base + rows, :] = cells.astype(jnp.float32)
-
-    def pixel_tile(i, m):
-        cols = slice(m * TL, (m + 1) * TL)
-        if i < 2 or i >= rows + 2:
-            r = i if i < 2 else i - rows - 2
-            above, below = ordered(odd, even_ref[r, :, cols], odd_ref[r, :, cols])
-            return above if i < 2 else below
-        return pixel_ref[m, pl.ds(i - 2, channels, stride=rows + PAD), :].astype(jnp.bfloat16)
-
-    def hidden_tile(i, m):
-        return hidden_ref[i, :, m * TL : (m + 1) * TL]
+    def halo_tile(r, side):
+        def tile_of(m):
+            cols = slice(m * TL, (m + 1) * TL)
+            return ordered(odd, even_ref[r, :, cols], odd_ref[r, :, cols])[side]
+
+        return tile_of
+
+    def hidden_tile(i):
+        return lambda m: hidden_ref[i, :, m * TL : (m + 1) * TL]
+
+    halo = [(r, side) for side in range(2) for r in range(2)]
+
+    def spread_halo(c):
+        spread(
+            lanes,
+            c * chunk,
+            chunk,
+            per_row,
+            [i * tap for i in range(len(halo))],
+            [halo_tile(*at) for at in halo],
+            halo_ref,
+        )
+
+    def spread_hidden(c):
+        spread(
+            lanes,
+            c * chunk,
+            chunk,
+            per_row,
+            [i * tap for i in range(rows + 2)],
+            [hidden_tile(i) for i in range(rows + 2)],
+            hidden_taps_ref,
+        )
 
     for kernel_ref, band_ref in ((first_kernel_ref, first_ref), (second_kernel_ref, second_ref)):
         band_ref[...] = jnp.zeros_like(band_ref)
@@ -128,13 +176,21 @@
         for j in range(c * CHUNK // step, (c + 1) * CHUNK // step):
             cols = slice(j * step, (j + 1) * step)
             for g in range(rows // GROUP):
-                window = taps_ref[g * GROUP * tap : g * GROUP * tap + reach, cols]
+                begin = (g * GROUP - 2) * tap
+                if g == 0:
+                    window = jnp.concatenate(
+                        [halo_ref[: 2 * tap, cols], strip_ref[: begin + reach, cols]], axis=0
+                    )
+                else:
+                    window = strip_ref[begin : begin + reach, cols]
                 out = activate(jnp.dot(first_ref[...], window, preferred_element_type=jnp.float32))
                 out = out.reshape(GROUP, channels, step)
                 if g == 0:
                     out = jnp.concatenate([out[:1] * has_above, out[1:]], axis=0)
                 hidden_ref[g * GROUP : (g + 1) * GROUP, :, cols] = out.astype(jnp.bfloat16)
-            window = taps_ref[rows * tap : (rows + 4) * tap, cols]
+            window = jnp.concatenate(
+                [strip_ref[(rows - 2) * tap :, cols], halo_ref[2 * tap :, cols]], axis=0
+            )
             out = activate(
                 jnp.dot(
                     first_ref[: 2 * channels, : 4 * tap], window, preferred_element_type=jnp.float32
@@ -156,18 +212,14 @@
                             r, :, half * TL : (half + 1) * TL
                         ]
 
-    turn_rows(0)
-    for s in range(chunks + 4):
-        if s + 1 < chunks:
-            turn_rows(s + 1)
+    for s in range(chunks + 3):
         if s < chunks:
-            spread(s, rows + 4, pixel_tile, taps_ref)
-        if 0 <= s - 1 < chunks:
-            convolve_first(s - 1)
+            spread_halo(s)
+            convolve_first(s)
+        if 0 <= s - 2 < chunks:
+            spread_hidden(s - 2)
         if 0 <= s - 3 < chunks:
-            spread(s - 3, rows + 2, hidden_tile, hidden_taps_ref)
-        if 0 <= s - 4 < chunks:
-            convolve_second(s - 4)
+            convolve_second(s - 3)
 
     peers, capacity = slot_ref.shape
     half = capacity // 2
@@ -464,14 +516,26 @@
         + (send_shift[0, 0] << SHIFT_BIT)
         + (jnp.where(used, send_weight[0, 0], 0) << WEIGHT_BIT)
     )
+    taps = jax.ShapeDtypeStruct((strip_rows * 3 * channels, width), half)
+    strip = pl.pallas_call(
+        strip_kernel,
+        out_shape=taps,
+        in_specs=[WHOLE],
+        out_specs=WHOLE,
+        scratch_shapes=[
+            pltpu.VMEM((width // TL, channels * (strip_rows + PAD), TL), jnp.float32)
+        ],
+        compiler_params=pltpu.CompilerParams(vmem_limit_bytes=STRIP_BYTES),
+        cost_estimate=pl.CostEstimate(flops=0, bytes_accessed=taps.size * 2, transcendentals=0),
+    )(pixels)
+    bands = pltpu.VMEM((GROUP * channels, (GROUP + 2) * 3 * channels), half)
     payload = pl.pallas_call(
         send_kernel,
         out_shape=jax.ShapeDtypeStruct((peers, message, TL), half),
         scratch_shapes=[
-            pltpu.VMEM((GROUP * channels, (GROUP + 2) * 3 * channels), half),
-            pltpu.VMEM((GROUP * channels, (GROUP + 2) * 3 * channels), half),
-            pltpu.VMEM((width // TL, channels * (strip_rows + PAD), TL), jnp.float32),
-            pltpu.VMEM(((strip_rows + 4) * 3 * channels, width), half),
+            pltpu.VMEM((4 * 3 * channels, width), half),
+            bands,
+            bands,
             pltpu.VMEM((strip_rows + 2, channels, width), half),
             pltpu.VMEM(((strip_rows + 2) * 3 * channels, width), half),
             pltpu.VMEM((strip_rows * width // TL, channels, TL), half),
@@ -482,7 +546,7 @@
         in_specs=[SCALARS] * 2 + [WHOLE] * 5,
         out_specs=pl.BlockSpec(memory_space=pl.ANY),
         compiler_params=pltpu.CompilerParams(vmem_limit_bytes=SEND_BYTES),
-    )(place, slots, pixels, *near, conv_first, conv_second)
+    )(place, slots, strip, *near, conv_first, conv_second)
     arrived = lax.all_to_all(payload, ("cam", "row"), split_axis=0, concat_axis=0, tiled=True)
     joined, plain, edge, *ends = join_call(place, recv_tile.reshape(1, entries), arrived, channels)
     ends = swap(*ends, "row")

time: 98 us -> 96.6 us (0.986)
  waiting for transfers between devices: 57 us -> 55.4 us
    ppermute x6, waiting for transfers between devices: 9.01 us -> 7.45 us  [swap(): lax.ppermute(cells, axis, pairs + [(j, i) for i, j in pairs])]
    pallas_call x0 -> x1, Pallas kernels: none -> 1.53 us  [local(): pl.pallas_call(strip_kernel, out_shape=taps, in_specs=[WHOLE], out_specs=...]
    pallas_call x1, Pallas kernels: 8.35 us -> 6.94 us  [local(): pl.pallas_call(send_kernel, out_shape=jax.ShapeDtypeStruct((peers, messag...]
  transfers between devices with their start and end apart: 7 -> 7, of which waited for: 5 -> 5; matrix products, arithmetic and copies ran while one was open for 1% -> 1% of each run, Pallas kernels for 0% -> 2%
where the time goes in v7:
time: 96.6 us; the launch traced here: 96.3 us
  waiting for transfers between devices  55.4 us (57%)
  Pallas kernels  20.7 us (21%)
  starting transfers between devices  15.8 us (16%)
  local copies, waits for them, and re-layouts  3.96 us (4%)
    all_to_all x1, waiting for transfers between devices, local(): lax.all_to_all(payload, ('cam', 'row'), split_axis=0, concat_axis=0, tile...  48 us
    ppermute x6, starting transfers between devices, swap(): lax.ppermute(cells, axis, pairs + [(j, i) for i, j in pairs])  10.4 us
    ppermute x6, waiting for transfers between devices, swap(): lax.ppermute(cells, axis, pairs + [(j, i) for i, j in pairs])  7.45 us
    pallas_call x1, Pallas kernels, texture_call(): pl.pallas_call(texture_kernel, out_shape=jax.ShapeDtypeStruct(plain.shape...  7.21 us
    pallas_call x1, Pallas kernels, local(): pl.pallas_call(send_kernel, out_shape=jax.ShapeDtypeStruct((peers, messag...  6.94 us
    all_to_all x1, starting transfers between devices, local(): lax.all_to_all(payload, ('cam', 'row'), split_axis=0, concat_axis=0, tile...  5.41 us
    pallas_call x1, Pallas kernels, join_call(): pl.pallas_call(join_kernel, out_shape=(jax.ShapeDtypeStruct((AR_DEV * cha...  5.03 us
    unnamed x32, local copies, waits for them, and re-layouts  3.72 us
  transfers between devices with their start and end apart: 7, of which 5 were waited for; matrix products, arithmetic and copies ran while one was open for 1% of the time, Pallas kernels for 2%

profile of v7, /device:TPU:11, one launch (start us, length us, event | category | flops | bytes accessed | tf_op | source)
XLA Modules:
  0.0 96.3 jit_solution(11237934533700177871)
XLA Ops:
  0.0 2.9 %copy.35 = bf16[1,16,32,2048]{3,1,2,0:T(8,128)(2,1)S(1)} copy(bf16[1,16,32,2048]{3,2,1,0:T(8,128)(2,1)} %param.9) | data formatting | bytes 4194304 | tf_op args[0]
  3.0 3.2 %collective-permute-start.1 = (bf16[2,16,2048]{2,1,0:T(8,128)(2,1)S(1)}, bf16[2,16,2048]{2,1,0:T(8,128)(2,1)S(1)}, u32[]{:S(2)}, u32[]{:S(2)}) collective-permute-start(bf16[2,16,2048]{2,1,0:T(8,128)(2,1)S(1)} %get-tuple-element.15), channel_id=1, source_target_pairs={{1,2},{2,1},{5,6},{6,5},{9,10},{10,9},{13,14},{14,13},{17,18},{18,... | collective-permute-start | bytes 393224 | tf_op jit(solution)/shard_map/ppermute | solution.py:27
  6.6 1.5 %shard_map.91.strip_ref = bf16[1536,2048]{1,0:T(8,128)(2,1)S(1)} custom-call(bf16[16,32,2048]{2,1,0:T(8,128)(2,1)S(1)} %bitcast.40), custom_call_target="tpu_custom_call" | custom-call | bytes 6291456 | tf_op jit(solution)/shard_map/pallas_call | solution.py:520
  8.1 0.1 pad_add_fusion.place_ref
  8.2 1.0 %collective-permute-done.1.odd_ref = bf16[2,16,2048]{2,1,0:T(8,128)(2,1)S(1)} collective-permute-done((bf16[2,16,2048]{2,1,0:T(8,128)(2,1)S(1)}, bf16[2,16,2048]{2,1,0:T(8,128)(2,1)S(1)}, u32[]{:S(2)}, u32[]{:S(2)}) %collective-permute-start.1) | collective-permute-done | bytes 131104 | tf_op jit(solution)/shard_map/ppermute | solution.py:27
  9.2 1.1 %collective-permute-done.even_ref = bf16[2,16,2048]{2,1,0:T(8,128)(2,1)S(1)} collective-permute-done((bf16[2,16,2048]{2,1,0:T(8,128)(2,1)S(1)}, bf16[2,16,2048]{2,1,0:T(8,128)(2,1)S(1)}, u32[]{:S(2)}, u32[]{:S(2)}) %collective-permute-start) | collective-permute-done | bytes 131104 | tf_op jit(solution)/shard_map/ppermute | solution.py:27
  10.4 6.9 %shard_map.92 = bf16[32,264,128]{2,1,0:T(8,128)(2,1)} custom-call(s32[3]{0:T(128)S(1)} %pad_add_fusion.place_ref, s32[32,16]{1,0:T(8,128)S(1)} %fusion.1.slot_ref, bf16[1536,2048]{1,0:T(8,128)(2,1)S(1)} %shard_map.91.strip_ref, bf16[2,16,2048]{2,1,0:T(8,128)(2,1)S(1)} %collective-permute-done.even_ref, ...), custom_call_target="tpu_custom_call" | custom-call | tf_op jit(solution)/shard_map/pallas_call | solution.py:532
  17.3 5.4 %all-to-all-start = ((bf16[32,264,128]{2,1,0:T(8,128)(2,1)}), bf16[32,264,128]{2,1,0:T(8,128)(2,1)S(1)}, u32[]{:S(2)}, u32[]{:S(2)}) async-start(bf16[32,264,128]{2,1,0:T(8,128)(2,1)} %shard_map.92), calls=%async_computation | async-start | bytes 4325376 | tf_op jit(solution)/shard_map/all_to_all | solution.py:550
  22.8 0.1 reshape.11.tile_ref
  22.9 0.1 constant_dynamic-update-slice_fusion.9
  23.0 0.1 constant_dynamic-update-slice_fusion.8
  23.1 0.1 constant_dynamic-update-slice_fusion.7
  23.2 0.1 constant_dynamic-update-slice_fusion.6
  23.2 0.1 constant_dynamic-update-slice_fusion.5
  23.4 48.0 %all-to-all-done.incoming_ref = bf16[32,264,128]{2,1,0:T(8,128)(2,1)S(1)} async-done(((bf16[32,264,128]{2,1,0:T(8,128)(2,1)}), bf16[32,264,128]{2,1,0:T(8,128)(2,1)S(1)}, u32[]{:S(2)}, u32[]{:S(2)}) %all-to-all-start) | async-done | bytes 2162720 | tf_op jit(solution)/shard_map/all_to_all | solution.py:550
  71.4 5.0 %shard_map.93 = (bf16[16384,128]{1,0:T(8,128)(2,1)S(1)}, bf16[16,1024,128]{2,1,0:T(8,128)(2,1)S(1)}, bf16[16,2048]{1,0:T(8,128)(2,1)S(1)}, bf16[16,128]{1,0:T(8,128)(2,1)S(1)}, bf16[16,128]{1,0:T(8,128)(2,1)S(1)}) custom-call(s32[3]{0:T(128)S(1)} %pad_add_fusion.place_ref, s32[1,512]{1,0:T(1,128)S(1)} %reshape.11.tile_ref, ...), custom_call_target="tpu_custom_call" | custom-call | tf_op jit(solution)/shard_map/pallas_call | solution.py:348
  76.4 1.6 %collective-permute-start.2 = (bf16[16,128]{1,0:T(8,128)(2,1)S(1)}, bf16[16,128]{1,0:T(8,128)(2,1)S(1)}, u32[]{:S(2)}, u32[]{:S(2)}) collective-permute-start(bf16[16,128]{1,0:T(8,128)(2,1)S(1)} %get-tuple-element.12), channel_id=1, source_target_pairs={{0,1},{2,3},{1,0},{3,2},{4,5},{6,7},{5,4},{7,6},{8,9},{10,11},{9,8... | collective-permute-start | bytes 12296 | tf_op jit(solution)/shard_map/ppermute | solution.py:27
  78.0 1.9 %collective-permute-start.3 = (bf16[16,128]{1,0:T(8,128)(2,1)S(1)}, bf16[16,128]{1,0:T(8,128)(2,1)S(1)}, u32[]{:S(2)}, u32[]{:S(2)}) collective-permute-start(bf16[16,128]{1,0:T(8,128)(2,1)S(1)} %get-tuple-element.13), channel_id=1, source_target_pairs={{1,2},{2,1},{5,6},{6,5},{9,10},{10,9},{13,14},{14,13},{17,18},{18,... | collective-permute-start | bytes 12296 | tf_op jit(solution)/shard_map/ppermute | solution.py:27
  80.0 2.4 %collective-permute-done.3.odd_end_ref = bf16[16,128]{1,0:T(8,128)(2,1)S(1)} collective-permute-done((bf16[16,128]{1,0:T(8,128)(2,1)S(1)}, bf16[16,128]{1,0:T(8,128)(2,1)S(1)}, u32[]{:S(2)}, u32[]{:S(2)}) %collective-permute-start.3) | collective-permute-done | bytes 4128 | tf_op jit(solution)/shard_map/ppermute | solution.py:27
  82.4 3.6 %collective-permute-start.5 = (bf16[16,2304]{1,0:T(8,128)(2,1)S(1)}, bf16[16,2304]{1,0:T(8,128)(2,1)S(1)}, u32[]{:S(2)}, u32[]{:S(2)}) collective-permute-start(bf16[16,2304]{1,0:T(8,128)(2,1)S(1)} %constant_dynamic-update-slice_fusion), channel_id=1, source_target_pairs={{4,8},{12,16},{20,24},{8,4},{16,12},{24,20},{5,9},{13,17},{21,25},... | collective-permute-start | bytes 221192 | tf_op jit(solution)/shard_map/ppermute | solution.py:27
  86.0 0.1 constant_dynamic-update-slice_fusion.3
  86.1 0.1 copy.36
  86.2 2.9 %collective-permute-done.5.odd_rim_ref = bf16[16,2304]{1,0:T(8,128)(2,1)S(1)} collective-permute-done((bf16[16,2304]{1,0:T(8,128)(2,1)S(1)}, bf16[16,2304]{1,0:T(8,128)(2,1)S(1)}, u32[]{:S(2)}, u32[]{:S(2)}) %collective-permute-start.5) | collective-permute-done | bytes 73760 | tf_op jit(solution)/shard_map/ppermute | solution.py:27
  89.1 7.2 %shard_map.94 = bf16[16,1024,128]{2,1,0:T(8,128)(2,1)} custom-call(s32[3]{0:T(128)S(1)} %pad_add_fusion.place_ref, bf16[16384,128]{1,0:T(8,128)(2,1)S(1)} %get-tuple-element.10.joined_ref, bf16[16,1024,128]{2,1,0:T(8,128)(2,1)S(1)} %get-tuple-element.11.plain_ref, bf16[16,128]{1,0:T(8,128)(2,1)S(1)} %collective-permute-done.2.even_end_ref, ...), custom_call_target="tpu_custom_call" | custom-call | tf_op jit(solution)/shard_map/pallas_call | solution.py:479
  (33 shorter events, 0.7 us)
Async XLA Ops:
  0.0 6.3 %copy-start.4 = (s32[1,1,32,16]{2,3,1,0:T(8,128)S(1)}, s32[1,1,32,16]{2,3,1,0:T(8,128)}, u32[]{:S(2)}) copy-start(s32[1,1,32,16]{2,3,1,0:T(8,128)} %param.13) | copy-start | bytes 6148
  0.0 6.3 %copy-start.5 = (s32[1,1,32,16]{2,3,1,0:T(8,128)S(1)}, s32[1,1,32,16]{2,3,1,0:T(8,128)}, u32[]{:S(2)}) copy-start(s32[1,1,32,16]{2,3,1,0:T(8,128)} %param.14) | copy-start | bytes 6148
  0.0 6.4 %copy-start.6 = (s32[1,1,32,16]{2,3,1,0:T(8,128)S(1)}, s32[1,1,32,16]{2,3,1,0:T(8,128)}, u32[]{:S(2)}) copy-start(s32[1,1,32,16]{2,3,1,0:T(8,128)} %param.15) | copy-start | bytes 6148
  0.0 6.5 %copy-start.8 = (s32[1,1,32]{2,1,0:T(1,128)S(1)}, s32[1,1,32]{2,1,0:T(1,128)}, u32[]{:S(2)}) copy-start(s32[1,1,32]{2,1,0:T(1,128)} %param.16) | copy-start | bytes 388
  0.0 6.5 %copy-start = (bf16[1,16,32,2048]{3,2,1,0:T(8,128)(2,1)S(1)}, bf16[1,16,32,2048]{3,2,1,0:T(8,128)(2,1)}, u32[]{:S(2)}) copy-start(bf16[1,16,32,2048]{3,2,1,0:T(8,128)(2,1)} %param.9) | copy-start | bytes 6291460
  3.0 6.3 %collective-permute-start.1 = (bf16[2,16,2048]{2,1,0:T(8,128)(2,1)S(1)}, bf16[2,16,2048]{2,1,0:T(8,128)(2,1)S(1)}, u32[]{:S(2)}, u32[]{:S(2)}) collective-permute-start(bf16[2,16,2048]{2,1,0:T(8,128)(2,1)S(1)} %get-tuple-element.15), channel_id=1, source_target_pairs={{1,2},{2,1},{5,6},{6,5},{9,10},{10,9},{13,14},{14,13},{17,18},{18,... | collective-permute-start | bytes 393224 | tf_op jit(solution)/shard_map/ppermute | solution.py:27
  6.2 4.2 %collective-permute-start = (bf16[2,16,2048]{2,1,0:T(8,128)(2,1)S(1)}, bf16[2,16,2048]{2,1,0:T(8,128)(2,1)S(1)}, u32[]{:S(2)}, u32[]{:S(2)}) collective-permute-start(bf16[2,16,2048]{2,1,0:T(8,128)(2,1)S(1)} %get-tuple-element.16), channel_id=1, source_target_pairs={{0,1},{2,3},{1,0},{3,2},{4,5},{6,7},{5,4},{7,6},{8,9},{10,11},{9,8... | collective-permute-start | bytes 393224 | tf_op jit(solution)/shard_map/ppermute | solution.py:27
  6.6 3.8 %copy-start.1 = (bf16[16,144]{1,0:T(8,128)(2,1)S(1)}, bf16[16,144]{1,0:T(8,128)(2,1)}, u32[]{:S(2)}) copy-start(bf16[16,144]{1,0:T(8,128)(2,1)} %first_kernel_ref.1) | copy-start | bytes 13828
  6.6 3.8 %copy-start.2 = (bf16[16,144]{1,0:T(8,128)(2,1)S(1)}, bf16[16,144]{1,0:T(8,128)(2,1)}, u32[]{:S(2)}) copy-start(bf16[16,144]{1,0:T(8,128)(2,1)} %second_kernel_ref.1) | copy-start | bytes 13828
  17.3 5.4 %copy-start.7 = (s32[1,1,32,16]{2,3,1,0:T(8,128)S(1)}, s32[1,1,32,16]{2,3,1,0:T(8,128)}, u32[]{:S(2)}) copy-start(s32[1,1,32,16]{2,3,1,0:T(8,128)} %param.17) | copy-start | bytes 6148
  17.3 5.6 %copy-start.3 = (bf16[16,144]{1,0:T(8,128)(2,1)S(1)}, bf16[16,144]{1,0:T(8,128)(2,1)}, u32[]{:S(2)}) copy-start(bf16[16,144]{1,0:T(8,128)(2,1)} %param.12) | copy-start | bytes 13828
  17.3 54.1 %all-to-all-start = ((bf16[32,264,128]{2,1,0:T(8,128)(2,1)}), bf16[32,264,128]{2,1,0:T(8,128)(2,1)S(1)}, u32[]{:S(2)}, u32[]{:S(2)}) async-start(bf16[32,264,128]{2,1,0:T(8,128)(2,1)} %shard_map.92), calls=%async_computation | async-start | bytes 4325376 | tf_op jit(solution)/shard_map/all_to_all | solution.py:550
  76.4 3.5 %collective-permute-start.2 = (bf16[16,128]{1,0:T(8,128)(2,1)S(1)}, bf16[16,128]{1,0:T(8,128)(2,1)S(1)}, u32[]{:S(2)}, u32[]{:S(2)}) collective-permute-start(bf16[16,128]{1,0:T(8,128)(2,1)S(1)} %get-tuple-element.12), channel_id=1, source_target_pairs={{0,1},{2,3},{1,0},{3,2},{4,5},{6,7},{5,4},{7,6},{8,9},{10,11},{9,8... | collective-permute-start | bytes 12296 | tf_op jit(solution)/shard_map/ppermute | solution.py:27
  78.0 4.3 %collective-permute-start.3 = (bf16[16,128]{1,0:T(8,128)(2,1)S(1)}, bf16[16,128]{1,0:T(8,128)(2,1)S(1)}, u32[]{:S(2)}, u32[]{:S(2)}) collective-permute-start(bf16[16,128]{1,0:T(8,128)(2,1)S(1)} %get-tuple-element.13), channel_id=1, source_target_pairs={{1,2},{2,1},{5,6},{6,5},{9,10},{10,9},{13,14},{14,13},{17,18},{18,... | collective-permute-start | bytes 12296 | tf_op jit(solution)/shard_map/ppermute | solution.py:27
  82.4 6.8 %collective-permute-start.5 = (bf16[16,2304]{1,0:T(8,128)(2,1)S(1)}, bf16[16,2304]{1,0:T(8,128)(2,1)S(1)}, u32[]{:S(2)}, u32[]{:S(2)}) collective-permute-start(bf16[16,2304]{1,0:T(8,128)(2,1)S(1)} %constant_dynamic-update-slice_fusion), channel_id=1, source_target_pairs={{4,8},{12,16},{20,24},{8,4},{16,12},{24,20},{5,9},{13,17},{21,25},... | collective-permute-start | bytes 221192 | tf_op jit(solution)/shard_map/ppermute | solution.py:27
  86.0 3.2 %collective-permute-start.4 = (bf16[16,2304]{1,0:T(8,128)(2,1)S(1)}, bf16[16,2304]{1,0:T(8,128)(2,1)S(1)}, u32[]{:S(2)}, u32[]{:S(2)}) collective-permute-start(bf16[16,2304]{1,0:T(8,128)(2,1)S(1)} %constant_dynamic-update-slice_fusion), channel_id=1, source_target_pairs={{0,4},{8,12},{16,20},{24,28},{4,0},{12,8},{20,16},{28,24},{1,5},{9... | collective-permute-start | bytes 221192 | tf_op jit(solution)/shard_map/ppermute | solution.py:27
